TPU v7x, 32 devices: a whole 2x2x4 slice. The times are simulated.
32 devices in a mesh: dp: 16 (over z, x, core), heads: 2 (over y).
Axes of the slice: x: 2, y: 2, z: 4, core: 2. Of those that a mesh axis runs over, the one named last changes fastest.
Arguments:
- images: bfloat16 [256, 196, 256], P(('dp', 'heads')), may hold values from -6 to 6
- cotangent: bfloat16 [256, 196, 256], P(('dp', 'heads')), may hold values from -6 to 6
- drop_masks: int32 [256, 2], P(('dp', 'heads')), may hold values 0 or 1
- group_master: float32 [2, 132608], P('heads', 'dp'), as said below
- group_m1: float32 [2, 132608], P('heads', 'dp'), as said below
- group_m2: float32 [2, 132608], P('heads', 'dp'), as said below
- shared_master: float32 [526848], P(('dp', 'heads')), as said below
- shared_m1: float32 [526848], P(('dp', 'heads')), as said below
- shared_m2: float32 [526848], P(('dp', 'heads')), as said below
Outputs:
- activations: float32 [256, 196, 256], P(('dp', 'heads'))
- input_grad: float32 [256, 196, 256], P(('dp', 'heads'))
- grad_norm: float32 [1], replicated
- group_grad: float32 [2, 132608], P('heads', 'dp')
- group_master_new: float32 [2, 132608], P('heads', 'dp')
- group_first: float32 [2, 132608], P('heads', 'dp')
- group_second: float32 [2, 132608], P('heads', 'dp')
- group_copy: bfloat16 [2, 132608], P('heads', 'dp')
- shared_grad: float32 [526848], P(('dp', 'heads'))
- shared_master_new: float32 [526848], P(('dp', 'heads'))
- shared_first: float32 [526848], P(('dp', 'heads'))
- shared_second: float32 [526848], P(('dp', 'heads'))
- shared_copy: bfloat16 [526848], P(('dp', 'heads'))
Inputs may be any that keep to these rules, and one draw needn't show every extreme that they name: `group_master`: entries of either sign. `group_m1`: entries of either sign. `group_m2`: every entry positive. `shared_master`: entries of either sign. `shared_m1`: entries of either sign. `shared_m2`: every entry positive.
All inputs are finite; a program needn't handle non-finite values. No bound on the sum of `drop_masks` on one device may be relied on, other than what follows from the above.
Results may differ from a plain program's by a relative error of at most 0.011.
Values may be sent and summed in bfloat16 or wider, within the bound.
A program may use at most 128 MiB of HBM per device.

v0:
```python
from functools import partial
import math

import jax
import jax.numpy as jnp
from jax import lax
from jax.sharding import PartitionSpec as P

D = 256
FF = 1024
SIDE = 14
SW = 7
STEP = 10
HD = 32
GROUP_PARAMS = 132608
SHARED_PARAMS = 526848


eps_norm = 1e-05
keep_prob = 0.8
beta_one = 0.9
beta_two = 0.999
adam_eps = 1e-08
learn_rate = 0.04
decay_rate = 0.05


def split_flat(flat, lengths):
    outcome = []
    offset = 0
    for length in lengths:
        outcome.append(flat[offset : offset + length])
        offset = offset + length
    return outcome


def shared_pieces(flat):
    parts = split_flat(flat, [D * FF, FF, FF * D, D, D, D, D, D, D])
    return (
        parts[0].reshape(D, FF),
        parts[1].astype(jnp.float32),
        parts[2].reshape(FF, D),
        parts[3].astype(jnp.float32),
        parts[4].astype(jnp.float32),
        parts[5].astype(jnp.float32),
        parts[6].astype(jnp.float32),
        parts[7].astype(jnp.float32),
        parts[8].astype(jnp.float32),
    )


def group_pieces(flat):
    half = D // 2
    parts = split_flat(flat, [D * 3 * half, 2 * half, half * D, 9 * half, half])
    return (
        parts[0].reshape(D, 3 * half),
        parts[1].astype(jnp.float32),
        parts[2].reshape(half, D),
        parts[3].reshape(9, half).astype(jnp.float32),
        parts[4].astype(jnp.float32),
    )


def norm_parts(values, gain, shift):
    center = values - jnp.mean(values, axis=-1, keepdims=True)
    inverse = lax.rsqrt(jnp.mean(center * center, axis=-1, keepdims=True) + eps_norm)
    unit = center * inverse
    return (unit * gain + shift, unit, inverse)


def norm_back(grad_after, unit, inverse, gain):
    scaled = grad_after * gain
    grad_before = inverse * (
        scaled
        - jnp.mean(scaled, axis=-1, keepdims=True)
        - unit * jnp.mean(scaled * unit, axis=-1, keepdims=True)
    )
    return (grad_before, jnp.sum(grad_after * unit, axis=(0, 1)), jnp.sum(grad_after, axis=(0, 1)))


def lepe_conv(values, kernel, shift):
    padded = jnp.pad(values, ((0, 0), (0, 0), (1, 1), (1, 1), (0, 0)))
    summed = jnp.zeros_like(values) + shift
    for row_step in range(3):
        for col_step in range(3):
            summed = (
                summed
                + kernel[row_step * 3 + col_step]
                * padded[:, :, row_step : row_step + SW, col_step : col_step + SIDE, :]
            )
    return summed


def orient(grid, turned):
    return jnp.where(turned, jnp.swapaxes(grid, 1, 2), grid)


def to_stripes(token_rows, turned):
    number, width = (token_rows.shape[0], token_rows.shape[-1])
    grid = orient(token_rows.reshape(number, SIDE, SIDE, width), turned)
    return grid.reshape(number, SIDE // SW, SW * SIDE, width)


def from_stripes(stripe_rows, turned):
    number, width = (stripe_rows.shape[0], stripe_rows.shape[-1])
    grid = orient(stripe_rows.reshape(number, SIDE, SIDE, width), turned)
    return grid.reshape(number, SIDE * SIDE, width)


def project_triple(normed, triple_weight, pair_bias):
    half = pair_bias.shape[0] // 2
    bias_full = jnp.concatenate(
        [pair_bias[:half], jnp.zeros((half,), jnp.float32), pair_bias[half:]]
    )
    return (
        jnp.einsum("ntd,de->nte", normed, triple_weight, preferred_element_type=jnp.float32)
        + bias_full
    ).astype(jnp.bfloat16)


def split_parts(projected, turned):
    number = projected.shape[0]
    half = projected.shape[-1] // 3
    parts = to_stripes(projected, turned).reshape(number, SIDE // SW, SW * SIDE, 3, half // HD, HD)
    return (parts[:, :, :, 0], parts[:, :, :, 1], parts[:, :, :, 2])


def attend(projected, turned, conv_kernel, conv_bias):
    number = projected.shape[0]
    half = projected.shape[-1] // 3
    stripes = SIDE // SW
    queries, key_part, value_part = split_parts(projected, turned)
    scores = jnp.einsum(
        "nsqhd,nskhd->nshqk", queries, key_part, preferred_element_type=jnp.float32
    ) * HD ** (-0.5)
    row_max = jnp.max(scores, axis=-1, keepdims=True)
    weights = jnp.exp(scores - row_max)
    row_sum = jnp.sum(weights, axis=-1, keepdims=True)
    softmax_low = (weights / row_sum).astype(jnp.bfloat16)
    log_total = row_max + jnp.log(row_sum)
    attended = jnp.einsum(
        "nshqk,nskhd->nsqhd", softmax_low, value_part, preferred_element_type=jnp.float32
    )
    position_term = lepe_conv(
        value_part.astype(jnp.float32).reshape(number, stripes, SW, SIDE, half),
        conv_kernel,
        conv_bias,
    )
    mixture = attended.reshape(number, stripes, SW * SIDE, half) + position_term.reshape(
        number, stripes, SW * SIDE, half
    )
    return (from_stripes(mixture, turned).astype(jnp.bfloat16), log_total)


def attend_back(projected, log_total, turned, conv_kernel, conv_bias, grad_heads):
    number = projected.shape[0]
    half = projected.shape[-1] // 3
    stripes = SIDE // SW
    queries, key_part, value_part = split_parts(projected, turned)
    grad_rows = to_stripes(grad_heads, turned).reshape(number, stripes, SW * SIDE, half // HD, HD)
    scores = jnp.einsum(
        "nsqhd,nskhd->nshqk", queries, key_part, preferred_element_type=jnp.float32
    ) * HD ** (-0.5)
    softmax_out = jnp.exp(scores - log_total)
    softmax_low = softmax_out.astype(jnp.bfloat16)
    grad_value = jnp.einsum(
        "nshqk,nsqhd->nskhd", softmax_low, grad_rows, preferred_element_type=jnp.float32
    )
    grad_softmax = jnp.einsum(
        "nsqhd,nskhd->nshqk", grad_rows, value_part, preferred_element_type=jnp.float32
    )
    grad_scores = (
        softmax_out * (grad_softmax - jnp.sum(softmax_out * grad_softmax, axis=-1, keepdims=True))
    ).astype(jnp.bfloat16)
    grad_query = jnp.einsum(
        "nshqk,nskhd->nsqhd", grad_scores, key_part, preferred_element_type=jnp.float32
    ) * HD ** (-0.5)
    grad_key = jnp.einsum(
        "nshqk,nsqhd->nskhd", grad_scores, queries, preferred_element_type=jnp.float32
    ) * HD ** (-0.5)
    shape_five = (number, stripes, SW, SIDE, half)
    _, conv_pull = jax.vjp(
        lepe_conv, value_part.astype(jnp.float32).reshape(shape_five), conv_kernel, conv_bias
    )
    grad_local, grad_kernel, grad_shift = conv_pull(
        grad_rows.astype(jnp.float32).reshape(shape_five)
    )
    shape_four = (number, stripes, SW * SIDE, half)
    grad_value = grad_value.reshape(shape_four) + grad_local.reshape(shape_four)
    combined = jnp.stack(
        [grad_query.reshape(shape_four), grad_key.reshape(shape_four), grad_value], axis=3
    )
    grad_triple = from_stripes(
        combined.reshape(number, stripes, SW * SIDE, 3 * half), turned
    ).astype(jnp.bfloat16)
    return (grad_triple, grad_kernel, grad_shift)


def pair_grad(grad_triple):
    summed = jnp.sum(grad_triple, axis=(0, 1), dtype=jnp.float32)
    half = summed.shape[0] // 3
    return jnp.concatenate([summed[:half], summed[2 * half :]])


def flatten_group(grad_triple_weight, grad_pair, grad_out_weight, grad_kernel, grad_shift):
    return jnp.concatenate(
        [
            grad_triple_weight.reshape(-1),
            grad_pair,
            grad_out_weight.reshape(-1),
            grad_kernel.reshape(-1),
            grad_shift,
        ]
    )


def adam_step(master, gradient, first, second, step):
    first_new = beta_one * first + (1.0 - beta_one) * gradient
    second_new = beta_two * second + (1.0 - beta_two) * gradient * gradient
    first_hat = first_new / (1.0 - jnp.power(jnp.float32(beta_one), step))
    second_hat = second_new / (1.0 - jnp.power(jnp.float32(beta_two), step))
    master_new = master - learn_rate * (
        first_hat / (jnp.sqrt(second_hat) + adam_eps) + decay_rate * master
    )
    return (master_new, first_new, second_new)


def on_device(
    images,
    cotangent,
    drop_masks,
    group_master,
    group_m1,
    group_m2,
    shared_master,
    shared_m1,
    shared_m2,
):
    shared_flat = lax.all_gather(
        shared_master.astype(jnp.bfloat16), ("dp", "heads"), axis=0, tiled=True
    )
    group_flat = lax.all_gather(group_master.astype(jnp.bfloat16), "dp", axis=1, tiled=True)
    (
        up_weight,
        up_bias,
        down_weight,
        down_bias,
        gain_one,
        shift_one,
        gain_two,
        shift_two,
        out_bias,
    ) = shared_pieces(shared_flat)
    values = images.astype(jnp.float32)
    scales = drop_masks.astype(jnp.float32) / keep_prob
    scale_one = scales[:, 0][:, None, None]
    scale_two = scales[:, 1][:, None, None]
    normed_f, unit_one, inverse_one = norm_parts(values, gain_one, shift_one)
    normed = normed_f.astype(jnp.bfloat16)
    turned = lax.axis_index("heads") == 1
    triple_weight, pair_bias, out_weight, conv_kernel, conv_bias = group_pieces(group_flat[0])
    normed_rows = lax.all_gather(normed, "heads", axis=0, tiled=True)
    projected = project_triple(normed_rows, triple_weight, pair_bias)
    heads_out, log_total = attend(projected, turned, conv_kernel, conv_bias)
    own_rows = heads_out
    branch = lax.psum_scatter(
        jnp.einsum("nte,ed->ntd", own_rows, out_weight, preferred_element_type=jnp.float32).astype(
            jnp.bfloat16
        ),
        "heads",
        scatter_dimension=0,
        tiled=True,
    ).astype(jnp.float32)
    middle = values + scale_one * (branch + out_bias)
    normed_two_f, unit_two, inverse_two = norm_parts(middle, gain_two, shift_two)
    normed_two = normed_two_f.astype(jnp.bfloat16)
    hidden = (
        jnp.einsum("ntd,df->ntf", normed_two, up_weight, preferred_element_type=jnp.float32)
        + up_bias
    )
    active_f, gelu_pull = jax.vjp(partial(jax.nn.gelu, approximate=False), hidden)
    active = active_f.astype(jnp.bfloat16)
    output = middle + scale_two * (
        jnp.einsum("ntf,fd->ntd", active, down_weight, preferred_element_type=jnp.float32)
        + down_bias
    )
    grad_output = cotangent.astype(jnp.float32)
    grad_mlp_f = scale_two * grad_output
    grad_down_bias = jnp.sum(grad_mlp_f, axis=(0, 1))
    grad_mlp = grad_mlp_f.astype(jnp.bfloat16)
    grad_down_weight = jnp.einsum(
        "ntf,ntd->fd", active, grad_mlp, preferred_element_type=jnp.float32
    )
    grad_active = jnp.einsum(
        "ntd,fd->ntf", grad_mlp, down_weight, preferred_element_type=jnp.float32
    )
    grad_hidden = gelu_pull(grad_active)[0].astype(jnp.bfloat16)
    grad_up_bias = jnp.sum(grad_hidden, axis=(0, 1), dtype=jnp.float32)
    grad_up_weight = jnp.einsum(
        "ntd,ntf->df", normed_two, grad_hidden, preferred_element_type=jnp.float32
    )
    grad_normed_two = jnp.einsum(
        "ntf,df->ntd", grad_hidden, up_weight, preferred_element_type=jnp.float32
    )
    grad_back_two, grad_gain_two, grad_shift_two = norm_back(
        grad_normed_two, unit_two, inverse_two, gain_two
    )
    grad_middle = grad_output + grad_back_two
    grad_branch_f = scale_one * grad_middle
    grad_out_bias = jnp.sum(grad_branch_f, axis=(0, 1))
    grad_branch = grad_branch_f.astype(jnp.bfloat16)
    portion = lax.all_gather(grad_branch, "heads", axis=0, tiled=True)
    grad_rows = jnp.einsum("ntd,ed->nte", portion, out_weight, preferred_element_type=jnp.float32)
    own_rows = heads_out
    grad_out_weight = jnp.einsum(
        "nte,ntd->ed", own_rows, portion, preferred_element_type=jnp.float32
    )
    grad_triple, grad_kernel, grad_shift = attend_back(
        projected, log_total, turned, conv_kernel, conv_bias, grad_rows.astype(jnp.bfloat16)
    )
    grad_triple_weight = jnp.einsum(
        "ntd,nte->de", normed_rows, grad_triple, preferred_element_type=jnp.float32
    )
    own_rows = grad_triple
    grad_normed = lax.psum_scatter(
        jnp.einsum(
            "nte,de->ntd", own_rows, triple_weight, preferred_element_type=jnp.float32
        ).astype(jnp.bfloat16),
        "heads",
        scatter_dimension=0,
        tiled=True,
    ).astype(jnp.float32)
    group_raw = flatten_group(
        grad_triple_weight, pair_grad(grad_triple), grad_out_weight, grad_kernel, grad_shift
    )
    grad_back_one, grad_gain_one, grad_shift_one = norm_back(
        grad_normed, unit_one, inverse_one, gain_one
    )
    input_grad = grad_middle + grad_back_one
    shared_raw = jnp.concatenate(
        [
            grad_up_weight.reshape(-1),
            grad_up_bias,
            grad_down_weight.reshape(-1),
            grad_down_bias,
            grad_gain_one,
            grad_shift_one,
            grad_gain_two,
            grad_shift_two,
            grad_out_bias,
        ]
    )
    group_share = lax.psum_scatter(group_raw, "dp", scatter_dimension=0, tiled=True)
    shared_share = lax.psum_scatter(shared_raw, ("dp", "heads"), scatter_dimension=0, tiled=True)
    group_share = group_share[None, :]
    squares = jnp.sum(group_share * group_share) + jnp.sum(shared_share * shared_share)
    grad_norm = jnp.sqrt(lax.psum(squares, ("dp", "heads")))
    threshold = math.sqrt(2 * GROUP_PARAMS + SHARED_PARAMS)
    factor = jnp.minimum(1.0, threshold / (grad_norm + 1e-06))
    group_grad = group_share * factor
    shared_grad = shared_share * factor
    step = jnp.float32(STEP)
    group_new, group_first, group_second = adam_step(
        group_master, group_grad, group_m1, group_m2, step
    )
    shared_new, shared_first, shared_second = adam_step(
        shared_master, shared_grad, shared_m1, shared_m2, step
    )
    return (
        output,
        input_grad,
        grad_norm.reshape(1),
        group_grad,
        group_new,
        group_first,
        group_second,
        group_new.astype(jnp.bfloat16),
        shared_grad,
        shared_new,
        shared_first,
        shared_second,
        shared_new.astype(jnp.bfloat16),
    )


def solution(mesh):
    in_specs = (
        P(("dp", "heads"), None, None),
        P(("dp", "heads"), None, None),
        P(("dp", "heads"), None),
        P("heads", "dp"),
        P("heads", "dp"),
        P("heads", "dp"),
        P(("dp", "heads")),
        P(("dp", "heads")),
        P(("dp", "heads")),
    )
    out_specs = (
        P(("dp", "heads"), None, None),
        P(("dp", "heads"), None, None),
        P(),
        P("heads", "dp"),
        P("heads", "dp"),
        P("heads", "dp"),
        P("heads", "dp"),
        P("heads", "dp"),
        P(("dp", "heads")),
        P(("dp", "heads")),
        P(("dp", "heads")),
        P(("dp", "heads")),
        P(("dp", "heads")),
    )
    return jax.shard_map(
        on_device, mesh=mesh, in_specs=in_specs, out_specs=out_specs, check_vma=False
    )
```

profile of v0, /device:TPU:0, one launch (start us, length us, event | category | flops | bytes accessed | tf_op | source)
XLA Modules:
  0.0 822.9 jit_solution(7297437329936739165)
XLA Ops:
  8.2 1.3 fusion.70
  16.3 87.3 %all-reduce.30.cloned.1.call-done = bf16[132608]{0:T(1024)(128)(2,1)} async-done(((bf16[132608]{0:T(1024)(128)(2,1)}), bf16[132608]{0:T(1024)(128)(2,1)}) %all-reduce.30.cloned.1.call-update) | async-done | bytes 265232
  103.6 3.4 reshape.295
  107.0 132.8 %all-reduce.28.cloned.1.call-done = bf16[526848]{0:T(1024)(128)(2,1)} async-done(((bf16[526848]{0:T(1024)(128)(2,1)}), bf16[526848]{0:T(1024)(128)(2,1)}) %all-reduce.28.cloned.1.call-update) | async-done | bytes 1053712
  239.8 1.4 slice_convert_fusion.3
  246.7 24.6 %all-gather.3.cloned.1.call-done = bf16[16,196,256]{2,0,1:T(8,128)(2,1)} async-done(((bf16[8,196,256]{2,0,1:T(8,128)(2,1)}), bf16[16,196,256]{2,0,1:T(8,128)(2,1)}) %all-gather.3.cloned.1.call-update) | async-done | bytes 1605648 | tf_op jit(solution)/shard_map/all_gather | solution.py:262
  271.4 2.7 add_convert_fusion.1
  274.6 8.0 reshape_reshape.10
  282.6 10.7 %fusion.68 = (bf16[16,2,98,1,4,32]{5,4,3,0,2,1:T(4,128)(2,1)}, bf16[16,2,98,1,4,32]{5,4,3,0,2,1:T(4,128)(2,1)}, bf16[16,2,98,1,4,32]{5,4,3,0,2,1:T(4,128)(2,1)}) fusion(bf16[16,2,98,3,4,32]{5,4,3,0,2,1:T(4,128)(2,1)} %reshape_reshape.10), kind=kLoop, calls=%fused_computation.211 | loop fusion | bytes 4816896 | tf_op jit(solution)/shard_map/slice | solution.py:125
  293.3 5.4 copy.105
  298.7 5.7 copy.106
  304.5 5.9 copy.107
  310.4 4.6 copy.75
  315.0 5.0 reshape.288
  320.0 3.8 multiply_reduce_fusion.1
  323.9 2.1 fusion.6
  326.6 2.9 fusion.41
  329.5 6.6 copy.74
  336.1 6.3 reshape.274
  345.0 1.8 convolution_convert_fusion
  348.9 5.3 reshape.290
  354.3 19.5 %reduce-scatter.3.cloned.1.call-done = bf16[8,196,256]{2,1,0:T(8,128)(2,1)} async-done(((bf16[16,196,256]{2,1,0:T(8,128)(2,1)}), bf16[8,196,256]{2,1,0:T(8,128)(2,1)}) %reduce-scatter.3.cloned.1.call-update) | async-done | bytes 802832 | tf_op jit(solution)/shard_map/reduce_scatter | solution.py:266
  373.7 1.6 fusion.62
  376.3 3.4 fusion.40
  379.7 14.9 %multiply_convert_fusion.1 = (bf16[8,196,1024]{2,1,0:T(8,128)(2,1)S(1)}, f32[8,196,1024]{2,1,0:T(8,128)S(1)}) fusion(f32[8,196,1024]{2,1,0:T(8,128)S(1)} %get-tuple-element.129, f32[1024]{0:T(1024)S(1)} %slice_convert_fusion.1, u8[196,1024]{1,0:T(8,128)(4,1)S(1)} %get-tuple-element.53, u8[196,1024]{1,0:T(8,128)(4,1)S(1)} %get-tuple-element.52), kind=kLoop, calls=%fused_computation.14 | loop fusion | flops 113999872 | bytes 16461824 | tf_op jit(solution)/shard_map/convert_element_type | solution.py:282
  394.7 3.9 convert_reduce_fusion
  398.5 1.7 convolution_bitcast_fusion.1
  401.4 1.3 convolution_bitcast_fusion
  402.7 1.5 copy.110
  404.2 1.8 multiply_reduce_fusion.2
  406.1 1.4 multiply_reduce_fusion.14
  410.0 2.3 constant_dynamic-update-slice_fusion.1
  412.9 2.3 constant_dynamic-update-slice_fusion.12
  416.5 21.2 %all-gather.5.cloned.1.call-done = bf16[16,196,256]{2,0,1:T(8,128)(2,1)} async-done(((bf16[8,196,256]{2,0,1:T(8,128)(2,1)}), bf16[16,196,256]{2,0,1:T(8,128)(2,1)}) %all-gather.5.cloned.1.call-update) | async-done | bytes 1605648 | tf_op jit(solution)/shard_map/all_gather | solution.py:312
  437.7 2.5 fusion.43
  441.7 2.8 reshape_reshape.11
  444.5 5.7 copy.83
  450.2 6.6 fusion.9
  456.8 5.1 multiply_reduce_fusion
  461.9 5.0 multiply_convert_fusion
  466.9 2.9 convolution_multiply_fusion
  469.8 2.1 convolution_multiply_fusion.1
  473.5 2.1 multiply_reduce_fusion.13
  475.5 1.9 copy.88
  477.5 1.9 copy.89
  479.4 2.8 copy.90
  482.3 1.8 broadcast_multiply_fusion
  486.7 3.4 copy.91
  490.1 6.2 reshape_reshape.12
  497.4 1.4 copy-done.27
  498.8 2.3 fusion.25
  501.2 2.8 convolution_bitcast_fusion.2
  505.0 23.0 %reduce-scatter.5.cloned.1.call-done = bf16[8,196,256]{2,1,0:T(8,128)(2,1)} async-done(((bf16[16,196,256]{2,1,0:T(8,128)(2,1)}), bf16[8,196,256]{2,1,0:T(8,128)(2,1)}) %reduce-scatter.5.cloned.1.call-update) | async-done | bytes 802832 | tf_op jit(solution)/shard_map/reduce_scatter | solution.py:325
  528.1 2.7 fusion.35
  537.3 3.2 multiply_add_fusion
  540.5 1.6 copy.97
  542.2 80.5 %all-reduce.32.cloned.1.call-done = f32[132608]{0:T(1024)} async-done(((f32[132608]{0:T(1024)}), f32[132608]{0:T(1024)}) %all-reduce.32.cloned.1.call-update) | async-done | bytes 530448
  622.7 1.5 multiply_reduce_fusion.17
  624.2 2.0 fusion.32
  626.2 137.5 %all-reduce.34.cloned.1.call-done = f32[526848]{0:T(1024)} async-done(((f32[526848]{0:T(1024)}), f32[526848]{0:T(1024)}) %all-reduce.34.cloned.1.call-update) | async-done | bytes 2107408
  763.7 1.6 multiply_reduce_fusion.16
  766.5 3.1 copy.98
  769.6 40.0 %psum.7 = f32[]{:T(128)} all-reduce(f32[]{:T(128)S(6)} %add.245), channel_id=1, replica_groups=mesh['dp'=16,'heads'=2] {'dp','heads'}, use_global_device_ids=true, to_apply=%region_35.36 | all-reduce | flops 1 | bytes 8 | tf_op jit(solution)/shard_map/psum | solution.py:357
  812.8 1.7 fusion.63
  (251 shorter events, 40.9 us)
Async XLA Ops:
  7.2 6.9 copy-start.77
  7.2 6.9 copy-start.1
  7.2 96.4 %all-reduce.30.cloned.1.call-start = ((), (), s32[]{:S(2)}) async-start(), calls=%async_computation.7 | async-start | bytes 532480
  11.4 228.4 %all-reduce.28.cloned.1.call-start = ((), (), s32[]{:S(2)}) async-start(), calls=%async_computation.6 | async-start | bytes 2109440
  14.0 257.4 %all-gather.3.cloned.1.call-start = ((), (), s32[]{:S(2)}) async-start(), calls=%async_computation.2 | async-start | bytes 2408448 | tf_op jit(solution)/shard_map/all_gather | solution.py:262
  14.4 228.8 %copy-start.38 = (f32[8,196]{1,0:T(8,128)}, f32[8,196]{1,0:T(8,128)S(1)}, u32[]{:S(2)}) copy-start(f32[8,196]{1,0:T(8,128)S(1)} %broadcast_multiply_fusion.15) | copy-start | bytes 18820
  16.3 227.0 %copy-start.43 = (f32[8,196]{1,0:T(8,128)}, f32[8,196]{1,0:T(8,128)S(1)}, u32[]{:S(2)}) copy-start(f32[8,196]{1,0:T(8,128)S(1)} %add_rsqrt_fusion.1) | copy-start | bytes 18820
  243.3 130.4 %reduce-scatter.3.cloned.1.call-start = ((), (), s32[]{:S(2)}) async-start(), calls=%async_computation.3 | async-start | bytes 2457600 | tf_op jit(solution)/shard_map/reduce_scatter | solution.py:266
  244.6 29.4 %copy-start.40 = (bf16[256,384,1]{1,0,2:T(8,128)(2,1)}, bf16[256,384,1]{1,0,2:T(8,128)(2,1)S(1)}, u32[]{:S(2)}) copy-start(bf16[256,384,1]{1,0,2:T(8,128)(2,1)S(1)} %reshape.298) | copy-start | bytes 589828
  246.7 95.7 %copy-start.55 = (f32[128]{0:T(128)}, f32[128]{0:T(128)S(1)}, u32[]{:S(2)}) copy-start(f32[128]{0:T(128)S(1)} %get-tuple-element.112) | copy-start | bytes 1540
  246.7 95.7 %copy-start.57 = (f32[128]{0:T(128)}, f32[128]{0:T(128)S(1)}, u32[]{:S(2)}) copy-start(f32[128]{0:T(128)S(1)} %get-tuple-element.113) | copy-start | bytes 1540
  246.7 95.7 %copy-start.59 = (f32[128]{0:T(128)}, f32[128]{0:T(128)S(1)}, u32[]{:S(2)}) copy-start(f32[128]{0:T(128)S(1)} %get-tuple-element.114) | copy-start | bytes 1540
  246.7 95.7 %copy-start.61 = (f32[128]{0:T(128)}, f32[128]{0:T(128)S(1)}, u32[]{:S(2)}) copy-start(f32[128]{0:T(128)S(1)} %get-tuple-element.115) | copy-start | bytes 1540
  246.7 95.7 %copy-start.63 = (f32[128]{0:T(128)}, f32[128]{0:T(128)S(1)}, u32[]{:S(2)}) copy-start(f32[128]{0:T(128)S(1)} %get-tuple-element.116) | copy-start | bytes 1540
  246.7 95.7 %copy-start.65 = (f32[128]{0:T(128)}, f32[128]{0:T(128)S(1)}, u32[]{:S(2)}) copy-start(f32[128]{0:T(128)S(1)} %get-tuple-element.117) | copy-start | bytes 1540
  246.7 95.7 %copy-start.67 = (f32[128]{0:T(128)}, f32[128]{0:T(128)S(1)}, u32[]{:S(2)}) copy-start(f32[128]{0:T(128)S(1)} %get-tuple-element.118) | copy-start | bytes 1540
  246.7 95.7 %copy-start.69 = (f32[128]{0:T(128)}, f32[128]{0:T(128)S(1)}, u32[]{:S(2)}) copy-start(f32[128]{0:T(128)S(1)} %get-tuple-element.119) | copy-start | bytes 1540
  298.7 11.7 %copy-start.9 = (bf16[16,2,98,1,4,32]{2,5,4,1,0,3:T(8,128)(2,1)}, bf16[16,2,98,1,4,32]{2,5,4,1,0,3:T(8,128)(2,1)S(1)}, u32[]{:S(2)}) copy-start(bf16[16,2,98,1,4,32]{2,5,4,1,0,3:T(8,128)(2,1)S(1)} %copy.105) | copy-start | bytes 2408452
  304.5 15.5 %copy-start.6 = (bf16[16,2,98,1,4,32]{2,5,4,1,0,3:T(8,128)(2,1)}, bf16[16,2,98,1,4,32]{2,5,4,1,0,3:T(8,128)(2,1)S(1)}, u32[]{:S(2)}) copy-start(bf16[16,2,98,1,4,32]{2,5,4,1,0,3:T(8,128)(2,1)S(1)} %copy.106) | copy-start | bytes 2408452
  320.0 22.4 %copy-start.4 = (f32[16,2,7,14,128]{4,0,3,2,1:T(8,128)}, f32[16,2,7,14,128]{4,0,3,2,1:T(8,128)S(1)}, u32[]{:S(2)}) copy-start(f32[16,2,7,14,128]{4,0,3,2,1:T(8,128)S(1)} %reshape.288) | copy-start | bytes 4816900
  336.1 6.4 copy-start.71
  336.1 6.4 copy-start.78
  346.8 90.9 %all-gather.5.cloned.1.call-start = ((), (), s32[]{:S(2)}) async-start(), calls=%async_computation.4 | async-start | bytes 2408448 | tf_op jit(solution)/shard_map/all_gather | solution.py:312
  348.9 24.8 %copy-start.51 = (f32[256]{0:T(256)S(1)}, f32[256]{0:T(256)}, u32[]{:S(2)}) copy-start(f32[256]{0:T(256)} %get-tuple-element.106) | copy-start | bytes 3076
  348.9 24.8 %copy-start.53 = (f32[8]{0:T(128)S(1)}, f32[8]{0:T(128)}, u32[]{:S(2)}) copy-start(f32[8]{0:T(128)} %get-tuple-element.122) | copy-start | bytes 100
  354.2 22.0 %copy-start.35 = (bf16[256,1024,1]{1,0,2:T(8,128)(2,1)S(1)}, bf16[256,1024,1]{1,0,2:T(8,128)(2,1)}, u32[]{:S(2)}) copy-start(bf16[256,1024,1]{1,0,2:T(8,128)(2,1)} %reshape.300) | copy-start | bytes 1572868
  354.2 22.0 %copy-start.73 = (f32[256]{0:T(256)S(1)}, f32[256]{0:T(256)}, u32[]{:S(2)}) copy-start(f32[256]{0:T(256)} %get-tuple-element.105) | copy-start | bytes 3076
  354.2 22.0 %copy-start.76 = (f32[256]{0:T(256)S(1)}, f32[256]{0:T(256)}, u32[]{:S(2)}) copy-start(f32[256]{0:T(256)} %get-tuple-element.104) | copy-start | bytes 3076
  379.7 15.0 %copy-start.32 = (bf16[8,196,256]{2,0,1:T(8,128)(2,1)S(1)}, bf16[8,196,256]{2,0,1:T(8,128)(2,1)}, u32[]{:S(2)}) copy-start(bf16[8,196,256]{2,0,1:T(8,128)(2,1)} %param.10) | copy-start | bytes 2408452
  379.7 15.0 %copy-start.33 = (bf16[1024,256,1]{1,0,2:T(8,128)(2,1)S(1)}, bf16[1024,256,1]{1,0,2:T(8,128)(2,1)}, u32[]{:S(2)}) copy-start(bf16[1024,256,1]{1,0,2:T(8,128)(2,1)} %reshape.301) | copy-start | bytes 1572868
  379.7 15.0 %copy-start.74 = (f32[8]{0:T(128)S(1)}, f32[8]{0:T(128)}, u32[]{:S(2)}) copy-start(f32[8]{0:T(128)} %get-tuple-element.121) | copy-start | bytes 100
  394.6 6.8 copy-start.25
  410.0 118.1 %reduce-scatter.5.cloned.1.call-start = ((), (), s32[]{:S(2)}) async-start(), calls=%async_computation.5 | async-start | bytes 2457600 | tf_op jit(solution)/shard_map/reduce_scatter | solution.py:325
  444.5 12.3 %slice-start = ((s8[6815744]{0:T(1024)(128)(4,1)}), s8[2621440]{0:T(1024)(128)(4,1)S(1)}, s32[]{:S(2)}) async-start(s8[6815744]{0:T(1024)(128)(4,1)} %bitcast.153), calls=%async_computation.10 | async-start | bytes 5242880
  450.2 6.6 slice-start.1
  450.2 6.6 copy-start.11
  450.2 6.6 copy-start.12
  461.9 5.0 copy-start.7
  477.4 4.8 copy-start.58
  477.4 4.8 copy-start.60
  477.4 4.8 copy-start.62
  477.4 4.8 copy-start.64
  477.4 4.8 copy-start.66
  477.5 4.8 copy-start.68
  477.5 4.8 copy-start.70
  477.5 4.8 copy-start.72
  501.1 121.6 %all-reduce.32.cloned.1.call-start = ((), (), s32[]{:S(2)}) async-start(), calls=%async_computation.8 | async-start | bytes 1064960
  504.0 24.1 %copy-start.39 = (f32[8,196]{1,0:T(8,128)S(1)}, f32[8,196]{1,0:T(8,128)}, u32[]{:S(2)}) copy-start(f32[8,196]{1,0:T(8,128)} %copy-done.38) | copy-start | bytes 18820
  504.0 24.1 %copy-start.44 = (f32[8,196]{1,0:T(8,128)S(1)}, f32[8,196]{1,0:T(8,128)}, u32[]{:S(2)}) copy-start(f32[8,196]{1,0:T(8,128)} %copy-done.43) | copy-start | bytes 18820
  504.0 24.1 %copy-start.50 = (f32[256]{0:T(256)S(1)}, f32[256]{0:T(256)}, u32[]{:S(2)}) copy-start(f32[256]{0:T(256)} %copy-done.49) | copy-start | bytes 3076
  504.2 33.1 %copy-start.15 = (bf16[8,196,256]{2,1,0:T(8,128)(2,1)S(1)}, bf16[8,196,256]{2,1,0:T(8,128)(2,1)}, u32[]{:S(2)}) copy-start(bf16[8,196,256]{2,1,0:T(8,128)(2,1)} %reduce-scatter.3.cloned.1.call-done) | copy-start | bytes 2408452
  504.2 33.1 %copy-start.34 = (bf16[1024,256,1]{1,0,2:T(8,128)(2,1)S(1)}, bf16[1024,256,1]{1,0,2:T(8,128)(2,1)}, u32[]{:S(2)}) copy-start(bf16[1024,256,1]{1,0,2:T(8,128)(2,1)} %reshape.301) | copy-start | bytes 1572868
  504.2 33.1 %copy-start.52 = (f32[256]{0:T(256)S(1)}, f32[256]{0:T(256)}, u32[]{:S(2)}) copy-start(f32[256]{0:T(256)} %get-tuple-element.106) | copy-start | bytes 3076
  504.2 33.1 %copy-start.54 = (f32[8]{0:T(128)S(1)}, f32[8]{0:T(128)}, u32[]{:S(2)}) copy-start(f32[8]{0:T(128)} %get-tuple-element.122) | copy-start | bytes 100
  504.2 33.1 %copy-start.75 = (f32[256]{0:T(256)S(1)}, f32[256]{0:T(256)}, u32[]{:S(2)}) copy-start(f32[256]{0:T(256)} %get-tuple-element.103) | copy-start | bytes 3076
  505.0 258.7 %all-reduce.34.cloned.1.call-start = ((), (), s32[]{:S(2)}) async-start(), calls=%async_computation.9 | async-start | bytes 4218880
  540.5 83.7 %copy-start.3 = (f32[8,196,256]{2,1,0:T(8,128)S(1)}, f32[8,196,256]{2,1,0:T(8,128)}, u32[]{:S(2)}) copy-start(f32[8,196,256]{2,1,0:T(8,128)} %copy-done.2) | copy-start | bytes 4816900
  540.5 83.7 %copy-start.24 = (bf16[8,196,256]{2,1,0:T(8,128)(2,1)S(1)}, bf16[8,196,256]{2,1,0:T(8,128)(2,1)}, u32[]{:S(2)}) copy-start(bf16[8,196,256]{2,1,0:T(8,128)(2,1)} %reduce-scatter.5.cloned.1.call-done) | copy-start | bytes 2408452
  626.1 185.7 %copy-start.42 = (f32[1,8288]{1,0:T(1,128)S(1)}, f32[1,8288]{1,0:T(1,128)}, u32[]{:S(2)}) copy-start(f32[1,8288]{1,0:T(1,128)} %param.12) | copy-start | bytes 99460
  626.1 185.7 %copy-start.47 = (f32[1,8288]{1,0:T(1,128)S(1)}, f32[1,8288]{1,0:T(1,128)}, u32[]{:S(2)}) copy-start(f32[1,8288]{1,0:T(1,128)} %param.14) | copy-start | bytes 99460
  626.1 185.7 %copy-start.48 = (f32[1,8288]{1,0:T(1,128)S(1)}, f32[1,8288]{1,0:T(1,128)}, u32[]{:S(2)}) copy-start(f32[1,8288]{1,0:T(1,128)} %param.13) | copy-start | bytes 99460
  626.1 186.6 %copy-start.36 = (f32[16464]{0:T(1024)S(1)}, f32[16464]{0:T(1024)}, u32[]{:S(2)}) copy-start(f32[16464]{0:T(1024)} %param.15) | copy-start | bytes 197572
  626.1 186.6 %copy-start.45 = (f32[16464]{0:T(1024)S(1)}, f32[16464]{0:T(1024)}, u32[]{:S(2)}) copy-start(f32[16464]{0:T(1024)} %param.17) | copy-start | bytes 197572
  626.2 186.6 %copy-start.46 = (f32[16464]{0:T(1024)S(1)}, f32[16464]{0:T(1024)}, u32[]{:S(2)}) copy-start(f32[16464]{0:T(1024)} %param.16) | copy-start | bytes 197572
  (26 other events, 50.5 us)
Sparse Core Ops, SparseCore 0:
  12.0 91.5 all-reduce.29
  109.6 130.1 all-reduce.27
  243.4 27.8 all-gather.2
  346.9 26.7 reduce-scatter.2
  410.1 27.5 all-gather.4
  501.3 26.7 reduce-scatter.4
  532.4 90.2 all-reduce.31
  629.2 134.4 all-reduce.33
where the time goes:
time: 831 us; the launch traced here: 823 us
  waiting for transfers between devices  527 us (63%)
  local copies, waits for them, and re-layouts  134 us (16%)
  matrix products  51 us (6%)
  other arithmetic  50.9 us (6%)
  blocking collectives  40 us (5%)
  between operations  20.4 us (2%)
    unnamed x12, waiting for transfers between devices  438 us
    unnamed x190, local copies, waits for them, and re-layouts  52.9 us
    psum x1, blocking collectives, on_device(): grad_norm = jnp.sqrt(lax.psum(squares, ('dp', 'heads')))  40 us
    all_gather x1, waiting for transfers between devices, on_device(): normed_rows = lax.all_gather(normed, 'heads', axis=0, tiled=True)  24.6 us
    reduce_scatter x1, waiting for transfers between devices, on_device(): lax.psum_scatter(jnp.einsum('nte,de->ntd', own_rows, triple_weight, prefe...  23 us
    all_gather x1, waiting for transfers between devices, on_device(): portion = lax.all_gather(grad_branch, 'heads', axis=0, tiled=True)  21.2 us
    reduce_scatter x1, waiting for transfers between devices, on_device(): lax.psum_scatter(jnp.einsum('nte,ed->ntd', own_rows, out_weight, preferre...  19.5 us
  transfers between devices with their start and end apart: 8, of which 8 were waited for; matrix products, arithmetic and copies ran while one was open for 5% of the time, Pallas kernels for 0%

commit v1 on v0

v1 whole, which is shorter than its diff:
```python
from functools import partial
import math

import jax
import jax.numpy as jnp
from jax import lax
from jax.experimental import pallas as pl
from jax.experimental.pallas import tpu as pltpu
from jax.sharding import PartitionSpec as P

D = 256
FF = 1024
SIDE = 14
SW = 7
STEP = 10
HD = 32
HALF = 128
GROUP_PARAMS = 132608
SHARED_PARAMS = 526848
TOK = SIDE * SIDE
GRID = 16 * SIDE
STRIPE = 16 * SW
HEADS = HALF // HD
UNIT = 1024

eps_norm = 1e-05
keep_prob = 0.8
beta_one = 0.9
beta_two = 0.999
adam_eps = 1e-08
learn_rate = 0.04
decay_rate = 0.05

f32 = jnp.float32
bf16 = jnp.bfloat16


def window_rows(total, count):
    share = total // count
    most = max((share * k) % UNIT + share for k in range(count))
    return 16 * (-(-most // (2 * UNIT)))


def first_row(total, count, k):
    return (total // count * k) // UNIT * 8


def nn(a, b):
    return lax.dot_general(a, b, (((1,), (0,)), ((), ())), preferred_element_type=f32)


def nt(a, b):
    return lax.dot_general(a, b, (((1,), (1,)), ((), ())), preferred_element_type=f32)


def tn(a, b):
    return lax.dot_general(a, b, (((0,), (0,)), ((), ())), preferred_element_type=f32)


def norm_parts(values):
    center = values - jnp.mean(values, axis=-1, keepdims=True)
    inverse = lax.rsqrt(jnp.mean(center * center, axis=-1, keepdims=True) + eps_norm)
    return center * inverse, inverse


def norm_back(grad_after, unit, inverse, gain):
    scaled = grad_after * gain
    return inverse * (
        scaled
        - jnp.mean(scaled, axis=-1, keepdims=True)
        - unit * jnp.mean(scaled * unit, axis=-1, keepdims=True)
    )


def column_sum(values):
    return jnp.sum(values, axis=0, keepdims=True)


def head_masks(dtype):
    lane = lax.broadcasted_iota(jnp.int32, (1, HALF), 1) // HD
    return [(lane == h).astype(f32).astype(dtype) for h in range(HEADS)]


def spread_heads(values, masks):
    return jnp.concatenate([values * masks[h] for h in range(HEADS)], axis=0)


def pick_heads(stacked):
    lane = lax.broadcasted_iota(jnp.int32, (STRIPE, HALF), 1)
    picked = stacked[(HEADS - 1) * STRIPE :]
    for h in range(HEADS - 2, -1, -1):
        picked = jnp.where(lane < (h + 1) * HD, stacked[h * STRIPE : (h + 1) * STRIPE], picked)
    return picked


def row_shift(values, step):
    if step == 0:
        return values
    zero = jnp.zeros((16, HALF), f32)
    if step > 0:
        return jnp.concatenate([values[16:], zero], axis=0)
    return jnp.concatenate([zero, values[:-16]], axis=0)


def neighbours(values):
    return [pltpu.roll(values, 1, 0), values, pltpu.roll(values, STRIPE - 1, 0)]


def tile_sum(values):
    return jnp.sum(values.reshape(-1, 8, HALF), axis=0)


def place_matrices(pp_ref, ppt_ref):
    place = lax.broadcasted_iota(jnp.int32, (GRID, TOK), 0)
    token = lax.broadcasted_iota(jnp.int32, (GRID, TOK), 1)
    first, second = place // 16, place % 16
    inside = second < SIDE
    pp_ref[0] = (inside & (token == first * SIDE + second)).astype(f32).astype(bf16)
    pp_ref[1] = (inside & (token == second * SIDE + first)).astype(f32).astype(bf16)
    place = lax.broadcasted_iota(jnp.int32, (TOK, GRID), 1)
    token = lax.broadcasted_iota(jnp.int32, (TOK, GRID), 0)
    first, second = place // 16, place % 16
    inside = second < SIDE
    ppt_ref[0] = (inside & (token == first * SIDE + second)).astype(f32).astype(bf16)
    ppt_ref[1] = (inside & (token == second * SIDE + first)).astype(f32).astype(bf16)


def compute_kernel(
    n_dp,
    srows,
    grows,
    drop_ref,
    x_ref,
    co_ref,
    blocks_ref,
    out_ref,
    gin_ref,
    gblocks_ref,
    flat,
    gflat,
    pp_ref,
    ppt_ref,
    wq,
    ow,
    uw,
    dw,
    qbias,
    ubias,
    vecs,
    conv,
    a_wq,
    a_ow,
    a_uw,
    a_dwt,
    a_pb,
    a_ub,
    a_vec,
    a_conv,
    p_ref,
    qkv_ref,
):
    image = pl.program_id(0)
    n = 2 * n_dp

    @pl.when(image == 0)
    def _():
        place_matrices(pp_ref, ppt_ref)
        flat[...] = jnp.zeros_like(flat)
        gflat[...] = jnp.zeros_like(gflat)
        for k in range(n):
            at = first_row(SHARED_PARAMS, n, k)
            flat[at : at + srows] += blocks_ref[k, 0:srows].astype(f32)
            at = first_row(GROUP_PARAMS, n_dp, k // 2)
            gflat[k % 2, at : at + grows] += blocks_ref[k, srows : srows + grows].astype(f32)
        for c in range(8):
            cols = slice(c * 128, (c + 1) * 128)
            uw[:, cols] = flat[pl.ds(c, D, stride=8), :].astype(bf16)
            ubias[:, cols] = flat[2048 + c : 2049 + c, :]
        for c in range(2):
            cols = slice(c * 128, (c + 1) * 128)
            dw[:, cols] = flat[pl.ds(2056 + c, FF, stride=2), :].astype(bf16)
            for i in range(6):
                vecs[i : i + 1, cols] = flat[4104 + 2 * i + c : 4105 + 2 * i + c, :]
        for j in range(2):
            for c in range(3):
                cols = slice(j * 384 + c * 128, j * 384 + (c + 1) * 128)
                wq[:, cols] = gflat[j, pl.ds(c, D, stride=3), :].astype(bf16)
            for c in range(2):
                cols = slice(c * 128, (c + 1) * 128)
                ow[j * 128 : (j + 1) * 128, cols] = gflat[
                    j, pl.ds(770 + c, HALF, stride=2), :
                ].astype(bf16)
            qbias[:, j * 384 : j * 384 + 128] = gflat[j, 768:769, :]
            qbias[:, j * 384 + 128 : j * 384 + 256] = jnp.zeros((1, 128), f32)
            qbias[:, j * 384 + 256 : j * 384 + 384] = gflat[j, 769:770, :]
            conv[j, 0:10] = gflat[j, 1026:1036, :]
        for ref in (a_wq, a_ow, a_uw, a_dwt, a_pb, a_ub, a_vec, a_conv):
            ref[...] = jnp.zeros_like(ref)

    scale_one = drop_ref[image, 0].astype(f32) / keep_prob
    scale_two = drop_ref[image, 1].astype(f32) / keep_prob
    down_bias, gain_one, shift_one = vecs[0:1], vecs[1:2], vecs[2:3]
    gain_two, shift_two, out_bias = vecs[3:4], vecs[4:5], vecs[5:6]
    masks = head_masks(bf16)
    ones = jnp.ones((8, TOK), bf16)
    key_row = lax.broadcasted_iota(jnp.int32, (1, SW, 16, STRIPE), 2)
    scale = HD ** (-0.5)

    values = x_ref[0].astype(f32)
    unit_one, inverse_one = norm_parts(values)
    normed = (unit_one * gain_one + shift_one).astype(bf16)
    triple = (nn(normed, wq[...]) + qbias[...]).astype(bf16)
    heads_out = []
    for j in range(2):
        qkv_ref[j] = nn(pp_ref[j], triple[:, j * 384 : (j + 1) * 384]).astype(bf16)
        parts = []
        for s in range(2):
            rows = slice(s * STRIPE, (s + 1) * STRIPE)
            query = qkv_ref[j, rows, 0:128]
            keys = spread_heads(qkv_ref[j, rows, 128:256], masks)
            value = qkv_ref[j, rows, 256:384]
            scores = nt(keys, query).reshape(HEADS, SW, 16, STRIPE) * scale
            scores = jnp.where(key_row < SIDE, scores, -1e30)
            scores = scores.reshape(HEADS, STRIPE, STRIPE)
            weights = jnp.exp(scores - jnp.max(scores, axis=1, keepdims=True))
            probs = weights * (1.0 / jnp.sum(weights, axis=1, keepdims=True))
            probs = probs.reshape(HEADS * STRIPE, STRIPE)
            p_ref[2 * j + s] = probs
            attended = tn(probs.astype(bf16), spread_heads(value, masks))
            near = neighbours(value.astype(f32))
            total = attended + conv[j, 9:10]
            for a in range(3):
                part = near[0] * conv[j, 3 * a : 3 * a + 1]
                for b in range(1, 3):
                    part = part + near[b] * conv[j, 3 * a + b : 3 * a + b + 1]
                total = total + row_shift(part, a - 1)
            parts.append(total.astype(bf16))
        padded = jnp.concatenate(parts, axis=0)
        heads_out.append(nn(ppt_ref[j], padded).astype(bf16))
    heads_out = jnp.concatenate(heads_out, axis=1)
    branch = nn(heads_out, ow[...])
    middle = values + scale_one * (branch + out_bias)
    unit_two, inverse_two = norm_parts(middle)
    normed_two = (unit_two * gain_two + shift_two).astype(bf16)
    grad_output = co_ref[0].astype(f32)
    grad_mlp_f = scale_two * grad_output
    a_vec[0:1] += column_sum(grad_mlp_f)
    grad_mlp = grad_mlp_f.astype(bf16)
    mlp = None
    grad_normed_two = None
    for c in range(4):
        cols = slice(c * 256, (c + 1) * 256)
        hidden = nn(normed_two, uw[:, cols]) + ubias[:, cols]
        density = jnp.exp(hidden * hidden * -0.5) * (1.0 / math.sqrt(2.0 * math.pi))
        phi = 0.5 + 0.5 * lax.erf(hidden * math.sqrt(0.5))
        active = (hidden * phi).astype(bf16)
        part = nn(active, dw[cols, :])
        mlp = part if mlp is None else mlp + part
        a_dwt[:, cols] += tn(grad_mlp, active)
        grad_active = nt(grad_mlp, dw[cols, :])
        grad_hidden = (grad_active * (phi + hidden * density)).astype(bf16)
        a_ub[:, cols] += nn(ones, grad_hidden)
        a_uw[:, cols] += tn(normed_two, grad_hidden)
        part = nt(grad_hidden, uw[:, cols])
        grad_normed_two = part if grad_normed_two is None else grad_normed_two + part
    out_ref[0] = middle + scale_two * (mlp + down_bias)

    a_vec[3:4] += column_sum(grad_normed_two * unit_two)
    a_vec[4:5] += column_sum(grad_normed_two)
    grad_middle = grad_output + norm_back(grad_normed_two, unit_two, inverse_two, gain_two)
    grad_branch_f = scale_one * grad_middle
    a_vec[5:6] += column_sum(grad_branch_f)
    grad_branch = grad_branch_f.astype(bf16)
    a_ow[...] += tn(heads_out, grad_branch)
    grad_heads = nt(grad_branch, ow[...]).astype(bf16)
    grad_triple = []
    for j in range(2):
        padded = nn(pp_ref[j], grad_heads[:, j * 128 : (j + 1) * 128])
        parts = []
        for s in range(2):
            rows = slice(s * STRIPE, (s + 1) * STRIPE)
            query = qkv_ref[j, rows, 0:128]
            keys = spread_heads(qkv_ref[j, rows, 128:256], masks)
            value = qkv_ref[j, rows, 256:384]
            grad_f = padded[rows]
            grad = grad_f.astype(bf16)
            probs = p_ref[2 * j + s]
            grad_probs = nt(spread_heads(value, masks), grad)
            product = (probs * grad_probs).reshape(HEADS, STRIPE, STRIPE)
            inner = jnp.sum(product, axis=1, keepdims=True)
            probs_three = probs.reshape(HEADS, STRIPE, STRIPE)
            grad_scores = product - probs_three * inner
            grad_scores = grad_scores.reshape(HEADS * STRIPE, STRIPE).astype(bf16)
            grad_query = tn(grad_scores, keys) * scale
            grad_key = pick_heads(nn(grad_scores, query)) * scale
            grad_value = pick_heads(nn(probs.astype(bf16), grad))
            near = neighbours(grad_f)
            for a in range(3):
                part = near[2] * conv[j, 3 * a : 3 * a + 1]
                for b in range(1, 3):
                    part = part + near[2 - b] * conv[j, 3 * a + b : 3 * a + b + 1]
                grad_value = grad_value + row_shift(part, 1 - a)
            near = neighbours(value.astype(f32))
            for b in range(3):
                a_conv[j, b] += tile_sum(grad_f[16:] * near[b][:-16])
                a_conv[j, 3 + b] += tile_sum(grad_f * near[b])
                a_conv[j, 6 + b] += tile_sum(grad_f[:-16] * near[b][16:])
            a_conv[j, 9] += tile_sum(grad_f)
            parts.append(
                jnp.concatenate([grad_query, grad_key, grad_value], axis=1).astype(bf16)
            )
        both = jnp.concatenate(parts, axis=0)
        grad_triple.append(nn(ppt_ref[j], both).astype(bf16))
    grad_triple = jnp.concatenate(grad_triple, axis=1)
    a_pb[...] += nn(ones, grad_triple)
    a_wq[...] += tn(normed, grad_triple)
    grad_normed = nt(grad_triple, wq[...])
    a_vec[1:2] += column_sum(grad_normed * unit_one)
    a_vec[2:3] += column_sum(grad_normed)
    gin_ref[0] = grad_middle + norm_back(grad_normed, unit_one, inverse_one, gain_one)

    @pl.when(image == pl.num_programs(0) - 1)
    def _():
        for c in range(8):
            cols = slice(c * 128, (c + 1) * 128)
            flat[pl.ds(c, D, stride=8), :] = a_uw[:, cols]
            flat[2048 + c : 2049 + c, :] = a_ub[0:1, cols]
        for q in range(4):
            turned = a_dwt[:, q * 256 : (q + 1) * 256].T
            for c in range(2):
                flat[pl.ds(2056 + 512 * q + c, 256, stride=2), :] = turned[
                    :, c * 128 : (c + 1) * 128
                ]
        for c in range(2):
            cols = slice(c * 128, (c + 1) * 128)
            for i in range(6):
                flat[4104 + 2 * i + c : 4105 + 2 * i + c, :] = a_vec[i : i + 1, cols]
        for j in range(2):
            for c in range(3):
                cols = slice(j * 384 + c * 128, j * 384 + (c + 1) * 128)
                gflat[j, pl.ds(c, D, stride=3), :] = a_wq[:, cols]
            for c in range(2):
                cols = slice(c * 128, (c + 1) * 128)
                gflat[j, pl.ds(770 + c, HALF, stride=2), :] = a_ow[
                    j * 128 : (j + 1) * 128, cols
                ]
            gflat[j, 768:769, :] = a_pb[0:1, j * 384 : j * 384 + 128]
            gflat[j, 769:770, :] = a_pb[0:1, j * 384 + 256 : j * 384 + 384]
            for i in range(10):
                gflat[j, 1026 + i : 1027 + i, :] = column_sum(a_conv[j, i])
        for k in range(n):
            at = first_row(SHARED_PARAMS, n, k)
            gblocks_ref[k, 0:srows] = flat[at : at + srows].astype(bf16)
            at = first_row(GROUP_PARAMS, n_dp, k // 2)
            gblocks_ref[k, srows : srows + grows] = gflat[k % 2, at : at + grows].astype(bf16)


def compute(n_dp, srows, grows, drops, images, cotangent, blocks):
    n = 2 * n_dp
    count = images.shape[0]
    rows = srows + grows
    flat_rows = max(4120, first_row(SHARED_PARAMS, n, n - 1) + srows)
    gflat_rows = max(1040, first_row(GROUP_PARAMS, n_dp, n_dp - 1) + grows)
    one_image = lambda i: (i, 0, 0)
    whole = lambda i: (0, 0, 0)
    return pl.pallas_call(
        partial(compute_kernel, n_dp, srows, grows),
        grid=(count,),
        in_specs=[
            pl.BlockSpec(memory_space=pltpu.SMEM),
            pl.BlockSpec((1, TOK, D), one_image),
            pl.BlockSpec((1, TOK, D), one_image),
            pl.BlockSpec((n, rows, 128), whole, pipeline_mode=pl.Buffered(1)),
        ],
        out_specs=[
            pl.BlockSpec((1, TOK, D), one_image),
            pl.BlockSpec((1, TOK, D), one_image),
            pl.BlockSpec((n, rows, 128), whole, pipeline_mode=pl.Buffered(1)),
        ],
        out_shape=[
            jax.ShapeDtypeStruct((count, TOK, D), f32),
            jax.ShapeDtypeStruct((count, TOK, D), f32),
            jax.ShapeDtypeStruct((n, rows, 128), bf16),
        ],
        scratch_shapes=[
            pltpu.VMEM((flat_rows, 128), f32),
            pltpu.VMEM((2, gflat_rows, 128), f32),
            pltpu.VMEM((2, GRID, TOK), bf16),
            pltpu.VMEM((2, TOK, GRID), bf16),
            pltpu.VMEM((D, 768), bf16),
            pltpu.VMEM((D, D), bf16),
            pltpu.VMEM((D, FF), bf16),
            pltpu.VMEM((FF, D), bf16),
            pltpu.VMEM((1, 768), f32),
            pltpu.VMEM((1, FF), f32),
            pltpu.VMEM((8, D), f32),
            pltpu.VMEM((2, 16, 128), f32),
            pltpu.VMEM((D, 768), f32),
            pltpu.VMEM((D, D), f32),
            pltpu.VMEM((D, FF), f32),
            pltpu.VMEM((D, FF), f32),
            pltpu.VMEM((8, 768), f32),
            pltpu.VMEM((8, FF), f32),
            pltpu.VMEM((8, D), f32),
            pltpu.VMEM((2, 10, 8, 128), f32),
            pltpu.VMEM((4, HEADS * STRIPE, STRIPE), f32),
            pltpu.VMEM((2, GRID, 384), bf16),
        ],
        compiler_params=pltpu.CompilerParams(
            dimension_semantics=("arbitrary",), vmem_limit_bytes=56 * 1024 * 1024
        ),
        name="block",
    )(drops, images, cotangent, blocks)


def adam_step(master, gradient, first, second, step):
    first_new = beta_one * first + (1.0 - beta_one) * gradient
    second_new = beta_two * second + (1.0 - beta_two) * gradient * gradient
    first_hat = first_new / (1.0 - jnp.power(jnp.float32(beta_one), step))
    second_hat = second_new / (1.0 - jnp.power(jnp.float32(beta_two), step))
    master_new = master - learn_rate * (
        first_hat / (jnp.sqrt(second_hat) + adam_eps) + decay_rate * master
    )
    return (master_new, first_new, second_new)


def on_device(
    n_dp,
    images,
    cotangent,
    drop_masks,
    group_master,
    group_m1,
    group_m2,
    shared_master,
    shared_m1,
    shared_m2,
):
    n = 2 * n_dp
    srows = window_rows(SHARED_PARAMS, n)
    grows = window_rows(GROUP_PARAMS, n_dp)
    dp = lax.axis_index("dp")
    me = dp * 2 + lax.axis_index("heads")
    sshare, gshare = SHARED_PARAMS // n, GROUP_PARAMS // n_dp
    soff = lax.rem(me * sshare, UNIT)
    goff = lax.rem(dp * gshare, UNIT)
    sblock = lax.dynamic_update_slice(jnp.zeros((srows * 128,), f32), shared_master, (soff,))
    gblock = lax.dynamic_update_slice(jnp.zeros((grows * 128,), f32), group_master[0], (goff,))
    block = jnp.concatenate(
        [sblock.reshape(srows, 128), gblock.reshape(grows, 128)], axis=0
    ).astype(bf16)
    blocks = lax.all_gather(block, ("dp", "heads"), axis=0)
    output, input_grad, gblocks = compute(
        n_dp, srows, grows, drop_masks, images, cotangent, blocks
    )
    mine = lax.psum_scatter(gblocks, ("dp", "heads"), scatter_dimension=0).astype(f32)
    shared_share = lax.dynamic_slice(mine[:srows].reshape(-1), (soff,), (sshare,))
    group_share = lax.dynamic_slice(mine[srows:].reshape(-1), (goff,), (gshare,))
    group_share = group_share[None, :]
    squares = jnp.sum(group_share * group_share) + jnp.sum(shared_share * shared_share)
    grad_norm = jnp.sqrt(lax.psum(squares, ("dp", "heads")))
    threshold = math.sqrt(2 * GROUP_PARAMS + SHARED_PARAMS)
    factor = jnp.minimum(1.0, threshold / (grad_norm + 1e-06))
    group_grad = group_share * factor
    shared_grad = shared_share * factor
    step = jnp.float32(STEP)
    group_new, group_first, group_second = adam_step(
        group_master, group_grad, group_m1, group_m2, step
    )
    shared_new, shared_first, shared_second = adam_step(
        shared_master, shared_grad, shared_m1, shared_m2, step
    )
    return (
        output,
        input_grad,
        grad_norm.reshape(1),
        group_grad,
        group_new,
        group_first,
        group_second,
        group_new.astype(jnp.bfloat16),
        shared_grad,
        shared_new,
        shared_first,
        shared_second,
        shared_new.astype(jnp.bfloat16),
    )


def solution(mesh):
    both = P(("dp", "heads"))
    rows = P(("dp", "heads"), None, None)
    split = P("heads", "dp")
    in_specs = (rows, rows, P(("dp", "heads"), None), split, split, split, both, both, both)
    out_specs = (rows, rows, P(), split, split, split, split, split, both, both, both, both, both)
    return jax.shard_map(
        partial(on_device, mesh.shape["dp"]),
        mesh=mesh,
        in_specs=in_specs,
        out_specs=out_specs,
        check_vma=False,
    )
```

time: 831 us -> 321 us (0.39)
  waiting for transfers between devices: 527 us -> 188 us
  local copies, waits for them, and re-layouts: 134 us -> 11.6 us
  Pallas kernels: 0 us -> 60.7 us
  matrix products: 51 us -> 0 us
  other arithmetic: 50.9 us -> 5.54 us
    unnamed x12 -> x2, waiting for transfers between devices: 438 us -> 0.03 us
    reduce_scatter x2 -> x1, waiting for transfers between devices: 42.5 us -> 133 us  [on_device(): lax.psum_scatter(gblocks, ('dp', 'heads'), scatter_dimension=0).astype(f32)]
    pallas_call x0 -> x1, Pallas kernels: none -> 60.7 us  [compute(): pl.pallas_call(partial(compute_kernel, n_dp, srows, grows), grid=(count,)...]
    dot_general x18 -> x0, matrix products: 51 us -> none  [the longest x1 6.59 us: attend_back(): jnp.einsum('nshqk,nsqhd->nskhd', softmax_low, grad_rows, preferred_elemen...]
    unnamed x190 -> x23, local copies, waits for them, and re-layouts: 52.9 us -> 9.31 us
    another operation x7 -> x0, local copies, waits for them, and re-layouts: 30.8 us -> none  [the longest x2 8.49 us: attend_back(): to_stripes(grad_heads, turned)]
    convert_element_type x12 -> x1, other arithmetic: 24.4 us -> 0.83 us  [on_device(): lax.psum_scatter(gblocks, ('dp', 'heads'), scatter_dimension=0).astype(f32)]
    convert_element_type x7 -> x0, local copies, waits for them, and re-layouts: 17.4 us -> none  [the longest x3 14.9 us: attend(): value_part.astype(jnp.float32).reshape(number, stripes, SW, SIDE, half)]
  transfers between devices with their start and end apart: 8 -> 2, of which waited for: 8 -> 2; matrix products, arithmetic and copies ran while one was open for 5% -> 2% of each run, Pallas kernels for 0% -> 0%
where the time goes in v1:
time: 321 us; the launch traced here: 320 us
  waiting for transfers between devices  188 us (59%)
  Pallas kernels  60.7 us (19%)
  blocking collectives  36.8 us (11%)
  between operations  17.4 us (5%)
  local copies, waits for them, and re-layouts  11.6 us (4%)
  other arithmetic  5.54 us (2%)
    reduce_scatter x1, waiting for transfers between devices, on_device(): lax.psum_scatter(gblocks, ('dp', 'heads'), scatter_dimension=0).astype(f32)  133 us
    pallas_call x1, Pallas kernels, compute(): pl.pallas_call(partial(compute_kernel, n_dp, srows, grows), grid=(count,)...  60.7 us
    all_gather x1, waiting for transfers between devices, on_device(): blocks = lax.all_gather(block, ('dp', 'heads'), axis=0)  55.1 us
    psum x1, blocking collectives, on_device(): grad_norm = jnp.sqrt(lax.psum(squares, ('dp', 'heads')))  36.8 us
    unnamed x23, local copies, waits for them, and re-layouts  9.31 us
  transfers between devices with their start and end apart: 2, of which 2 were waited for; matrix products, arithmetic and copies ran while one was open for 2% of the time, Pallas kernels for 0%

profile of v1, /device:TPU:0, one launch (start us, length us, event | category | flops | bytes accessed | tf_op | source)
XLA Modules:
  0.0 319.7 jit_solution(4898070690546305727)
XLA Ops:
  7.2 0.0 copy-start.2
  7.2 0.0 all-gather.2.cloned.1.call-start
  7.3 0.9 reduce.2
  8.2 0.4 dynamic_update_slice.7
  8.6 1.2 dynamic_update_slice.6
  9.8 0.6 pad_maximum_fusion
  10.4 0.0 all-gather.2.cloned.1.call-update
  10.4 0.0 reduce-scatter.2.cloned.1.call-start
  10.5 1.3 copy.27.drop_ref
  11.8 2.2 copy.28.x_ref
  14.0 0.0 copy-done.2
  14.0 1.0 copy.29.co_ref
  15.1 55.1 %all-gather.2.cloned.1.call-done.blocks_ref = bf16[32,224,128]{2,1,0:T(8,128)(2,1)} async-done(((bf16[1,224,128]{2,1,0:T(8,128)(2,1)}), bf16[32,224,128]{2,1,0:T(8,128)(2,1)}) %all-gather.2.cloned.1.call-update) | async-done | bytes 1835024 | tf_op jit(solution)/shard_map/all_gather | solution.py:452
  70.1 60.7 %block.1 = (f32[8,196,256]{2,1,0:T(8,128)}, f32[8,196,256]{2,1,0:T(8,128)}, bf16[32,224,128]{2,1,0:T(8,128)(2,1)}) custom-call(s32[8,2]{1,0:T(8,128)} %copy.27.drop_ref, bf16[8,196,256]{2,1,0:T(8,128)(2,1)} %copy.28.x_ref, bf16[8,196,256]{2,1,0:T(8,128)(2,1)} %copy.29.co_ref, bf16[32,224,128]{2,1,0:T(8,128)(2,1)} %all-gather.2.cloned.1.call-done.blocks_ref), custom_call_target="tpu_custom_call" | custom-call | tf_op jit(solution)/shard_map/block/pallas_call | solution.py:366
  130.8 0.0 copy-start.1
  130.9 0.0 reduce-scatter.2.cloned.1.call-update
  130.9 1.4 copy-done.1
  132.3 0.0 copy-start
  132.3 1.6 copy.30
  133.9 132.5 %reduce-scatter.2.cloned.1.call-done = bf16[1,224,128]{2,1,0:T(8,128)(2,1)} async-done(((bf16[32,224,128]{2,1,0:T(8,128)(2,1)}), bf16[1,224,128]{2,1,0:T(8,128)(2,1)}) %reduce-scatter.2.cloned.1.call-update) | async-done | bytes 57360 | tf_op jit(solution)/shard_map/reduce_scatter | solution.py:456
  266.4 0.8 convert_element_type.18
  267.3 0.7 multiply_reduce_fusion.1
  268.0 0.7 multiply_reduce_fusion
  270.0 0.0 copy-done
  270.0 0.0 copy-start.3
  270.0 0.0 copy-start.5
  270.0 0.0 copy-start.6
  270.0 0.0 copy-start.4
  270.0 0.0 copy-start.7
  270.1 0.0 copy-start.8
  270.1 1.6 copy.31
  271.7 36.8 %psum.7 = f32[]{:T(128)} all-reduce(f32[]{:T(128)S(6)} %add.54), channel_id=1, replica_groups=mesh['dp'=16,'heads'=2] {'dp','heads'}, use_global_device_ids=true, to_apply=%region_3.0 | all-reduce | flops 1 | bytes 8 | tf_op jit(solution)/shard_map/psum | solution.py:461
  309.3 0.1 multiply_multiply_fusion.1
  309.4 0.6 mul.123
  310.0 0.0 copy-done.3
  310.0 0.0 copy-done.5
  310.0 0.0 copy-done.6
  310.0 0.8 fusion.1
  310.9 0.0 copy-done.4
  310.9 0.0 copy-done.7
  310.9 0.0 copy-done.8
  310.9 0.9 fusion.3
  (5 shorter events, 0.0 us)
Async XLA Ops:
  7.2 6.8 %copy-start.2 = (bf16[8,196,256]{2,0,1:T(8,128)(2,1)S(1)}, bf16[8,196,256]{2,0,1:T(8,128)(2,1)}, u32[]{:S(2)}) copy-start(bf16[8,196,256]{2,0,1:T(8,128)(2,1)} %param.10) | copy-start | bytes 2408452
  7.2 63.0 %all-gather.2.cloned.1.call-start = ((), (), s32[]{:S(2)}) async-start(), calls=%async_computation.1 | async-start | bytes 1892352 | tf_op jit(solution)/shard_map/all_gather | solution.py:452
  10.4 256.0 %reduce-scatter.2.cloned.1.call-start = ((), (), s32[]{:S(2)}) async-start(), calls=%async_computation.2 | async-start | bytes 1892352 | tf_op jit(solution)/shard_map/reduce_scatter | solution.py:456
  130.8 1.4 copy-start.1
  132.3 137.7 %copy-start = (f32[8,196,256]{2,1,0:T(8,128)S(1)}, f32[8,196,256]{2,1,0:T(8,128)}, u32[]{:S(2)}) copy-start(f32[8,196,256]{2,1,0:T(8,128)} %get-tuple-element.33) | copy-start | bytes 4816900
  270.0 40.0 %copy-start.3 = (f32[16464]{0:T(1024)S(1)}, f32[16464]{0:T(1024)}, u32[]{:S(2)}) copy-start(f32[16464]{0:T(1024)} %param.15) | copy-start | bytes 197572
  270.0 40.0 %copy-start.5 = (f32[16464]{0:T(1024)S(1)}, f32[16464]{0:T(1024)}, u32[]{:S(2)}) copy-start(f32[16464]{0:T(1024)} %param.17) | copy-start | bytes 197572
  270.0 40.0 %copy-start.6 = (f32[16464]{0:T(1024)S(1)}, f32[16464]{0:T(1024)}, u32[]{:S(2)}) copy-start(f32[16464]{0:T(1024)} %param.16) | copy-start | bytes 197572
  270.0 40.8 %copy-start.4 = (f32[1,8288]{1,0:T(1,128)S(1)}, f32[1,8288]{1,0:T(1,128)}, u32[]{:S(2)}) copy-start(f32[1,8288]{1,0:T(1,128)} %param.12) | copy-start | bytes 99460
  270.0 40.8 %copy-start.7 = (f32[1,8288]{1,0:T(1,128)S(1)}, f32[1,8288]{1,0:T(1,128)}, u32[]{:S(2)}) copy-start(f32[1,8288]{1,0:T(1,128)} %param.14) | copy-start | bytes 99460
  270.1 40.8 %copy-start.8 = (f32[1,8288]{1,0:T(1,128)S(1)}, f32[1,8288]{1,0:T(1,128)}, u32[]{:S(2)}) copy-start(f32[1,8288]{1,0:T(1,128)} %param.13) | copy-start | bytes 99460
Sparse Core Ops, SparseCore 0:
  11.5 58.5 all-gather.1
  131.0 135.4 reduce-scatter.1

commit v2 on v1

--- a/solution.py
+++ b/solution.py
@@ -45,6 +45,283 @@
     return (total // count * k) // UNIT * 8
 
 
+HEADS_BIT = -1
+FAST_BITS = 2
+
+
+def exchange_orders(n_dp):
+    bits = n_dp.bit_length() - 1
+    far = list(range(bits - 1, 1, -1))
+    near = [1] if bits > 1 else []
+    core = [0] if bits > 0 else []
+    return far + near + [HEADS_BIT] + core, far + [HEADS_BIT] + near + core
+
+
+def place_of(order, k):
+    dp, heads = k // 2, k % 2
+    return sum(
+        (heads if bit == HEADS_BIT else (dp >> bit) & 1) << t for t, bit in enumerate(order)
+    )
+
+
+def own_bits(order):
+    dp, heads = lax.axis_index("dp"), lax.axis_index("heads")
+    return [heads if bit == HEADS_BIT else (dp // (1 << bit)) % 2 for bit in order]
+
+
+def partner(bit):
+    if bit == HEADS_BIT:
+        return {"heads": 1 - lax.axis_index("heads")}
+    dp = lax.axis_index("dp")
+    return {"dp": dp + (1 << bit) * (1 - 2 * ((dp // (1 << bit)) % 2))}
+
+
+def half_rows(rows):
+    first = 16 * (-(-rows // 32))
+    return first, rows - first
+
+
+def greet(devices):
+    barrier = pltpu.get_barrier_semaphore()
+    for device in devices:
+        pl.semaphore_signal(barrier, inc=1, device_id=device)
+    pl.semaphore_wait(barrier, len(devices))
+
+
+def gather_kernel(orders, halves, own_ref, first_ref, second_ref, send_sem, recv_sem):
+    greet([partner(bit) for bit in orders[0]])
+    outs = (first_ref, second_ref)
+    start = 0
+    pending = []
+    bits = [own_bits(order) for order in orders]
+    for h in range(2):
+        mine = sum(b * (1 << t) for t, b in enumerate(bits[h]))
+        outs[h][mine] = own_ref[start : start + halves[h]].astype(bf16)
+        start += halves[h]
+        pending.append(None)
+    for t in range(len(orders[0])):
+        for h in range(2):
+            if pending[h] is not None:
+                pending[h].wait()
+            base = sum(b * (1 << u) for u, b in enumerate(bits[h]) if u >= t)
+            held = outs[h].at[pl.ds(base, 1 << t)]
+            pending[h] = pltpu.make_async_remote_copy(
+                src_ref=held,
+                dst_ref=held,
+                send_sem=send_sem.at[h, t],
+                recv_sem=recv_sem.at[h, t],
+                device_id=partner(orders[h][t]),
+            )
+            pending[h].start()
+    for h in range(2):
+        pending[h].wait()
+
+
+def gather(n_dp, rows, own):
+    n = 2 * n_dp
+    orders = exchange_orders(n_dp)
+    halves = half_rows(rows)
+    stages = len(orders[0])
+    return pl.pallas_call(
+        partial(gather_kernel, orders, halves),
+        in_specs=[pl.BlockSpec(memory_space=pltpu.VMEM)],
+        out_specs=[pl.BlockSpec(memory_space=pltpu.VMEM)] * 2,
+        out_shape=[jax.ShapeDtypeStruct((n, half, 128), bf16) for half in halves],
+        scratch_shapes=[
+            pltpu.SemaphoreType.DMA((2, stages)),
+            pltpu.SemaphoreType.DMA((2, stages)),
+        ],
+        compiler_params=pltpu.CompilerParams(collective_id=0, has_side_effects=True),
+        name="gather",
+    )(own)
+
+
+def group_peers(n_dp):
+    dp, heads = lax.axis_index("dp"), lax.axis_index("heads")
+    fast = min(1 << FAST_BITS, n_dp)
+    low, high = dp % fast, dp // fast
+    count = 2 * fast
+    me = low * 2 + heads
+    near = []
+    for step in range(1, count):
+        other = (me + step) % count
+        near.append((other, {"dp": high * fast + other // 2, "heads": other % 2}))
+    far = []
+    for step in range(1, n_dp // fast):
+        other = (high + step) % (n_dp // fast)
+        far.append((other, {"dp": other * fast + low}))
+    return (me, near), (high, far)
+
+
+def all_share(me, peers, stat_ref, send_sem, recv_sem):
+    copies = []
+    for other, device in peers:
+        copy = pltpu.make_async_remote_copy(
+            src_ref=stat_ref.at[me],
+            dst_ref=stat_ref.at[me],
+            send_sem=send_sem.at[other],
+            recv_sem=recv_sem.at[me],
+            device_id=device,
+        )
+        copy.start()
+        copies.append(copy)
+    for other, device in peers:
+        pltpu.make_async_remote_copy(
+            src_ref=stat_ref.at[other],
+            dst_ref=stat_ref.at[other],
+            send_sem=send_sem.at[other],
+            recv_sem=recv_sem.at[other],
+            device_id=device,
+        ).wait_recv()
+    for copy in copies:
+        copy.wait_send()
+    return jnp.sum(stat_ref[...], axis=0)
+
+
+def reduce_kernel(
+    n_dp,
+    srows,
+    orders,
+    halves,
+    first_ref,
+    second_ref,
+    out_ref,
+    norm_ref,
+    acc_first,
+    acc_second,
+    out_first,
+    out_second,
+    in_first,
+    in_second,
+    near_stat,
+    far_stat,
+    send_sem,
+    recv_sem,
+    near_send,
+    near_recv,
+    far_send,
+    far_recv,
+):
+    n = 2 * n_dp
+    (near_me, near), (far_me, far) = group_peers(n_dp)
+    greet([device for _, device in near] + [device for _, device in far])
+    stages = len(orders[0])
+    held = [first_ref, second_ref]
+    accs = (acc_first, acc_second)
+    outgoing = (out_first, out_second)
+    incoming = (in_first, in_second)
+    bits = [own_bits(order) for order in orders]
+    pending = [None, None]
+    start = [0, halves[0]]
+    for t in range(stages - 1, -1, -1):
+        count = 1 << t
+        for h in range(2):
+            source = held[h]
+            if pending[h] is not None:
+                pending[h].wait()
+            arrived = 2 * count - 1
+            keep, give = bits[h][t] * count, (1 - bits[h][t]) * count
+
+            def value(i, at, h=h, source=source, arrived=arrived, last=pending[h] is None):
+                got = source[at + i]
+                if last:
+                    return got
+                return got + incoming[h][arrived + at + i].astype(f32)
+
+            def fill(i, carry, h=h, give=give, count=count, value=value):
+                outgoing[h][count - 1 + i] = value(i, give).astype(bf16)
+                return carry
+
+            lax.fori_loop(0, count, fill, 0)
+            copy = pltpu.make_async_remote_copy(
+                src_ref=outgoing[h].at[pl.ds(count - 1, count)],
+                dst_ref=incoming[h].at[pl.ds(count - 1, count)],
+                send_sem=send_sem.at[h, t],
+                recv_sem=recv_sem.at[h, t],
+                device_id=partner(orders[h][t]),
+            )
+            copy.start()
+            pending[h] = copy
+
+            def retain(i, carry, h=h, keep=keep, count=count, value=value):
+                accs[h][count - 1 + i] = value(i, keep)
+                return carry
+
+            lax.fori_loop(0, count, retain, 0)
+            held[h] = accs[h].at[pl.ds(count - 1, count)]
+    dp = lax.axis_index("dp")
+    me = dp * 2 + lax.axis_index("heads")
+    sshare, gshare = SHARED_PARAMS // n, GROUP_PARAMS // n_dp
+    soff = (me * sshare) % UNIT
+    goff = (dp * gshare) % UNIT
+    total = jnp.zeros((8, 128), f32)
+    for h in range(2):
+        pending[h].wait()
+        value = held[h][0] + incoming[h][0].astype(f32)
+        out_ref[start[h] : start[h] + halves[h]] = value
+        row = lax.broadcasted_iota(jnp.int32, (halves[h], 128), 0) + start[h]
+        place = row * 128 + lax.broadcasted_iota(jnp.int32, (halves[h], 128), 1)
+        shared = (row < srows) & (place >= soff) & (place < soff + sshare)
+        place = place - srows * 128
+        grouped = (row >= srows) & (place >= goff) & (place < goff + gshare)
+        own = jnp.where(shared | grouped, value, 0.0)
+        total = total + jnp.sum((own * own).reshape(-1, 8, 128), axis=0)
+    near_stat[near_me] = total
+    far_stat[far_me] = all_share(near_me, near, near_stat, near_send, near_recv)
+    total = all_share(far_me, far, far_stat, far_send, far_recv)
+    total = jnp.sum(jnp.sum(total, axis=0, keepdims=True), axis=1, keepdims=True)
+    norm = jnp.sqrt(total)
+    norm_ref[...] = jnp.broadcast_to(norm, (8, 128))
+    threshold = math.sqrt(2 * GROUP_PARAMS + SHARED_PARAMS)
+    out_ref[...] = out_ref[...] * jnp.minimum(1.0, threshold / (norm + 1e-06))
+
+
+def reduce(n_dp, srows, first, second):
+    n = 2 * n_dp
+    orders = exchange_orders(n_dp)
+    halves = (first.shape[1], second.shape[1])
+    stages = len(orders[0])
+    fast = min(1 << FAST_BITS, n_dp)
+    near, far = 2 * fast, n_dp // fast
+    dma = pltpu.SemaphoreType.DMA
+    return pl.pallas_call(
+        partial(reduce_kernel, n_dp, srows, orders, halves),
+        in_specs=[pl.BlockSpec(memory_space=pltpu.VMEM)] * 2,
+        out_specs=[pl.BlockSpec(memory_space=pltpu.VMEM)] * 2,
+        out_shape=[
+            jax.ShapeDtypeStruct((sum(halves), 128), f32),
+            jax.ShapeDtypeStruct((8, 128), f32),
+        ],
+        scratch_shapes=[pltpu.VMEM((n - 1, half, 128), f32) for half in halves]
+        + [pltpu.VMEM((n - 1, half, 128), bf16) for half in halves] * 2
+        + [
+            pltpu.VMEM((near, 8, 128), f32),
+            pltpu.VMEM((far, 8, 128), f32),
+            dma((2, stages)),
+            dma((2, stages)),
+            dma((near,)),
+            dma((near,)),
+            dma((far,)),
+            dma((far,)),
+        ],
+        compiler_params=pltpu.CompilerParams(
+            collective_id=1, has_side_effects=True, vmem_limit_bytes=56 * 1024 * 1024
+        ),
+        name="reduce",
+    )(first, second)
+
+
+def window_parts(halves, rows):
+    parts = []
+    start = 0
+    for h, size in enumerate(halves):
+        low, high = max(rows[0], start), min(rows[1], start + size)
+        if low < high:
+            parts.append((h, low - start, high - start, low - rows[0], high - rows[0]))
+        start += size
+    return parts
+
+
 def nn(a, b):
     return lax.dot_general(a, b, (((1,), (0,)), ((), ())), preferred_element_type=f32)
 
@@ -129,13 +406,17 @@
     n_dp,
     srows,
     grows,
+    orders,
+    halves,
     drop_ref,
     x_ref,
     co_ref,
-    blocks_ref,
+    first_ref,
+    second_ref,
     out_ref,
     gin_ref,
-    gblocks_ref,
+    gfirst_ref,
+    gsecond_ref,
     flat,
     gflat,
     pp_ref,
@@ -161,6 +442,9 @@
 ):
     image = pl.program_id(0)
     n = 2 * n_dp
+    weights, gradients = (first_ref, second_ref), (gfirst_ref, gsecond_ref)
+    shared_parts = window_parts(halves, (0, srows))
+    group_parts = window_parts(halves, (srows, srows + grows))
 
     @pl.when(image == 0)
     def _():
@@ -169,9 +453,13 @@
         gflat[...] = jnp.zeros_like(gflat)
         for k in range(n):
             at = first_row(SHARED_PARAMS, n, k)
-            flat[at : at + srows] += blocks_ref[k, 0:srows].astype(f32)
+            for h, low, high, begin, end in shared_parts:
+                window = weights[h][place_of(orders[h], k), low:high]
+                flat[at + begin : at + end] += window.astype(f32)
             at = first_row(GROUP_PARAMS, n_dp, k // 2)
-            gflat[k % 2, at : at + grows] += blocks_ref[k, srows : srows + grows].astype(f32)
+            for h, low, high, begin, end in group_parts:
+                window = weights[h][place_of(orders[h], k), low:high]
+                gflat[k % 2, at + begin : at + end] += window.astype(f32)
         for c in range(8):
             cols = slice(c * 128, (c + 1) * 128)
             uw[:, cols] = flat[pl.ds(c, D, stride=8), :].astype(bf16)
@@ -350,38 +638,46 @@
                 gflat[j, 1026 + i : 1027 + i, :] = column_sum(a_conv[j, i])
         for k in range(n):
             at = first_row(SHARED_PARAMS, n, k)
-            gblocks_ref[k, 0:srows] = flat[at : at + srows].astype(bf16)
+            for h, low, high, begin, end in shared_parts:
+                gradients[h][place_of(orders[h], k), low:high] = flat[at + begin : at + end]
             at = first_row(GROUP_PARAMS, n_dp, k // 2)
-            gblocks_ref[k, srows : srows + grows] = gflat[k % 2, at : at + grows].astype(bf16)
-
-
-def compute(n_dp, srows, grows, drops, images, cotangent, blocks):
+            for h, low, high, begin, end in group_parts:
+                gradients[h][place_of(orders[h], k), low:high] = gflat[
+                    k % 2, at + begin : at + end
+                ]
+
+
+def compute(n_dp, srows, grows, drops, images, cotangent, first, second):
     n = 2 * n_dp
     count = images.shape[0]
-    rows = srows + grows
+    halves = (first.shape[1], second.shape[1])
     flat_rows = max(4120, first_row(SHARED_PARAMS, n, n - 1) + srows)
     gflat_rows = max(1040, first_row(GROUP_PARAMS, n_dp, n_dp - 1) + grows)
     one_image = lambda i: (i, 0, 0)
     whole = lambda i: (0, 0, 0)
     return pl.pallas_call(
-        partial(compute_kernel, n_dp, srows, grows),
+        partial(compute_kernel, n_dp, srows, grows, exchange_orders(n_dp), halves),
         grid=(count,),
         in_specs=[
             pl.BlockSpec(memory_space=pltpu.SMEM),
             pl.BlockSpec((1, TOK, D), one_image),
             pl.BlockSpec((1, TOK, D), one_image),
-            pl.BlockSpec((n, rows, 128), whole, pipeline_mode=pl.Buffered(1)),
+        ]
+        + [
+            pl.BlockSpec((n, half, 128), whole, pipeline_mode=pl.Buffered(1)) for half in halves
         ],
         out_specs=[
             pl.BlockSpec((1, TOK, D), one_image),
             pl.BlockSpec((1, TOK, D), one_image),
-            pl.BlockSpec((n, rows, 128), whole, pipeline_mode=pl.Buffered(1)),
+        ]
+        + [
+            pl.BlockSpec((n, half, 128), whole, pipeline_mode=pl.Buffered(1)) for half in halves
         ],
         out_shape=[
             jax.ShapeDtypeStruct((count, TOK, D), f32),
             jax.ShapeDtypeStruct((count, TOK, D), f32),
-            jax.ShapeDtypeStruct((n, rows, 128), bf16),
-        ],
+        ]
+        + [jax.ShapeDtypeStruct((n, half, 128), f32) for half in halves],
         scratch_shapes=[
             pltpu.VMEM((flat_rows, 128), f32),
             pltpu.VMEM((2, gflat_rows, 128), f32),
@@ -410,7 +706,7 @@
             dimension_semantics=("arbitrary",), vmem_limit_bytes=56 * 1024 * 1024
         ),
         name="block",
-    )(drops, images, cotangent, blocks)
+    )(drops, images, cotangent, first, second)
 
 
 def adam_step(master, gradient, first, second, step):
@@ -446,23 +742,14 @@
     goff = lax.rem(dp * gshare, UNIT)
     sblock = lax.dynamic_update_slice(jnp.zeros((srows * 128,), f32), shared_master, (soff,))
     gblock = lax.dynamic_update_slice(jnp.zeros((grows * 128,), f32), group_master[0], (goff,))
-    block = jnp.concatenate(
-        [sblock.reshape(srows, 128), gblock.reshape(grows, 128)], axis=0
-    ).astype(bf16)
-    blocks = lax.all_gather(block, ("dp", "heads"), axis=0)
-    output, input_grad, gblocks = compute(
-        n_dp, srows, grows, drop_masks, images, cotangent, blocks
+    own = jnp.concatenate([sblock.reshape(srows, 128), gblock.reshape(grows, 128)], axis=0)
+    first, second = gather(n_dp, srows + grows, own)
+    output, input_grad, first, second = compute(
+        n_dp, srows, grows, drop_masks, images, cotangent, first, second
     )
-    mine = lax.psum_scatter(gblocks, ("dp", "heads"), scatter_dimension=0).astype(f32)
-    shared_share = lax.dynamic_slice(mine[:srows].reshape(-1), (soff,), (sshare,))
-    group_share = lax.dynamic_slice(mine[srows:].reshape(-1), (goff,), (gshare,))
-    group_share = group_share[None, :]
-    squares = jnp.sum(group_share * group_share) + jnp.sum(shared_share * shared_share)
-    grad_norm = jnp.sqrt(lax.psum(squares, ("dp", "heads")))
-    threshold = math.sqrt(2 * GROUP_PARAMS + SHARED_PARAMS)
-    factor = jnp.minimum(1.0, threshold / (grad_norm + 1e-06))
-    group_grad = group_share * factor
-    shared_grad = shared_share * factor
+    mine, norm = reduce(n_dp, srows, first, second)
+    shared_grad = lax.dynamic_slice(mine[:srows].reshape(-1), (soff,), (sshare,))
+    group_grad = lax.dynamic_slice(mine[srows:].reshape(-1), (goff,), (gshare,))[None, :]
     step = jnp.float32(STEP)
     group_new, group_first, group_second = adam_step(
         group_master, group_grad, group_m1, group_m2, step
@@ -473,7 +760,7 @@
     return (
         output,
         input_grad,
-        grad_norm.reshape(1),
+        norm[0, 0:1],
         group_grad,
         group_new,
         group_first,

time: 321 us -> 140 us (0.44)
  waiting for transfers between devices: 188 us -> 0 us
  Pallas kernels: 60.7 us -> 121 us
  blocking collectives: 36.8 us -> 0 us
  between operations: 17.4 us -> 0.79 us
    reduce_scatter x1 -> x0, waiting for transfers between devices: 133 us -> none  [on_device(): lax.psum_scatter(gblocks, ('dp', 'heads'), scatter_dimension=0).astype(f32)]
    pallas_call x1 -> x3, Pallas kernels: 60.7 us -> 121 us  [the longest x1 61.3 us: compute(): pl.pallas_call(partial(compute_kernel, n_dp, srows, grows, exchange_order...]
    all_gather x1 -> x0, waiting for transfers between devices: 55.1 us -> none  [on_device(): blocks = lax.all_gather(block, ('dp', 'heads'), axis=0)]
    psum x1 -> x0, blocking collectives: 36.8 us -> none  [on_device(): grad_norm = jnp.sqrt(lax.psum(squares, ('dp', 'heads')))]
    unnamed x23 -> x21, local copies, waits for them, and re-layouts: 9.31 us -> 9.43 us
  transfers between devices with their start and end apart: 2 -> 0, of which waited for: 2 -> 0; matrix products, arithmetic and copies ran while one was open for 2% -> 0% of each run, Pallas kernels for 0% -> 0%
where the time goes in v2:
time: 140 us; the launch traced here: 139 us
  Pallas kernels  121 us (86%)
  local copies, waits for them, and re-layouts  14.7 us (10%)
  other arithmetic  3.25 us (2%)
    pallas_call x1, Pallas kernels, compute(): pl.pallas_call(partial(compute_kernel, n_dp, srows, grows, exchange_order...  61.3 us
    pallas_call x1, Pallas kernels, reduce(): pl.pallas_call(partial(reduce_kernel, n_dp, srows, orders, halves), in_sp...  33.6 us
    pallas_call x1, Pallas kernels, gather(): pl.pallas_call(partial(gather_kernel, orders, halves), in_specs=[pl.Block...  25.8 us
    unnamed x21, local copies, waits for them, and re-layouts  9.43 us

profile of v2, /device:TPU:0, one launch (start us, length us, event | category | flops | bytes accessed | tf_op | source)
XLA Modules:
  0.0 139.5 jit_solution(6592692408938188473)
XLA Ops:
  0.6 0.0 copy-start.1
  0.7 1.4 %copy.22.drop_ref = s32[8,2]{1,0:T(8,128)} copy(s32[8,2]{0,1:T(2,128)} %param.11) | data formatting | bytes 128 | tf_op args[2]
  2.1 0.8 reduce.1
  2.9 0.5 dynamic_update_slice.7
  3.5 1.3 dynamic_update_slice.6
  4.8 0.6 pad_maximum_fusion.own_ref
  5.4 2.2 %copy.23.x_ref = bf16[8,196,256]{2,1,0:T(8,128)(2,1)} copy(bf16[8,196,256]{2,0,1:T(8,128)(2,1)} %param.9) | data formatting | bytes 1605632 | tf_op args[0]
  7.6 0.0 copy-done.1
  7.6 1.0 copy.24.co_ref
  8.7 25.8 %gather.1 = (bf16[32,112,128]{2,1,0:T(8,128)(2,1)}, bf16[32,112,128]{2,1,0:T(8,128)(2,1)}) custom-call(f32[224,128]{1,0:T(8,128)} %pad_maximum_fusion.own_ref), custom_call_target="tpu_custom_call" | custom-call | tf_op jit(solution)/shard_map/gather/pallas_call | solution.py:125
  34.4 61.3 %block.1 = (f32[8,196,256]{2,1,0:T(8,128)}, f32[8,196,256]{2,1,0:T(8,128)}, f32[32,112,128]{2,1,0:T(8,128)}, f32[32,112,128]{2,1,0:T(8,128)}) custom-call(s32[8,2]{1,0:T(8,128)} %copy.22.drop_ref, bf16[8,196,256]{2,1,0:T(8,128)(2,1)} %copy.23.x_ref, bf16[8,196,256]{2,1,0:T(8,128)(2,1)} %copy.24.co_ref, bf16[32,112,128]{2,1,0:T(8,128)(2,1)} %get-tuple-element.21.first_ref, ...), custom_call_target="tpu_custom_call" | custom-call | tf_op jit(solution)/shard_map/block/pallas_call | solution.py:658
  95.8 3.1 %copy.25 = f32[8,196,256]{2,0,1:T(8,128)} copy(f32[8,196,256]{2,1,0:T(8,128)} %get-tuple-element.29) | data formatting | bytes 3211264
  98.9 0.0 copy-start.3
  98.9 0.0 copy-start.6
  98.9 0.0 copy-start.7
  98.9 0.0 copy-start.2
  98.9 0.0 copy-start.4
  98.9 0.0 copy-start.5
  98.9 0.0 copy-start
  98.9 33.6 %reduce.2 = (f32[224,128]{1,0:T(8,128)}, f32[8,128]{1,0:T(8,128)}) custom-call(f32[32,112,128]{2,1,0:T(8,128)} %get-tuple-element.25.first_ref, f32[32,112,128]{2,1,0:T(8,128)} %get-tuple-element.26.second_ref), custom_call_target="tpu_custom_call" | custom-call | tf_op jit(solution)/shard_map/reduce/pallas_call | solution.py:287
  132.5 1.2 slice.9
  133.7 0.8 slice_bitcast_fusion.1
  134.5 0.9 slice_bitcast_fusion
  135.4 0.1 multiply_multiply_fusion.1
  135.5 0.6 broadcast_in_dim.11
  136.1 0.0 copy-done.3
  136.1 0.0 copy-done.6
  136.1 0.0 copy-done.7
  136.1 0.9 fusion.3
  137.0 0.0 copy-done.2
  137.0 0.0 copy-done.4
  137.0 0.0 copy-done.5
  137.0 0.8 fusion.1
  137.8 0.0 copy-done
  137.8 1.6 %copy.26 = f32[8,196,256]{2,0,1:T(8,128)} copy(f32[8,196,256]{2,1,0:T(8,128)S(1)} %copy-done) | data formatting | bytes 3211264
  (3 shorter events, 0.0 us)
Async XLA Ops:
  0.6 7.0 %copy-start.1 = (bf16[8,196,256]{2,0,1:T(8,128)(2,1)S(1)}, bf16[8,196,256]{2,0,1:T(8,128)(2,1)}, u32[]{:S(2)}) copy-start(bf16[8,196,256]{2,0,1:T(8,128)(2,1)} %param.10) | copy-start | bytes 2408452
  98.9 37.2 %copy-start.3 = (f32[1,8288]{1,0:T(1,128)S(1)}, f32[1,8288]{1,0:T(1,128)}, u32[]{:S(2)}) copy-start(f32[1,8288]{1,0:T(1,128)} %param.12) | copy-start | bytes 99460
  98.9 37.2 %copy-start.6 = (f32[1,8288]{1,0:T(1,128)S(1)}, f32[1,8288]{1,0:T(1,128)}, u32[]{:S(2)}) copy-start(f32[1,8288]{1,0:T(1,128)} %param.14) | copy-start | bytes 99460
  98.9 37.2 %copy-start.7 = (f32[1,8288]{1,0:T(1,128)S(1)}, f32[1,8288]{1,0:T(1,128)}, u32[]{:S(2)}) copy-start(f32[1,8288]{1,0:T(1,128)} %param.13) | copy-start | bytes 99460
  98.9 38.1 %copy-start.2 = (f32[16464]{0:T(1024)S(1)}, f32[16464]{0:T(1024)}, u32[]{:S(2)}) copy-start(f32[16464]{0:T(1024)} %param.15) | copy-start | bytes 197572
  98.9 38.1 %copy-start.4 = (f32[16464]{0:T(1024)S(1)}, f32[16464]{0:T(1024)}, u32[]{:S(2)}) copy-start(f32[16464]{0:T(1024)} %param.17) | copy-start | bytes 197572
  98.9 38.1 %copy-start.5 = (f32[16464]{0:T(1024)S(1)}, f32[16464]{0:T(1024)}, u32[]{:S(2)}) copy-start(f32[16464]{0:T(1024)} %param.16) | copy-start | bytes 197572
  98.9 38.9 %copy-start = (f32[8,196,256]{2,1,0:T(8,128)S(1)}, f32[8,196,256]{2,1,0:T(8,128)}, u32[]{:S(2)}) copy-start(f32[8,196,256]{2,1,0:T(8,128)} %get-tuple-element.30) | copy-start | bytes 4816900

commit v3 on v2

--- a/solution.py
+++ b/solution.py
@@ -384,22 +384,333 @@
 
 
 def tile_sum(values):
-    return jnp.sum(values.reshape(-1, 8, HALF), axis=0)
-
-
-def place_matrices(pp_ref, ppt_ref):
-    place = lax.broadcasted_iota(jnp.int32, (GRID, TOK), 0)
-    token = lax.broadcasted_iota(jnp.int32, (GRID, TOK), 1)
-    first, second = place // 16, place % 16
-    inside = second < SIDE
-    pp_ref[0] = (inside & (token == first * SIDE + second)).astype(f32).astype(bf16)
-    pp_ref[1] = (inside & (token == second * SIDE + first)).astype(f32).astype(bf16)
-    place = lax.broadcasted_iota(jnp.int32, (TOK, GRID), 1)
-    token = lax.broadcasted_iota(jnp.int32, (TOK, GRID), 0)
-    first, second = place // 16, place % 16
-    inside = second < SIDE
-    ppt_ref[0] = (inside & (token == first * SIDE + second)).astype(f32).astype(bf16)
-    ppt_ref[1] = (inside & (token == second * SIDE + first)).astype(f32).astype(bf16)
+    return jnp.sum(values.reshape(-1, 8, values.shape[1]), axis=0)
+
+
+def turn_matrix():
+    to = lax.broadcasted_iota(jnp.int32, (GRID, GRID), 0)
+    src = lax.broadcasted_iota(jnp.int32, (GRID, GRID), 1)
+    first, second = to // 16, to % 16
+    return ((second < SIDE) & (src == second * 16 + first)).astype(f32).astype(bf16)
+
+
+def row_mask():
+    row = lax.broadcasted_iota(jnp.int32, (GRID, 1), 0)
+    return (row % 16 < SIDE).astype(f32)
+
+
+def to_grid(source, tokens, grid_ref):
+    images = grid_ref.shape[0]
+    grid_ref[...] = jnp.zeros_like(grid_ref)
+    for half in range(2):
+        cols = slice(half * 128, (half + 1) * 128)
+        tokens[half] = source[:, cols].astype(f32)
+        for image in range(images):
+            for r in range(SIDE):
+                grid_ref[image, 16 * r : 16 * r + SIDE, cols] = tokens[
+                    half, pl.ds(r * SIDE * images + image, SIDE, stride=images), :
+                ]
+
+
+def from_grid(value, tokens, image, images):
+    for half in range(2):
+        for r in range(SIDE):
+            tokens[half, pl.ds(r * SIDE * images + image, SIDE, stride=images), :] = value[
+                16 * r : 16 * r + SIDE, half * 128 : (half + 1) * 128
+            ]
+
+
+def prepare_weights(n_dp, srows, grows, orders, halves, weights, sc):
+    n = 2 * n_dp
+    flat, gflat = sc["flat"], sc["gflat"]
+    flat[...] = jnp.zeros_like(flat)
+    gflat[...] = jnp.zeros_like(gflat)
+    for k in range(n):
+        at = first_row(SHARED_PARAMS, n, k)
+        for h, low, high, begin, end in window_parts(halves, (0, srows)):
+            window = weights[h][place_of(orders[h], k), low:high]
+            flat[at + begin : at + end] += window.astype(f32)
+        at = first_row(GROUP_PARAMS, n_dp, k // 2)
+        for h, low, high, begin, end in window_parts(halves, (srows, srows + grows)):
+            window = weights[h][place_of(orders[h], k), low:high]
+            gflat[k % 2, at + begin : at + end] += window.astype(f32)
+    for c in range(8):
+        cols = slice(c * 128, (c + 1) * 128)
+        sc["uw"][:, cols] = flat[pl.ds(c, D, stride=8), :].astype(bf16)
+        sc["ubias"][:, cols] = flat[2048 + c : 2049 + c, :]
+    for c in range(2):
+        cols = slice(c * 128, (c + 1) * 128)
+        sc["dw"][:, cols] = flat[pl.ds(2056 + c, FF, stride=2), :].astype(bf16)
+        for i in range(6):
+            sc["vecs"][i : i + 1, cols] = flat[4104 + 2 * i + c : 4105 + 2 * i + c, :]
+    for j in range(2):
+        for c in range(3):
+            cols = slice(j * 384 + c * 128, j * 384 + (c + 1) * 128)
+            sc["wq"][:, cols] = gflat[j, pl.ds(c, D, stride=3), :].astype(bf16)
+        for c in range(2):
+            cols = slice(c * 128, (c + 1) * 128)
+            sc["ow"][j * 128 : (j + 1) * 128, cols] = gflat[
+                j, pl.ds(770 + c, HALF, stride=2), :
+            ].astype(bf16)
+        sc["qbias"][:, j * 384 : j * 384 + 128] = gflat[j, 768:769, :]
+        sc["qbias"][:, j * 384 + 128 : j * 384 + 256] = jnp.zeros((1, 128), f32)
+        sc["qbias"][:, j * 384 + 256 : j * 384 + 384] = gflat[j, 769:770, :]
+        sc["conv"][j, 0:10] = gflat[j, 1026:1036, :]
+
+
+def place_gradients(n_dp, srows, grows, orders, halves, gradients, sc):
+    n = 2 * n_dp
+    flat, gflat = sc["flat"], sc["gflat"]
+    for c in range(8):
+        cols = slice(c * 128, (c + 1) * 128)
+        flat[pl.ds(c, D, stride=8), :] = sc["a_uw"][:, cols]
+        flat[2048 + c : 2049 + c, :] = sc["a_ub"][0:1, cols]
+    for q in range(4):
+        turned = sc["a_dwt"][:, q * 256 : (q + 1) * 256].T
+        for c in range(2):
+            flat[pl.ds(2056 + 512 * q + c, 256, stride=2), :] = turned[
+                :, c * 128 : (c + 1) * 128
+            ]
+    for c in range(2):
+        cols = slice(c * 128, (c + 1) * 128)
+        for i in range(6):
+            flat[4104 + 2 * i + c : 4105 + 2 * i + c, :] = column_sum(
+                sc["a_vec"][i, :, cols]
+            )
+    for j in range(2):
+        for c in range(3):
+            cols = slice(j * 384 + c * 128, j * 384 + (c + 1) * 128)
+            gflat[j, pl.ds(c, D, stride=3), :] = sc["a_wq"][:, cols]
+        for c in range(2):
+            cols = slice(c * 128, (c + 1) * 128)
+            gflat[j, pl.ds(770 + c, HALF, stride=2), :] = sc["a_ow"][
+                j * 128 : (j + 1) * 128, cols
+            ]
+        gflat[j, 768:769, :] = sc["a_pb"][0:1, j * 384 : j * 384 + 128]
+        gflat[j, 769:770, :] = sc["a_pb"][0:1, j * 384 + 256 : j * 384 + 384]
+        for i in range(10):
+            gflat[j, 1026 + i : 1027 + i, :] = column_sum(sc["a_conv"][j, i])
+    for k in range(n):
+        at = first_row(SHARED_PARAMS, n, k)
+        for h, low, high, begin, end in window_parts(halves, (0, srows)):
+            gradients[h][place_of(orders[h], k), low:high] = flat[at + begin : at + end]
+        at = first_row(GROUP_PARAMS, n_dp, k // 2)
+        for h, low, high, begin, end in window_parts(halves, (srows, srows + grows)):
+            gradients[h][place_of(orders[h], k), low:high] = gflat[
+                k % 2, at + begin : at + end
+            ]
+
+
+def attention_forward(images, sc):
+    scale = HD ** (-0.5)
+    masks = head_masks(bf16)
+    inside = row_mask()
+    key_row = lax.broadcasted_iota(jnp.int32, (1, SW, 16, STRIPE), 2)
+    gain_one, shift_one = sc["vecs"][1:2], sc["vecs"][2:3]
+    qkv_ref, conv = sc["qkv"], sc["conv"]
+    for image in images:
+        unit, inverse = norm_parts(sc["x"][image])
+        sc["unit"][image] = unit
+        sc["inverse"][image] = inverse
+        sc["normed"][image] = (unit * gain_one + shift_one).astype(bf16)
+    for image in images:
+        triple = (nn(sc["normed"][image], sc["wq"][...]) + sc["qbias"][...]) * inside
+        triple = triple.astype(bf16)
+        qkv_ref[image, 0] = triple[:, :384]
+        qkv_ref[image, 1] = nn(sc["turn"][...], triple[:, 384:]).astype(bf16)
+    for j in range(2):
+        padded = [[] for _ in images]
+        for s in range(2):
+            for image, parts in zip(images, padded):
+                rows = slice(s * STRIPE, (s + 1) * STRIPE)
+                query = qkv_ref[image, j, rows, 0:128]
+                keys = spread_heads(qkv_ref[image, j, rows, 128:256], masks)
+                value = qkv_ref[image, j, rows, 256:384]
+                scores = nt(keys, query).reshape(HEADS, SW, 16, STRIPE) * scale
+                scores = jnp.where(key_row < SIDE, scores, -1e30)
+                scores = scores.reshape(HEADS, STRIPE, STRIPE)
+                weights = jnp.exp(scores - jnp.max(scores, axis=1, keepdims=True))
+                probs = weights * (1.0 / jnp.sum(weights, axis=1, keepdims=True))
+                probs = probs.reshape(HEADS * STRIPE, STRIPE)
+                sc["probs"][image, 2 * j + s] = probs
+                attended = tn(probs.astype(bf16), spread_heads(value, masks))
+                near = neighbours(value.astype(f32))
+                total = attended + conv[j, 9:10]
+                for a in range(3):
+                    part = near[0] * conv[j, 3 * a : 3 * a + 1]
+                    for b in range(1, 3):
+                        part = part + near[b] * conv[j, 3 * a + b : 3 * a + b + 1]
+                    total = total + row_shift(part, a - 1)
+                parts.append(total.astype(bf16))
+        for image, parts in zip(images, padded):
+            both = jnp.concatenate(parts, axis=0)
+            if j == 1:
+                both = nn(sc["turn"][...], both).astype(bf16)
+            sc["heads"][image, :, j * 128 : (j + 1) * 128] = both
+
+
+def mlp_both(images, count, drop_ref, sc):
+    down_bias = sc["vecs"][0:1]
+    gain_two, shift_two, out_bias = sc["vecs"][3:4], sc["vecs"][4:5], sc["vecs"][5:6]
+    ones = jnp.ones((8, GRID), bf16)
+    a_vec = sc["a_vec"]
+    uw, dw, ubias = sc["uw"], sc["dw"], sc["ubias"]
+    state = []
+    for image in images:
+        scale_one = drop_ref[0, image].astype(f32) / keep_prob
+        scale_two = drop_ref[1, image].astype(f32) / keep_prob
+        branch = nn(sc["heads"][image], sc["ow"][...])
+        middle = sc["x"][image] + scale_one * (branch + out_bias)
+        unit_two, inverse_two = norm_parts(middle)
+        normed_two = (unit_two * gain_two + shift_two).astype(bf16)
+        grad_output = sc["co"][image]
+        grad_mlp_f = scale_two * grad_output
+        a_vec[0] += tile_sum(grad_mlp_f)
+        grad_mlp = grad_mlp_f.astype(bf16)
+        state.append(
+            (scale_one, scale_two, middle, unit_two, inverse_two, normed_two, grad_output, grad_mlp)
+        )
+    mlps = [None] * len(images)
+    grads = [None] * len(images)
+    for c in range(4):
+        cols = slice(c * 256, (c + 1) * 256)
+        for i in range(len(images)):
+            normed_two, grad_mlp = state[i][5], state[i][7]
+            hidden = nn(normed_two, uw[:, cols]) + ubias[:, cols]
+            density = jnp.exp(hidden * hidden * -0.5) * (1.0 / math.sqrt(2.0 * math.pi))
+            phi = 0.5 + 0.5 * lax.erf(hidden * math.sqrt(0.5))
+            active = (hidden * phi).astype(bf16)
+            part = nn(active, dw[cols, :])
+            mlps[i] = part if mlps[i] is None else mlps[i] + part
+            sc["a_dwt"][:, cols] += tn(grad_mlp, active)
+            grad_active = nt(grad_mlp, dw[cols, :])
+            grad_hidden = (grad_active * (phi + hidden * density)).astype(bf16)
+            sc["a_ub"][:, cols] += nn(ones, grad_hidden)
+            sc["a_uw"][:, cols] += tn(normed_two, grad_hidden)
+            part = nt(grad_hidden, uw[:, cols])
+            grads[i] = part if grads[i] is None else grads[i] + part
+    for i, image in enumerate(images):
+        scale_one, scale_two, middle, unit_two, inverse_two, _, grad_output, _ = state[i]
+        from_grid(middle + scale_two * (mlps[i] + down_bias), sc["tokens"], image, count)
+        a_vec[3] += tile_sum(grads[i] * unit_two)
+        a_vec[4] += tile_sum(grads[i])
+        grad_middle = grad_output + norm_back(grads[i], unit_two, inverse_two, gain_two)
+        sc["gmid"][image] = grad_middle
+        grad_branch_f = scale_one * grad_middle
+        a_vec[5] += tile_sum(grad_branch_f)
+        grad_branch = grad_branch_f.astype(bf16)
+        sc["a_ow"][...] += tn(sc["heads"][image], grad_branch)
+        sc["gheads"][image] = nt(grad_branch, sc["ow"][...]).astype(bf16)
+
+
+def attention_back(images, count, sc):
+    scale = HD ** (-0.5)
+    masks = head_masks(bf16)
+    inside = row_mask()[:STRIPE]
+    gain_one = sc["vecs"][1:2]
+    ones = jnp.ones((8, GRID), bf16)
+    a_vec, a_conv = sc["a_vec"], sc["a_conv"]
+    qkv_ref, conv = sc["qkv"], sc["conv"]
+    for j in range(2):
+        if j == 0:
+            grads = [sc["gheads"][image, :, 0:128] for image in images]
+        else:
+            grads = [
+                nn(sc["turn"][...], sc["gheads"][image, :, 128:256]).astype(bf16)
+                for image in images
+            ]
+        padded = [[] for _ in images]
+        for s in range(2):
+            for image, parts, all_grad in zip(images, padded, grads):
+                rows = slice(s * STRIPE, (s + 1) * STRIPE)
+                query = qkv_ref[image, j, rows, 0:128]
+                keys = spread_heads(qkv_ref[image, j, rows, 128:256], masks)
+                value = qkv_ref[image, j, rows, 256:384]
+                grad = all_grad[rows]
+                grad_f = grad.astype(f32)
+                probs = sc["probs"][image, 2 * j + s]
+                grad_probs = nt(spread_heads(value, masks), grad)
+                product = (probs * grad_probs).reshape(HEADS, STRIPE, STRIPE)
+                inner = jnp.sum(product, axis=1, keepdims=True)
+                grad_scores = product - probs.reshape(HEADS, STRIPE, STRIPE) * inner
+                grad_scores = grad_scores.reshape(HEADS * STRIPE, STRIPE).astype(bf16)
+                grad_query = tn(grad_scores, keys) * scale
+                grad_key = pick_heads(nn(grad_scores, query)) * scale
+                grad_value = pick_heads(nn(probs.astype(bf16), grad))
+                near = neighbours(grad_f)
+                for a in range(3):
+                    part = near[2] * conv[j, 3 * a : 3 * a + 1]
+                    for b in range(1, 3):
+                        part = part + near[2 - b] * conv[j, 3 * a + b : 3 * a + b + 1]
+                    grad_value = grad_value + row_shift(part, 1 - a)
+                grad_value = grad_value * inside
+                near = neighbours(value.astype(f32))
+                for b in range(3):
+                    a_conv[j, b] += tile_sum(grad_f[16:] * near[b][:-16])
+                    a_conv[j, 3 + b] += tile_sum(grad_f * near[b])
+                    a_conv[j, 6 + b] += tile_sum(grad_f[:-16] * near[b][16:])
+                a_conv[j, 9] += tile_sum(grad_f)
+                parts.append(
+                    jnp.concatenate([grad_query, grad_key, grad_value], axis=1).astype(bf16)
+                )
+        for image, parts in zip(images, padded):
+            both = jnp.concatenate(parts, axis=0)
+            if j == 1:
+                both = nn(sc["turn"][...], both).astype(bf16)
+            sc["gtriple"][image, :, j * 384 : (j + 1) * 384] = both
+    for image in images:
+        grad_triple = sc["gtriple"][image]
+        sc["a_pb"][...] += nn(ones, grad_triple)
+        sc["a_wq"][...] += tn(sc["normed"][image], grad_triple)
+        grad_normed = nt(grad_triple, sc["wq"][...])
+        unit, inverse = sc["unit"][image], sc["inverse"][image]
+        a_vec[1] += tile_sum(grad_normed * unit)
+        a_vec[2] += tile_sum(grad_normed)
+        grad = sc["gmid"][image] + norm_back(grad_normed, unit, inverse, gain_one)
+        from_grid(grad, sc["tokens"], image, count)
+
+
+def scratch_shapes(n_dp, srows, grows, count):
+    n = 2 * n_dp
+    flat_rows = max(4120, first_row(SHARED_PARAMS, n, n - 1) + srows)
+    gflat_rows = max(1040, first_row(GROUP_PARAMS, n_dp, n_dp - 1) + grows)
+    return dict(
+        flat=((flat_rows, 128), f32),
+        gflat=((2, gflat_rows, 128), f32),
+        turn=((GRID, GRID), bf16),
+        wq=((D, 768), bf16),
+        ow=((D, D), bf16),
+        uw=((D, FF), bf16),
+        dw=((FF, D), bf16),
+        qbias=((1, 768), f32),
+        ubias=((1, FF), f32),
+        vecs=((8, D), f32),
+        conv=((2, 16, 128), f32),
+        a_wq=((D, 768), f32),
+        a_ow=((D, D), f32),
+        a_uw=((D, FF), f32),
+        a_dwt=((D, FF), f32),
+        a_pb=((8, 768), f32),
+        a_ub=((8, FF), f32),
+        a_vec=((6, 8, D), f32),
+        a_conv=((2, 10, 8, 128), f32),
+        tokens=((2, TOK * count, 128), f32),
+        x=((count, GRID, D), f32),
+        co=((count, GRID, D), f32),
+        unit=((count, GRID, D), f32),
+        inverse=((count, GRID, 1), f32),
+        normed=((count, GRID, D), bf16),
+        qkv=((count, 2, GRID, 384), bf16),
+        probs=((count, 4, HEADS * STRIPE, STRIPE), f32),
+        heads=((count, GRID, D), bf16),
+        gmid=((count, GRID, D), f32),
+        gheads=((count, GRID, D), bf16),
+        gtriple=((count, GRID, 768), bf16),
+    )
+
+
+ACCUMULATORS = ("a_wq", "a_ow", "a_uw", "a_dwt", "a_pb", "a_ub", "a_vec", "a_conv")
+TOGETHER = 2
 
 
 def compute_kernel(
@@ -408,6 +719,8 @@
     grows,
     orders,
     halves,
+    count,
+    names,
     drop_ref,
     x_ref,
     co_ref,
@@ -417,296 +730,66 @@
     gin_ref,
     gfirst_ref,
     gsecond_ref,
-    flat,
-    gflat,
-    pp_ref,
-    ppt_ref,
-    wq,
-    ow,
-    uw,
-    dw,
-    qbias,
-    ubias,
-    vecs,
-    conv,
-    a_wq,
-    a_ow,
-    a_uw,
-    a_dwt,
-    a_pb,
-    a_ub,
-    a_vec,
-    a_conv,
-    p_ref,
-    qkv_ref,
+    *scratch,
 ):
-    image = pl.program_id(0)
-    n = 2 * n_dp
-    weights, gradients = (first_ref, second_ref), (gfirst_ref, gsecond_ref)
-    shared_parts = window_parts(halves, (0, srows))
-    group_parts = window_parts(halves, (srows, srows + grows))
-
-    @pl.when(image == 0)
-    def _():
-        place_matrices(pp_ref, ppt_ref)
-        flat[...] = jnp.zeros_like(flat)
-        gflat[...] = jnp.zeros_like(gflat)
-        for k in range(n):
-            at = first_row(SHARED_PARAMS, n, k)
-            for h, low, high, begin, end in shared_parts:
-                window = weights[h][place_of(orders[h], k), low:high]
-                flat[at + begin : at + end] += window.astype(f32)
-            at = first_row(GROUP_PARAMS, n_dp, k // 2)
-            for h, low, high, begin, end in group_parts:
-                window = weights[h][place_of(orders[h], k), low:high]
-                gflat[k % 2, at + begin : at + end] += window.astype(f32)
-        for c in range(8):
-            cols = slice(c * 128, (c + 1) * 128)
-            uw[:, cols] = flat[pl.ds(c, D, stride=8), :].astype(bf16)
-            ubias[:, cols] = flat[2048 + c : 2049 + c, :]
-        for c in range(2):
-            cols = slice(c * 128, (c + 1) * 128)
-            dw[:, cols] = flat[pl.ds(2056 + c, FF, stride=2), :].astype(bf16)
-            for i in range(6):
-                vecs[i : i + 1, cols] = flat[4104 + 2 * i + c : 4105 + 2 * i + c, :]
-        for j in range(2):
-            for c in range(3):
-                cols = slice(j * 384 + c * 128, j * 384 + (c + 1) * 128)
-                wq[:, cols] = gflat[j, pl.ds(c, D, stride=3), :].astype(bf16)
-            for c in range(2):
-                cols = slice(c * 128, (c + 1) * 128)
-                ow[j * 128 : (j + 1) * 128, cols] = gflat[
-                    j, pl.ds(770 + c, HALF, stride=2), :
-                ].astype(bf16)
-            qbias[:, j * 384 : j * 384 + 128] = gflat[j, 768:769, :]
-            qbias[:, j * 384 + 128 : j * 384 + 256] = jnp.zeros((1, 128), f32)
-            qbias[:, j * 384 + 256 : j * 384 + 384] = gflat[j, 769:770, :]
-            conv[j, 0:10] = gflat[j, 1026:1036, :]
-        for ref in (a_wq, a_ow, a_uw, a_dwt, a_pb, a_ub, a_vec, a_conv):
-            ref[...] = jnp.zeros_like(ref)
-
-    scale_one = drop_ref[image, 0].astype(f32) / keep_prob
-    scale_two = drop_ref[image, 1].astype(f32) / keep_prob
-    down_bias, gain_one, shift_one = vecs[0:1], vecs[1:2], vecs[2:3]
-    gain_two, shift_two, out_bias = vecs[3:4], vecs[4:5], vecs[5:6]
-    masks = head_masks(bf16)
-    ones = jnp.ones((8, TOK), bf16)
-    key_row = lax.broadcasted_iota(jnp.int32, (1, SW, 16, STRIPE), 2)
-    scale = HD ** (-0.5)
-
-    values = x_ref[0].astype(f32)
-    unit_one, inverse_one = norm_parts(values)
-    normed = (unit_one * gain_one + shift_one).astype(bf16)
-    triple = (nn(normed, wq[...]) + qbias[...]).astype(bf16)
-    heads_out = []
-    for j in range(2):
-        qkv_ref[j] = nn(pp_ref[j], triple[:, j * 384 : (j + 1) * 384]).astype(bf16)
-        parts = []
-        for s in range(2):
-            rows = slice(s * STRIPE, (s + 1) * STRIPE)
-            query = qkv_ref[j, rows, 0:128]
-            keys = spread_heads(qkv_ref[j, rows, 128:256], masks)
-            value = qkv_ref[j, rows, 256:384]
-            scores = nt(keys, query).reshape(HEADS, SW, 16, STRIPE) * scale
-            scores = jnp.where(key_row < SIDE, scores, -1e30)
-            scores = scores.reshape(HEADS, STRIPE, STRIPE)
-            weights = jnp.exp(scores - jnp.max(scores, axis=1, keepdims=True))
-            probs = weights * (1.0 / jnp.sum(weights, axis=1, keepdims=True))
-            probs = probs.reshape(HEADS * STRIPE, STRIPE)
-            p_ref[2 * j + s] = probs
-            attended = tn(probs.astype(bf16), spread_heads(value, masks))
-            near = neighbours(value.astype(f32))
-            total = attended + conv[j, 9:10]
-            for a in range(3):
-                part = near[0] * conv[j, 3 * a : 3 * a + 1]
-                for b in range(1, 3):
-                    part = part + near[b] * conv[j, 3 * a + b : 3 * a + b + 1]
-                total = total + row_shift(part, a - 1)
-            parts.append(total.astype(bf16))
-        padded = jnp.concatenate(parts, axis=0)
-        heads_out.append(nn(ppt_ref[j], padded).astype(bf16))
-    heads_out = jnp.concatenate(heads_out, axis=1)
-    branch = nn(heads_out, ow[...])
-    middle = values + scale_one * (branch + out_bias)
-    unit_two, inverse_two = norm_parts(middle)
-    normed_two = (unit_two * gain_two + shift_two).astype(bf16)
-    grad_output = co_ref[0].astype(f32)
-    grad_mlp_f = scale_two * grad_output
-    a_vec[0:1] += column_sum(grad_mlp_f)
-    grad_mlp = grad_mlp_f.astype(bf16)
-    mlp = None
-    grad_normed_two = None
-    for c in range(4):
-        cols = slice(c * 256, (c + 1) * 256)
-        hidden = nn(normed_two, uw[:, cols]) + ubias[:, cols]
-        density = jnp.exp(hidden * hidden * -0.5) * (1.0 / math.sqrt(2.0 * math.pi))
-        phi = 0.5 + 0.5 * lax.erf(hidden * math.sqrt(0.5))
-        active = (hidden * phi).astype(bf16)
-        part = nn(active, dw[cols, :])
-        mlp = part if mlp is None else mlp + part
-        a_dwt[:, cols] += tn(grad_mlp, active)
-        grad_active = nt(grad_mlp, dw[cols, :])
-        grad_hidden = (grad_active * (phi + hidden * density)).astype(bf16)
-        a_ub[:, cols] += nn(ones, grad_hidden)
-        a_uw[:, cols] += tn(normed_two, grad_hidden)
-        part = nt(grad_hidden, uw[:, cols])
-        grad_normed_two = part if grad_normed_two is None else grad_normed_two + part
-    out_ref[0] = middle + scale_two * (mlp + down_bias)
-
-    a_vec[3:4] += column_sum(grad_normed_two * unit_two)
-    a_vec[4:5] += column_sum(grad_normed_two)
-    grad_middle = grad_output + norm_back(grad_normed_two, unit_two, inverse_two, gain_two)
-    grad_branch_f = scale_one * grad_middle
-    a_vec[5:6] += column_sum(grad_branch_f)
-    grad_branch = grad_branch_f.astype(bf16)
-    a_ow[...] += tn(heads_out, grad_branch)
-    grad_heads = nt(grad_branch, ow[...]).astype(bf16)
-    grad_triple = []
-    for j in range(2):
-        padded = nn(pp_ref[j], grad_heads[:, j * 128 : (j + 1) * 128])
-        parts = []
-        for s in range(2):
-            rows = slice(s * STRIPE, (s + 1) * STRIPE)
-            query = qkv_ref[j, rows, 0:128]
-            keys = spread_heads(qkv_ref[j, rows, 128:256], masks)
-            value = qkv_ref[j, rows, 256:384]
-            grad_f = padded[rows]
-            grad = grad_f.astype(bf16)
-            probs = p_ref[2 * j + s]
-            grad_probs = nt(spread_heads(value, masks), grad)
-            product = (probs * grad_probs).reshape(HEADS, STRIPE, STRIPE)
-            inner = jnp.sum(product, axis=1, keepdims=True)
-            probs_three = probs.reshape(HEADS, STRIPE, STRIPE)
-            grad_scores = product - probs_three * inner
-            grad_scores = grad_scores.reshape(HEADS * STRIPE, STRIPE).astype(bf16)
-            grad_query = tn(grad_scores, keys) * scale
-            grad_key = pick_heads(nn(grad_scores, query)) * scale
-            grad_value = pick_heads(nn(probs.astype(bf16), grad))
-            near = neighbours(grad_f)
-            for a in range(3):
-                part = near[2] * conv[j, 3 * a : 3 * a + 1]
-                for b in range(1, 3):
-                    part = part + near[2 - b] * conv[j, 3 * a + b : 3 * a + b + 1]
-                grad_value = grad_value + row_shift(part, 1 - a)
-            near = neighbours(value.astype(f32))
-            for b in range(3):
-                a_conv[j, b] += tile_sum(grad_f[16:] * near[b][:-16])
-                a_conv[j, 3 + b] += tile_sum(grad_f * near[b])
-                a_conv[j, 6 + b] += tile_sum(grad_f[:-16] * near[b][16:])
-            a_conv[j, 9] += tile_sum(grad_f)
-            parts.append(
-                jnp.concatenate([grad_query, grad_key, grad_value], axis=1).astype(bf16)
-            )
-        both = jnp.concatenate(parts, axis=0)
-        grad_triple.append(nn(ppt_ref[j], both).astype(bf16))
-    grad_triple = jnp.concatenate(grad_triple, axis=1)
-    a_pb[...] += nn(ones, grad_triple)
-    a_wq[...] += tn(normed, grad_triple)
-    grad_normed = nt(grad_triple, wq[...])
-    a_vec[1:2] += column_sum(grad_normed * unit_one)
-    a_vec[2:3] += column_sum(grad_normed)
-    gin_ref[0] = grad_middle + norm_back(grad_normed, unit_one, inverse_one, gain_one)
-
-    @pl.when(image == pl.num_programs(0) - 1)
-    def _():
-        for c in range(8):
-            cols = slice(c * 128, (c + 1) * 128)
-            flat[pl.ds(c, D, stride=8), :] = a_uw[:, cols]
-            flat[2048 + c : 2049 + c, :] = a_ub[0:1, cols]
-        for q in range(4):
-            turned = a_dwt[:, q * 256 : (q + 1) * 256].T
-            for c in range(2):
-                flat[pl.ds(2056 + 512 * q + c, 256, stride=2), :] = turned[
-                    :, c * 128 : (c + 1) * 128
-                ]
-        for c in range(2):
-            cols = slice(c * 128, (c + 1) * 128)
-            for i in range(6):
-                flat[4104 + 2 * i + c : 4105 + 2 * i + c, :] = a_vec[i : i + 1, cols]
-        for j in range(2):
-            for c in range(3):
-                cols = slice(j * 384 + c * 128, j * 384 + (c + 1) * 128)
-                gflat[j, pl.ds(c, D, stride=3), :] = a_wq[:, cols]
-            for c in range(2):
-                cols = slice(c * 128, (c + 1) * 128)
-                gflat[j, pl.ds(770 + c, HALF, stride=2), :] = a_ow[
-                    j * 128 : (j + 1) * 128, cols
-                ]
-            gflat[j, 768:769, :] = a_pb[0:1, j * 384 : j * 384 + 128]
-            gflat[j, 769:770, :] = a_pb[0:1, j * 384 + 256 : j * 384 + 384]
-            for i in range(10):
-                gflat[j, 1026 + i : 1027 + i, :] = column_sum(a_conv[j, i])
-        for k in range(n):
-            at = first_row(SHARED_PARAMS, n, k)
-            for h, low, high, begin, end in shared_parts:
-                gradients[h][place_of(orders[h], k), low:high] = flat[at + begin : at + end]
-            at = first_row(GROUP_PARAMS, n_dp, k // 2)
-            for h, low, high, begin, end in group_parts:
-                gradients[h][place_of(orders[h], k), low:high] = gflat[
-                    k % 2, at + begin : at + end
-                ]
+    sc = dict(zip(names, scratch))
+    sc["turn"][...] = turn_matrix()
+    to_grid(x_ref, sc["tokens"], sc["x"])
+    to_grid(co_ref, sc["tokens"], sc["co"])
+    for name in ACCUMULATORS:
+        sc[name][...] = jnp.zeros_like(sc[name])
+    prepare_weights(n_dp, srows, grows, orders, halves, (first_ref, second_ref), sc)
+
+    def run(phase):
+        def body(i, carry):
+            phase([i * TOGETHER + k for k in range(TOGETHER)])
+            return carry
+
+        lax.fori_loop(0, count // TOGETHER, body, 0)
+
+    run(lambda images: attention_forward(images, sc))
+    run(lambda images: mlp_both(images, count, drop_ref, sc))
+    for half in range(2):
+        out_ref[:, half * 128 : (half + 1) * 128] = sc["tokens"][half]
+    run(lambda images: attention_back(images, count, sc))
+    for half in range(2):
+        gin_ref[:, half * 128 : (half + 1) * 128] = sc["tokens"][half]
+    place_gradients(n_dp, srows, grows, orders, halves, (gfirst_ref, gsecond_ref), sc)
 
 
 def compute(n_dp, srows, grows, drops, images, cotangent, first, second):
     n = 2 * n_dp
     count = images.shape[0]
     halves = (first.shape[1], second.shape[1])
-    flat_rows = max(4120, first_row(SHARED_PARAMS, n, n - 1) + srows)
-    gflat_rows = max(1040, first_row(GROUP_PARAMS, n_dp, n_dp - 1) + grows)
-    one_image = lambda i: (i, 0, 0)
-    whole = lambda i: (0, 0, 0)
-    return pl.pallas_call(
-        partial(compute_kernel, n_dp, srows, grows, exchange_orders(n_dp), halves),
-        grid=(count,),
-        in_specs=[
-            pl.BlockSpec(memory_space=pltpu.SMEM),
-            pl.BlockSpec((1, TOK, D), one_image),
-            pl.BlockSpec((1, TOK, D), one_image),
-        ]
-        + [
-            pl.BlockSpec((n, half, 128), whole, pipeline_mode=pl.Buffered(1)) for half in halves
-        ],
-        out_specs=[
-            pl.BlockSpec((1, TOK, D), one_image),
-            pl.BlockSpec((1, TOK, D), one_image),
-        ]
-        + [
-            pl.BlockSpec((n, half, 128), whole, pipeline_mode=pl.Buffered(1)) for half in halves
-        ],
-        out_shape=[
-            jax.ShapeDtypeStruct((count, TOK, D), f32),
-            jax.ShapeDtypeStruct((count, TOK, D), f32),
-        ]
+    shapes = scratch_shapes(n_dp, srows, grows, count)
+    vmem = pl.BlockSpec(memory_space=pltpu.VMEM)
+
+    def rows(array):
+        return jnp.swapaxes(array, 0, 1).reshape(TOK * count, D)
+
+    def unrows(array):
+        return jnp.swapaxes(array.reshape(TOK, count, D), 0, 1)
+
+    out, gin, first, second = pl.pallas_call(
+        partial(
+            compute_kernel,
+            n_dp,
+            srows,
+            grows,
+            exchange_orders(n_dp),
+            halves,
+            count,
+            tuple(shapes),
+        ),
+        in_specs=[pl.BlockSpec(memory_space=pltpu.SMEM)] + [vmem] * 4,
+        out_specs=[vmem] * 4,
+        out_shape=[jax.ShapeDtypeStruct((TOK * count, D), f32)] * 2
         + [jax.ShapeDtypeStruct((n, half, 128), f32) for half in halves],
-        scratch_shapes=[
-            pltpu.VMEM((flat_rows, 128), f32),
-            pltpu.VMEM((2, gflat_rows, 128), f32),
-            pltpu.VMEM((2, GRID, TOK), bf16),
-            pltpu.VMEM((2, TOK, GRID), bf16),
-            pltpu.VMEM((D, 768), bf16),
-            pltpu.VMEM((D, D), bf16),
-            pltpu.VMEM((D, FF), bf16),
-            pltpu.VMEM((FF, D), bf16),
-            pltpu.VMEM((1, 768), f32),
-            pltpu.VMEM((1, FF), f32),
-            pltpu.VMEM((8, D), f32),
-            pltpu.VMEM((2, 16, 128), f32),
-            pltpu.VMEM((D, 768), f32),
-            pltpu.VMEM((D, D), f32),
-            pltpu.VMEM((D, FF), f32),
-            pltpu.VMEM((D, FF), f32),
-            pltpu.VMEM((8, 768), f32),
-            pltpu.VMEM((8, FF), f32),
-            pltpu.VMEM((8, D), f32),
-            pltpu.VMEM((2, 10, 8, 128), f32),
-            pltpu.VMEM((4, HEADS * STRIPE, STRIPE), f32),
-            pltpu.VMEM((2, GRID, 384), bf16),
-        ],
-        compiler_params=pltpu.CompilerParams(
-            dimension_semantics=("arbitrary",), vmem_limit_bytes=56 * 1024 * 1024
-        ),
+        scratch_shapes=[pltpu.VMEM(*shape) for shape in shapes.values()],
+        compiler_params=pltpu.CompilerParams(vmem_limit_bytes=60 * 1024 * 1024),
         name="block",
-    )(drops, images, cotangent, first, second)
+    )(drops.T, rows(images), rows(cotangent), first, second)
+    return unrows(out), unrows(gin), first, second
 
 
 def adam_step(master, gradient, first, second, step):

time: 140 us -> 114 us (0.81)
  Pallas kernels: 121 us -> 104 us
  local copies, waits for them, and re-layouts: 14.7 us -> 5.35 us
    pallas_call x1, Pallas kernels: 61.3 us -> 45 us  [compute(): pl.pallas_call(partial(compute_kernel, n_dp, srows, grows, exchange_order...]
    unnamed x21 -> x12, local copies, waits for them, and re-layouts: 9.43 us -> 0.03 us
where the time goes in v3:
time: 114 us
  Pallas kernels  104 us (91%)
  local copies, waits for them, and re-layouts  5.35 us (5%)
  other arithmetic  3.27 us (3%)
    pallas_call x1, Pallas kernels, compute(): pl.pallas_call(partial(compute_kernel, n_dp, srows, grows, exchange_order...  45 us
    pallas_call x1, Pallas kernels, reduce(): pl.pallas_call(partial(reduce_kernel, n_dp, srows, orders, halves), in_sp...  33.5 us
    pallas_call x1, Pallas kernels, gather(): pl.pallas_call(partial(gather_kernel, orders, halves), in_specs=[pl.Block...  25.7 us

profile of v3, /device:TPU:0, one launch (start us, length us, event | category | flops | bytes accessed | tf_op | source)
XLA Modules:
  0.0 113.6 jit_solution(17667413751470178473)
XLA Ops:
  0.7 0.8 reduce.1
  1.5 0.5 dynamic_update_slice.7
  2.1 1.3 %dynamic_update_slice.6 = f32[18432]{0:T(1024)S(1)} dynamic-update-slice(f32[18432]{0:T(1024)S(1)} %broadcast_in_dim.9, f32[16464]{0:T(1024)} %param.15, s32[]{:T(128)S(6)} %select_n.8) | dynamic-update-slice | bytes 131716 | tf_op jit(solution)/shard_map/dynamic_update_slice | solution.py:826
  3.4 0.7 pad_maximum_fusion.own_ref
  4.0 25.7 %gather.1 = (bf16[32,112,128]{2,1,0:T(8,128)(2,1)}, bf16[32,112,128]{2,1,0:T(8,128)(2,1)}) custom-call(f32[224,128]{1,0:T(8,128)} %pad_maximum_fusion.own_ref), custom_call_target="tpu_custom_call" | custom-call | tf_op jit(solution)/shard_map/gather/pallas_call | solution.py:125
  29.8 45.0 %block.1 = (f32[1568,256]{1,0:T(8,128)}, f32[1568,256]{1,0:T(8,128)}, f32[32,112,128]{2,1,0:T(8,128)}, f32[32,112,128]{2,1,0:T(8,128)}) custom-call(s32[2,8]{1,0:T(2,128)} %bitcast.24, bf16[1568,256]{1,0:T(8,128)(2,1)} %bitcast.20, bf16[1568,256]{1,0:T(8,128)(2,1)} %bitcast.21, bf16[32,112,128]{2,1,0:T(8,128)(2,1)} %get-tuple-element.21.first_ref, ...), custom_call_target="tpu_custom_call" | custom-call | tf_op jit(solution)/shard_map/block/pallas_call | solution.py:773
  74.8 0.0 copy-start.1
  74.8 0.0 copy-start.4
  74.8 0.0 copy-start.5
  74.8 0.0 copy-start
  74.8 0.0 copy-start.2
  74.8 0.0 copy-start.3
  74.9 33.5 %reduce.2 = (f32[224,128]{1,0:T(8,128)}, f32[8,128]{1,0:T(8,128)}) custom-call(f32[32,112,128]{2,1,0:T(8,128)} %get-tuple-element.25.first_ref, f32[32,112,128]{2,1,0:T(8,128)} %get-tuple-element.26.second_ref), custom_call_target="tpu_custom_call" | custom-call | tf_op jit(solution)/shard_map/reduce/pallas_call | solution.py:287
  108.3 1.2 %slice.9 = f32[1,1]{1,0:T(1,128)} slice(f32[8,128]{1,0:T(8,128)} %get-tuple-element.27), slice={[0:1], [0:1]} | slice | bytes 8 | tf_op jit(solution)/shard_map/slice | solution.py:846
  109.5 0.8 slice_bitcast_fusion.1
  110.3 0.9 slice_bitcast_fusion
  111.2 0.1 multiply_multiply_fusion.1
  111.3 0.6 broadcast_in_dim.11
  111.9 0.0 copy-done.1
  111.9 0.0 copy-done.4
  111.9 0.0 copy-done.5
  112.0 0.9 fusion.3
  112.8 0.0 copy-done
  112.8 0.0 copy-done.2
  112.8 0.0 copy-done.3
  112.8 0.8 fusion.1
  (3 shorter events, 0.0 us)
Async XLA Ops:
  74.8 37.1 %copy-start.1 = (f32[1,8288]{1,0:T(1,128)S(1)}, f32[1,8288]{1,0:T(1,128)}, u32[]{:S(2)}) copy-start(f32[1,8288]{1,0:T(1,128)} %param.12) | copy-start | bytes 99460
  74.8 37.1 %copy-start.4 = (f32[1,8288]{1,0:T(1,128)S(1)}, f32[1,8288]{1,0:T(1,128)}, u32[]{:S(2)}) copy-start(f32[1,8288]{1,0:T(1,128)} %param.14) | copy-start | bytes 99460
  74.8 37.1 %copy-start.5 = (f32[1,8288]{1,0:T(1,128)S(1)}, f32[1,8288]{1,0:T(1,128)}, u32[]{:S(2)}) copy-start(f32[1,8288]{1,0:T(1,128)} %param.13) | copy-start | bytes 99460
  74.8 38.0 %copy-start = (f32[16464]{0:T(1024)S(1)}, f32[16464]{0:T(1024)}, u32[]{:S(2)}) copy-start(f32[16464]{0:T(1024)} %param.15) | copy-start | bytes 197572
  74.8 38.0 %copy-start.2 = (f32[16464]{0:T(1024)S(1)}, f32[16464]{0:T(1024)}, u32[]{:S(2)}) copy-start(f32[16464]{0:T(1024)} %param.17) | copy-start | bytes 197572
  74.8 38.0 %copy-start.3 = (f32[16464]{0:T(1024)S(1)}, f32[16464]{0:T(1024)}, u32[]{:S(2)}) copy-start(f32[16464]{0:T(1024)} %param.16) | copy-start | bytes 197572

commit v4 on v3

--- a/solution.py
+++ b/solution.py
@@ -35,9 +35,9 @@
 bf16 = jnp.bfloat16
 
 
-def window_rows(total, count):
+def window_rows(total, count, extra=0):
     share = total // count
-    most = max((share * k) % UNIT + share for k in range(count))
+    most = max((share * k) % UNIT + share for k in range(count)) + extra * 128
     return 16 * (-(-most // (2 * UNIT)))
 
 
@@ -47,93 +47,58 @@
 
 HEADS_BIT = -1
 FAST_BITS = 2
-
-
-def exchange_orders(n_dp):
+CARRIED = 4
+GAIN_ROW = 4106
+
+
+def exchange_stages(n_dp):
     bits = n_dp.bit_length() - 1
     far = list(range(bits - 1, 1, -1))
-    near = [1] if bits > 1 else []
-    core = [0] if bits > 0 else []
-    return far + near + [HEADS_BIT] + core, far + [HEADS_BIT] + near + core
-
-
-def place_of(order, k):
-    dp, heads = k // 2, k % 2
+    stages = [tuple(far[i : i + 2]) for i in range(0, len(far), 2)]
+    stages.append((1, HEADS_BIT) if bits > 1 else (HEADS_BIT,))
+    if bits > 0:
+        stages.append((0,))
+    return stages
+
+
+def weight_of(bit):
+    return 1 if bit == HEADS_BIT else 2 << bit
+
+
+def flat_bits(stages):
+    return [bit for stage in stages for bit in stage]
+
+
+def place_of(stages, k):
+    return sum(((k // weight_of(bit)) % 2) << t for t, bit in enumerate(flat_bits(stages)))
+
+
+def device_at(stages, place, first=0):
     return sum(
-        (heads if bit == HEADS_BIT else (dp >> bit) & 1) << t for t, bit in enumerate(order)
+        ((place // (1 << t)) % 2) * weight_of(bit)
+        for t, bit in enumerate(flat_bits(stages))
+        if t >= first
     )
 
 
-def own_bits(order):
+def own_number():
+    return lax.axis_index("dp") * 2 + lax.axis_index("heads")
+
+
+def own_bits(stages):
+    me = own_number()
+    return [(me // weight_of(bit)) % 2 for bit in flat_bits(stages)]
+
+
+def peer(bits, mask):
     dp, heads = lax.axis_index("dp"), lax.axis_index("heads")
-    return [heads if bit == HEADS_BIT else (dp // (1 << bit)) % 2 for bit in order]
-
-
-def partner(bit):
-    if bit == HEADS_BIT:
-        return {"heads": 1 - lax.axis_index("heads")}
-    dp = lax.axis_index("dp")
-    return {"dp": dp + (1 << bit) * (1 - 2 * ((dp // (1 << bit)) % 2))}
-
-
-def half_rows(rows):
-    first = 16 * (-(-rows // 32))
-    return first, rows - first
-
-
-def greet(devices):
-    barrier = pltpu.get_barrier_semaphore()
-    for device in devices:
-        pl.semaphore_signal(barrier, inc=1, device_id=device)
-    pl.semaphore_wait(barrier, len(devices))
-
-
-def gather_kernel(orders, halves, own_ref, first_ref, second_ref, send_sem, recv_sem):
-    greet([partner(bit) for bit in orders[0]])
-    outs = (first_ref, second_ref)
-    start = 0
-    pending = []
-    bits = [own_bits(order) for order in orders]
-    for h in range(2):
-        mine = sum(b * (1 << t) for t, b in enumerate(bits[h]))
-        outs[h][mine] = own_ref[start : start + halves[h]].astype(bf16)
-        start += halves[h]
-        pending.append(None)
-    for t in range(len(orders[0])):
-        for h in range(2):
-            if pending[h] is not None:
-                pending[h].wait()
-            base = sum(b * (1 << u) for u, b in enumerate(bits[h]) if u >= t)
-            held = outs[h].at[pl.ds(base, 1 << t)]
-            pending[h] = pltpu.make_async_remote_copy(
-                src_ref=held,
-                dst_ref=held,
-                send_sem=send_sem.at[h, t],
-                recv_sem=recv_sem.at[h, t],
-                device_id=partner(orders[h][t]),
-            )
-            pending[h].start()
-    for h in range(2):
-        pending[h].wait()
-
-
-def gather(n_dp, rows, own):
-    n = 2 * n_dp
-    orders = exchange_orders(n_dp)
-    halves = half_rows(rows)
-    stages = len(orders[0])
-    return pl.pallas_call(
-        partial(gather_kernel, orders, halves),
-        in_specs=[pl.BlockSpec(memory_space=pltpu.VMEM)],
-        out_specs=[pl.BlockSpec(memory_space=pltpu.VMEM)] * 2,
-        out_shape=[jax.ShapeDtypeStruct((n, half, 128), bf16) for half in halves],
-        scratch_shapes=[
-            pltpu.SemaphoreType.DMA((2, stages)),
-            pltpu.SemaphoreType.DMA((2, stages)),
-        ],
-        compiler_params=pltpu.CompilerParams(collective_id=0, has_side_effects=True),
-        name="gather",
-    )(own)
+    for i, bit in enumerate(bits):
+        if mask >> i & 1:
+            if bit == HEADS_BIT:
+                heads = 1 - heads
+            else:
+                dp = dp + (1 << bit) * (1 - 2 * ((dp // (1 << bit)) % 2))
+    return {"dp": dp, "heads": heads}
 
 
 def group_peers(n_dp):
@@ -149,8 +114,110 @@
     far = []
     for step in range(1, n_dp // fast):
         other = (high + step) % (n_dp // fast)
-        far.append((other, {"dp": other * fast + low}))
+        far.append((other, {"dp": other * fast + low, "heads": heads}))
     return (me, near), (high, far)
+
+
+class Gather:
+    def __init__(self, stages, buffer, send_sem, recv_sem):
+        self.stages, self.buffer = stages, buffer
+        self.send_sem, self.recv_sem = send_sem, recv_sem
+        self.bits = own_bits(stages)
+
+    def copies(self, g, arriving):
+        start = sum(len(stage) for stage in self.stages[:g])
+        for mask in range(1, 1 << len(self.stages[g])):
+            base = 0
+            for u, bit in enumerate(self.bits):
+                flipped = start <= u < start + len(self.stages[g]) and mask >> (u - start) & 1
+                if u >= start:
+                    base = base + (1 << u) * (1 - bit if flipped and arriving else bit)
+            held = self.buffer.at[pl.ds(base, 1 << start)]
+            yield pltpu.make_async_remote_copy(
+                src_ref=held,
+                dst_ref=held,
+                send_sem=self.send_sem.at[g, mask - 1],
+                recv_sem=self.recv_sem.at[g, mask - 1],
+                device_id=peer(self.stages[g], mask),
+            )
+
+    def start(self, g):
+        for copy in self.copies(g, False):
+            copy.start()
+
+    def wait(self, g):
+        for copy in self.copies(g, True):
+            copy.wait_recv()
+        for copy in self.copies(g, False):
+            copy.wait_send()
+
+
+class Scatter:
+    def __init__(self, stages, window, outgoing, incoming, sums, send_sem, recv_sem):
+        self.stages, self.window = stages, window
+        self.outgoing, self.incoming, self.sums = outgoing, incoming, sums
+        self.send_sem, self.recv_sem = send_sem, recv_sem
+        self.bits = own_bits(stages)
+
+    def offset(self, g):
+        return sum(len(stage) for stage in self.stages[:g])
+
+    def held(self, g, place):
+        if g == len(self.stages) - 1:
+            return self.window(place)
+        return self.sums[g + 1][place]
+
+    def copy(self, g, mask):
+        return pltpu.make_async_remote_copy(
+            src_ref=self.outgoing[g].at[mask - 1],
+            dst_ref=self.incoming[g].at[mask - 1],
+            send_sem=self.send_sem.at[g, mask - 1],
+            recv_sem=self.recv_sem.at[g, mask - 1],
+            device_id=peer(self.stages[g], mask),
+        )
+
+    def part(self, g, mask):
+        start = self.offset(g)
+        return sum(
+            (1 << (start + i)) * (1 - self.bits[start + i] if mask >> i & 1 else self.bits[start + i])
+            for i in range(len(self.stages[g]))
+        )
+
+    def start(self, g):
+        for mask in range(1, 1 << len(self.stages[g])):
+            part = self.part(g, mask)
+
+            def fill(i, carry, mask=mask, part=part):
+                self.outgoing[g][mask - 1, i] = self.held(g, part + i).astype(bf16)
+                return carry
+
+            lax.fori_loop(0, 1 << self.offset(g), fill, 0)
+            self.copy(g, mask).start()
+
+    def wait(self, g):
+        masks = range(1, 1 << len(self.stages[g]))
+        for mask in masks:
+            self.copy(g, mask).wait()
+        part = self.part(g, 0)
+
+        def add(i, carry):
+            value = self.held(g, part + i)
+            for mask in masks:
+                value = value + self.incoming[g][mask - 1, i].astype(f32)
+            self.sums[g][i] = value
+            return carry
+
+        lax.fori_loop(0, 1 << self.offset(g), add, 0)
+
+
+def scatter_shapes(stages, rows):
+    outgoing, sums = [], []
+    start = 0
+    for stage in stages:
+        outgoing.append(((1 << len(stage)) - 1, 1 << start, rows, 128))
+        sums.append((1 << start, rows, 128))
+        start += len(stage)
+    return outgoing, sums
 
 
 def all_share(me, peers, stat_ref, send_sem, recv_sem):
@@ -178,148 +245,21 @@
     return jnp.sum(stat_ref[...], axis=0)
 
 
-def reduce_kernel(
-    n_dp,
-    srows,
-    orders,
-    halves,
-    first_ref,
-    second_ref,
-    out_ref,
-    norm_ref,
-    acc_first,
-    acc_second,
-    out_first,
-    out_second,
-    in_first,
-    in_second,
-    near_stat,
-    far_stat,
-    send_sem,
-    recv_sem,
-    near_send,
-    near_recv,
-    far_send,
-    far_recv,
-):
-    n = 2 * n_dp
-    (near_me, near), (far_me, far) = group_peers(n_dp)
-    greet([device for _, device in near] + [device for _, device in far])
-    stages = len(orders[0])
-    held = [first_ref, second_ref]
-    accs = (acc_first, acc_second)
-    outgoing = (out_first, out_second)
-    incoming = (in_first, in_second)
-    bits = [own_bits(order) for order in orders]
-    pending = [None, None]
-    start = [0, halves[0]]
-    for t in range(stages - 1, -1, -1):
-        count = 1 << t
-        for h in range(2):
-            source = held[h]
-            if pending[h] is not None:
-                pending[h].wait()
-            arrived = 2 * count - 1
-            keep, give = bits[h][t] * count, (1 - bits[h][t]) * count
-
-            def value(i, at, h=h, source=source, arrived=arrived, last=pending[h] is None):
-                got = source[at + i]
-                if last:
-                    return got
-                return got + incoming[h][arrived + at + i].astype(f32)
-
-            def fill(i, carry, h=h, give=give, count=count, value=value):
-                outgoing[h][count - 1 + i] = value(i, give).astype(bf16)
-                return carry
-
-            lax.fori_loop(0, count, fill, 0)
-            copy = pltpu.make_async_remote_copy(
-                src_ref=outgoing[h].at[pl.ds(count - 1, count)],
-                dst_ref=incoming[h].at[pl.ds(count - 1, count)],
-                send_sem=send_sem.at[h, t],
-                recv_sem=recv_sem.at[h, t],
-                device_id=partner(orders[h][t]),
-            )
-            copy.start()
-            pending[h] = copy
-
-            def retain(i, carry, h=h, keep=keep, count=count, value=value):
-                accs[h][count - 1 + i] = value(i, keep)
-                return carry
-
-            lax.fori_loop(0, count, retain, 0)
-            held[h] = accs[h].at[pl.ds(count - 1, count)]
-    dp = lax.axis_index("dp")
-    me = dp * 2 + lax.axis_index("heads")
-    sshare, gshare = SHARED_PARAMS // n, GROUP_PARAMS // n_dp
-    soff = (me * sshare) % UNIT
-    goff = (dp * gshare) % UNIT
-    total = jnp.zeros((8, 128), f32)
-    for h in range(2):
-        pending[h].wait()
-        value = held[h][0] + incoming[h][0].astype(f32)
-        out_ref[start[h] : start[h] + halves[h]] = value
-        row = lax.broadcasted_iota(jnp.int32, (halves[h], 128), 0) + start[h]
-        place = row * 128 + lax.broadcasted_iota(jnp.int32, (halves[h], 128), 1)
-        shared = (row < srows) & (place >= soff) & (place < soff + sshare)
-        place = place - srows * 128
-        grouped = (row >= srows) & (place >= goff) & (place < goff + gshare)
-        own = jnp.where(shared | grouped, value, 0.0)
-        total = total + jnp.sum((own * own).reshape(-1, 8, 128), axis=0)
-    near_stat[near_me] = total
-    far_stat[far_me] = all_share(near_me, near, near_stat, near_send, near_recv)
-    total = all_share(far_me, far, far_stat, far_send, far_recv)
-    total = jnp.sum(jnp.sum(total, axis=0, keepdims=True), axis=1, keepdims=True)
-    norm = jnp.sqrt(total)
-    norm_ref[...] = jnp.broadcast_to(norm, (8, 128))
-    threshold = math.sqrt(2 * GROUP_PARAMS + SHARED_PARAMS)
-    out_ref[...] = out_ref[...] * jnp.minimum(1.0, threshold / (norm + 1e-06))
-
-
-def reduce(n_dp, srows, first, second):
-    n = 2 * n_dp
-    orders = exchange_orders(n_dp)
-    halves = (first.shape[1], second.shape[1])
-    stages = len(orders[0])
-    fast = min(1 << FAST_BITS, n_dp)
-    near, far = 2 * fast, n_dp // fast
-    dma = pltpu.SemaphoreType.DMA
-    return pl.pallas_call(
-        partial(reduce_kernel, n_dp, srows, orders, halves),
-        in_specs=[pl.BlockSpec(memory_space=pltpu.VMEM)] * 2,
-        out_specs=[pl.BlockSpec(memory_space=pltpu.VMEM)] * 2,
-        out_shape=[
-            jax.ShapeDtypeStruct((sum(halves), 128), f32),
-            jax.ShapeDtypeStruct((8, 128), f32),
-        ],
-        scratch_shapes=[pltpu.VMEM((n - 1, half, 128), f32) for half in halves]
-        + [pltpu.VMEM((n - 1, half, 128), bf16) for half in halves] * 2
-        + [
-            pltpu.VMEM((near, 8, 128), f32),
-            pltpu.VMEM((far, 8, 128), f32),
-            dma((2, stages)),
-            dma((2, stages)),
-            dma((near,)),
-            dma((near,)),
-            dma((far,)),
-            dma((far,)),
-        ],
-        compiler_params=pltpu.CompilerParams(
-            collective_id=1, has_side_effects=True, vmem_limit_bytes=56 * 1024 * 1024
-        ),
-        name="reduce",
-    )(first, second)
-
-
-def window_parts(halves, rows):
-    parts = []
-    start = 0
-    for h, size in enumerate(halves):
-        low, high = max(rows[0], start), min(rows[1], start + size)
-        if low < high:
-            parts.append((h, low - start, high - start, low - rows[0], high - rows[0]))
-        start += size
-    return parts
+def shift_on(rows, amount):
+    lanes = amount % 128
+    turned = pltpu.roll(rows, lanes, 1)
+    lane = lax.broadcasted_iota(jnp.int32, rows.shape, 1)
+    turned = jnp.where(lane < lanes, pltpu.roll(turned, 1, 0), turned)
+    return pltpu.roll(turned, amount // 128, 0)
+
+
+def shift_back(rows, amount):
+    count = rows.shape[0]
+    lanes = amount % 128
+    turned = pltpu.roll(rows, (128 - lanes) % 128, 1)
+    lane = lax.broadcasted_iota(jnp.int32, rows.shape, 1)
+    turned = jnp.where(lane >= 128 - lanes, pltpu.roll(turned, count - 1, 0), turned)
+    return pltpu.roll(turned, (count - amount // 128) % count, 0)
 
 
 def nn(a, b):
@@ -420,29 +360,20 @@
             ]
 
 
-def prepare_weights(n_dp, srows, grows, orders, halves, weights, sc):
+def prepare_group(n_dp, stages, sc):
     n = 2 * n_dp
-    flat, gflat = sc["flat"], sc["gflat"]
-    flat[...] = jnp.zeros_like(flat)
+    gflat, buffer = sc["gflat"], sc["gweights"]
+    grows = buffer.shape[1]
     gflat[...] = jnp.zeros_like(gflat)
     for k in range(n):
-        at = first_row(SHARED_PARAMS, n, k)
-        for h, low, high, begin, end in window_parts(halves, (0, srows)):
-            window = weights[h][place_of(orders[h], k), low:high]
-            flat[at + begin : at + end] += window.astype(f32)
         at = first_row(GROUP_PARAMS, n_dp, k // 2)
-        for h, low, high, begin, end in window_parts(halves, (srows, srows + grows)):
-            window = weights[h][place_of(orders[h], k), low:high]
-            gflat[k % 2, at + begin : at + end] += window.astype(f32)
-    for c in range(8):
-        cols = slice(c * 128, (c + 1) * 128)
-        sc["uw"][:, cols] = flat[pl.ds(c, D, stride=8), :].astype(bf16)
-        sc["ubias"][:, cols] = flat[2048 + c : 2049 + c, :]
+        size = grows - CARRIED
+        gflat[k % 2, at : at + size] += buffer[place_of(stages, k), 0:size].astype(f32)
+    carried = buffer[place_of(stages, n - 1)].astype(f32)[grows - CARRIED :]
     for c in range(2):
         cols = slice(c * 128, (c + 1) * 128)
-        sc["dw"][:, cols] = flat[pl.ds(2056 + c, FF, stride=2), :].astype(bf16)
-        for i in range(6):
-            sc["vecs"][i : i + 1, cols] = flat[4104 + 2 * i + c : 4105 + 2 * i + c, :]
+        sc["vecs"][1:2, cols] = carried[c : c + 1]
+        sc["vecs"][2:3, cols] = carried[2 + c : 3 + c]
     for j in range(2):
         for c in range(3):
             cols = slice(j * 384 + c * 128, j * 384 + (c + 1) * 128)
@@ -458,9 +389,27 @@
         sc["conv"][j, 0:10] = gflat[j, 1026:1036, :]
 
 
-def place_gradients(n_dp, srows, grows, orders, halves, gradients, sc):
+def prepare_shared(n_dp, stages, sc):
     n = 2 * n_dp
-    flat, gflat = sc["flat"], sc["gflat"]
+    flat, buffer = sc["flat"], sc["sweights"]
+    srows = buffer.shape[1]
+    flat[...] = jnp.zeros_like(flat)
+    for k in range(n):
+        at = first_row(SHARED_PARAMS, n, k)
+        flat[at : at + srows] += buffer[place_of(stages, k)].astype(f32)
+    for c in range(8):
+        cols = slice(c * 128, (c + 1) * 128)
+        sc["uw"][:, cols] = flat[pl.ds(c, D, stride=8), :].astype(bf16)
+        sc["ubias"][:, cols] = flat[2048 + c : 2049 + c, :]
+    for c in range(2):
+        cols = slice(c * 128, (c + 1) * 128)
+        sc["dw"][:, cols] = flat[pl.ds(2056 + c, FF, stride=2), :].astype(bf16)
+        for i in (0, 3, 4, 5):
+            sc["vecs"][i : i + 1, cols] = flat[4104 + 2 * i + c : 4105 + 2 * i + c, :]
+
+
+def place_shared(sc):
+    flat = sc["flat"]
     for c in range(8):
         cols = slice(c * 128, (c + 1) * 128)
         flat[pl.ds(c, D, stride=8), :] = sc["a_uw"][:, cols]
@@ -473,10 +422,15 @@
             ]
     for c in range(2):
         cols = slice(c * 128, (c + 1) * 128)
-        for i in range(6):
+        for i in (0, 3, 4, 5):
             flat[4104 + 2 * i + c : 4105 + 2 * i + c, :] = column_sum(
                 sc["a_vec"][i, :, cols]
             )
+    flat[GAIN_ROW : GAIN_ROW + CARRIED, :] = jnp.zeros((CARRIED, 128), f32)
+
+
+def place_group(sc):
+    gflat = sc["gflat"]
     for j in range(2):
         for c in range(3):
             cols = slice(j * 384 + c * 128, j * 384 + (c + 1) * 128)
@@ -490,15 +444,16 @@
         gflat[j, 769:770, :] = sc["a_pb"][0:1, j * 384 + 256 : j * 384 + 384]
         for i in range(10):
             gflat[j, 1026 + i : 1027 + i, :] = column_sum(sc["a_conv"][j, i])
-    for k in range(n):
-        at = first_row(SHARED_PARAMS, n, k)
-        for h, low, high, begin, end in window_parts(halves, (0, srows)):
-            gradients[h][place_of(orders[h], k), low:high] = flat[at + begin : at + end]
-        at = first_row(GROUP_PARAMS, n_dp, k // 2)
-        for h, low, high, begin, end in window_parts(halves, (srows, srows + grows)):
-            gradients[h][place_of(orders[h], k), low:high] = gflat[
-                k % 2, at + begin : at + end
-            ]
+    for c in range(2):
+        cols = slice(c * 128, (c + 1) * 128)
+        sc["carried"][4 + c : 5 + c, :] = column_sum(sc["a_vec"][1, :, cols])
+        sc["carried"][6 + c : 7 + c, :] = column_sum(sc["a_vec"][2, :, cols])
+    sc["carried"][0:4, :] = jnp.zeros((4, 128), f32)
+
+
+def first_norm(images, sc):
+    for image in images:
+        sc["unit"][image], sc["inverse"][image] = norm_parts(sc["x"][image])
 
 
 def attention_forward(images, sc):
@@ -509,10 +464,7 @@
     gain_one, shift_one = sc["vecs"][1:2], sc["vecs"][2:3]
     qkv_ref, conv = sc["qkv"], sc["conv"]
     for image in images:
-        unit, inverse = norm_parts(sc["x"][image])
-        sc["unit"][image] = unit
-        sc["inverse"][image] = inverse
-        sc["normed"][image] = (unit * gain_one + shift_one).astype(bf16)
+        sc["normed"][image] = (sc["unit"][image] * gain_one + shift_one).astype(bf16)
     for image in images:
         triple = (nn(sc["normed"][image], sc["wq"][...]) + sc["qbias"][...]) * inside
         triple = triple.astype(bf16)
@@ -591,7 +543,7 @@
             grads[i] = part if grads[i] is None else grads[i] + part
     for i, image in enumerate(images):
         scale_one, scale_two, middle, unit_two, inverse_two, _, grad_output, _ = state[i]
-        from_grid(middle + scale_two * (mlps[i] + down_bias), sc["tokens"], image, count)
+        from_grid(middle + scale_two * (mlps[i] + down_bias), sc["outs"], image, count)
         a_vec[3] += tile_sum(grads[i] * unit_two)
         a_vec[4] += tile_sum(grads[i])
         grad_middle = grad_output + norm_back(grads[i], unit_two, inverse_two, gain_two)
@@ -674,9 +626,13 @@
     n = 2 * n_dp
     flat_rows = max(4120, first_row(SHARED_PARAMS, n, n - 1) + srows)
     gflat_rows = max(1040, first_row(GROUP_PARAMS, n_dp, n_dp - 1) + grows)
-    return dict(
+    shapes = dict(
         flat=((flat_rows, 128), f32),
         gflat=((2, gflat_rows, 128), f32),
+        sweights=((n, srows, 128), bf16),
+        gweights=((n, grows, 128), bf16),
+        raw=((grows, 128), f32),
+        carried=((8, 128), f32),
         turn=((GRID, GRID), bf16),
         wq=((D, 768), bf16),
         ow=((D, D), bf16),
@@ -694,7 +650,10 @@
         a_ub=((8, FF), f32),
         a_vec=((6, 8, D), f32),
         a_conv=((2, 10, 8, 128), f32),
+        x_in=((TOK * count, D), bf16),
+        co_in=((TOK * count, D), bf16),
         tokens=((2, TOK * count, 128), f32),
+        outs=((2, TOK * count, 128), f32),
         x=((count, GRID, D), f32),
         co=((count, GRID, D), f32),
         unit=((count, GRID, D), f32),
@@ -707,62 +666,255 @@
         gheads=((count, GRID, D), bf16),
         gtriple=((count, GRID, 768), bf16),
     )
+    stages = exchange_stages(n_dp)
+    for name, rows in (("s", srows), ("g", grows)):
+        outgoing, sums = scatter_shapes(stages, rows)
+        for g, shape in enumerate(outgoing):
+            shapes[f"{name}out{g}"] = (shape, bf16)
+            shapes[f"{name}in{g}"] = (shape, bf16)
+            shapes[f"{name}sum{g}"] = (sums[g], f32)
+    fast = min(1 << FAST_BITS, n_dp)
+    shapes["near_stat"] = ((2 * fast, 8, 128), f32)
+    shapes["far_stat"] = ((n_dp // fast, 8, 128), f32)
+    made = {name: pltpu.VMEM(*shape) for name, shape in shapes.items()}
+    dma = pltpu.SemaphoreType.DMA
+    for name in ("sgather", "ggather", "sscatter", "gscatter"):
+        made[name + "_send"] = dma((len(stages), 3))
+        made[name + "_recv"] = dma((len(stages), 3))
+    for name, size in (("near", 2 * fast), ("far", n_dp // fast)):
+        made[name + "_send"] = dma((size,))
+        made[name + "_recv"] = dma((size,))
+    made["local"] = dma((4,))
+    return made
 
 
 ACCUMULATORS = ("a_wq", "a_ow", "a_uw", "a_dwt", "a_pb", "a_ub", "a_vec", "a_conv")
 TOGETHER = 2
 
 
-def compute_kernel(
+def own_windows(n_dp, sown_ref, gown_ref, soff, goff, stages, sc):
+    n = 2 * n_dp
+    mine = sum((1 << t) * bit for t, bit in enumerate(own_bits(stages)))
+    window = shift_on(sown_ref[...], soff)
+    sc["sweights"][mine] = window.astype(bf16)
+    raw = sc["raw"]
+    grows = raw.shape[0]
+    share = GROUP_PARAMS // n_dp
+    raw[...] = jnp.zeros_like(raw)
+    for r in range(-(-share // 128)):
+        size = min(128, share - 128 * r)
+        raw[r : r + 1, 0:size] = gown_ref[0:1, 128 * r : 128 * r + size]
+    at = GAIN_ROW - first_row(SHARED_PARAMS, n, n - 1)
+    raw[...] = shift_on(raw[...], goff)
+    raw[grows - CARRIED :, :] = window[at : at + CARRIED]
+    sc["gweights"][mine] = raw[...].astype(bf16)
+
+
+def finish(n_dp, soff, goff, ssum, gsum, smine_ref, gmine_ref, norm_ref, near, far, sc):
+    n = 2 * n_dp
+    srows, grows = ssum.shape[0], gsum.shape[0]
+    sshare, gshare = SHARED_PARAMS // n, GROUP_PARAMS // n_dp
+    place = lax.broadcasted_iota(jnp.int32, (srows, 128), 0) * 128
+    place = place + lax.broadcasted_iota(jnp.int32, (srows, 128), 1)
+    shared = jnp.where((place >= soff) & (place < soff + sshare), ssum, 0.0)
+    last = jnp.where(own_number() == n - 1, 1.0, 0.0)
+    at = GAIN_ROW - first_row(SHARED_PARAMS, n, n - 1)
+    smine_ref[...] = shared
+    smine_ref[at : at + CARRIED, :] += gsum[grows - CARRIED :] * last
+    shared = smine_ref[...]
+    place = lax.broadcasted_iota(jnp.int32, (grows, 128), 0) * 128
+    place = place + lax.broadcasted_iota(jnp.int32, (grows, 128), 1)
+    grouped = jnp.where((place >= goff) & (place < goff + gshare), gsum, 0.0)
+    near_me, near_peers = near
+    far_me, far_peers = far
+    sc["near_stat"][near_me] = tile_sum(shared * shared) + tile_sum(grouped * grouped)
+    total = all_share(near_me, near_peers, sc["near_stat"], sc["near_send"], sc["near_recv"])
+    sc["far_stat"][far_me] = total
+    total = all_share(far_me, far_peers, sc["far_stat"], sc["far_send"], sc["far_recv"])
+    total = jnp.sum(jnp.sum(total, axis=0, keepdims=True), axis=1, keepdims=True)
+    norm = jnp.sqrt(total)
+    norm_ref[...] = jnp.broadcast_to(norm, (8, 128))
+    threshold = math.sqrt(2 * GROUP_PARAMS + SHARED_PARAMS)
+    factor = jnp.minimum(1.0, threshold / (norm + 1e-06))
+    smine_ref[...] = shift_back(shared * factor, soff)
+    gmine_ref[...] = shift_back(grouped * factor, goff)
+
+
+def step_kernel(
     n_dp,
-    srows,
-    grows,
-    orders,
-    halves,
     count,
     names,
     drop_ref,
     x_ref,
     co_ref,
-    first_ref,
-    second_ref,
+    sown_ref,
+    gown_ref,
     out_ref,
     gin_ref,
-    gfirst_ref,
-    gsecond_ref,
+    smine_ref,
+    gmine_ref,
+    norm_ref,
     *scratch,
 ):
     sc = dict(zip(names, scratch))
-    sc["turn"][...] = turn_matrix()
-    to_grid(x_ref, sc["tokens"], sc["x"])
-    to_grid(co_ref, sc["tokens"], sc["co"])
-    for name in ACCUMULATORS:
-        sc[name][...] = jnp.zeros_like(sc[name])
-    prepare_weights(n_dp, srows, grows, orders, halves, (first_ref, second_ref), sc)
-
-    def run(phase):
+    n = 2 * n_dp
+    stages = exchange_stages(n_dp)
+    near, far = group_peers(n_dp)
+    devices = [device for _, device in near[1] + far[1]]
+    barrier = pltpu.get_barrier_semaphore()
+    for device in devices:
+        pl.semaphore_signal(barrier, inc=1, device_id=device)
+    load_x = pltpu.make_async_copy(x_ref, sc["x_in"], sc["local"].at[0])
+    load_co = pltpu.make_async_copy(co_ref, sc["co_in"], sc["local"].at[1])
+    load_x.start()
+    load_co.start()
+    soff = (own_number() * (SHARED_PARAMS // n)) % UNIT
+    goff = (lax.axis_index("dp") * (GROUP_PARAMS // n_dp)) % UNIT
+    own_windows(n_dp, sown_ref, gown_ref, soff, goff, stages, sc)
+    pl.semaphore_wait(barrier, len(devices))
+    ggather = Gather(stages, sc["gweights"], sc["ggather_send"], sc["ggather_recv"])
+    sgather = Gather(stages, sc["sweights"], sc["sgather_send"], sc["sgather_recv"])
+
+    def run(phase, extra=None, together=TOGETHER):
         def body(i, carry):
-            phase([i * TOGETHER + k for k in range(TOGETHER)])
+            if extra is not None:
+                for at, action in extra.items():
+                    pl.when(i == at)(action)
+            phase([i * together + k for k in range(together)])
             return carry
 
-        lax.fori_loop(0, count // TOGETHER, body, 0)
-
-    run(lambda images: attention_forward(images, sc))
+        lax.fori_loop(0, count // together, body, 0)
+
+    last = len(stages) - 1
+    ggather.start(0)
+    sgather.start(0)
+    load_x.wait()
+    to_grid(sc["x_in"], sc["tokens"], sc["x"])
+    for g in range(last):
+        ggather.wait(g)
+        ggather.start(g + 1)
+        if g == 0:
+            sc["turn"][...] = turn_matrix()
+            run(lambda images: first_norm(images, sc))
+            for name in ACCUMULATORS:
+                sc[name][...] = jnp.zeros_like(sc[name])
+    load_co.wait()
+    to_grid(sc["co_in"], sc["tokens"], sc["co"])
+    ggather.wait(last)
+    prepare_group(n_dp, stages, sc)
+
+    steps = count // TOGETHER
+    forward, backward = {}, {}
+    for g in range(last):
+        def advance(g=g):
+            sgather.wait(g)
+            sgather.start(g + 1)
+
+        at = min(g, steps - 1)
+        forward[at] = forward.get(at, []) + [advance]
+    run(lambda images: attention_forward(images, sc), {at: chain(todo) for at, todo in forward.items()})
+    sgather.wait(last)
+    prepare_shared(n_dp, stages, sc)
     run(lambda images: mlp_both(images, count, drop_ref, sc))
+    stores = []
     for half in range(2):
-        out_ref[:, half * 128 : (half + 1) * 128] = sc["tokens"][half]
-    run(lambda images: attention_back(images, count, sc))
+        cols = slice(half * 128, (half + 1) * 128)
+        stores.append(
+            pltpu.make_async_copy(sc["outs"].at[half], out_ref.at[:, cols], sc["local"].at[half])
+        )
+        stores[-1].start()
+    place_shared(sc)
+
+    half_bits = len(flat_bits(stages)) - 1
+    top = own_bits(stages)[half_bits]
+    srows, grows = sc["sweights"].shape[1], sc["gweights"].shape[1]
+
+    def swindow(place):
+        k = device_at(stages, place)
+        row = (k * (SHARED_PARAMS // n)) // UNIT * 8
+        return sc["flat"][pl.ds(pl.multiple_of(row, 8), srows), :]
+
+    upper = (lax.broadcasted_iota(jnp.int32, (8, 128), 0) < 8 - CARRIED).astype(f32)
+
+    def gwindow(place):
+        k = device_at(stages, place)
+        row = ((k // 2) * (GROUP_PARAMS // n_dp)) // UNIT * 8
+        return jnp.concatenate(
+            [
+                sc["gflat"][k % 2, pl.ds(pl.multiple_of(row, 8), grows - 8), :],
+                sc["gflat"][k % 2, pl.ds(pl.multiple_of(row + grows - 8, 8), 8), :] * upper
+                + sc["carried"][...],
+            ],
+            axis=0,
+        )
+
+    def scatter(name, window):
+        parts = [[sc[f"{name}{kind}{g}"] for g in range(last + 1)] for kind in ("out", "in", "sum")]
+        return Scatter(
+            stages, window, *parts, sc[name + "scatter_send"], sc[name + "scatter_recv"]
+        )
+
+    sscatter = scatter("s", swindow)
+    gscatter = scatter("g", gwindow)
+    sscatter.start(last)
+    for g in range(last, -1, -1):
+        def advance(g=g):
+            sscatter.wait(g)
+            if g > 0:
+                sscatter.start(g - 1)
+
+        at = min(last - g + 1, steps - 1)
+        backward[at] = backward.get(at, []) + [advance]
+    run(
+        lambda images: attention_back(images, count, sc),
+        {at: chain(todo) for at, todo in backward.items()},
+    )
     for half in range(2):
-        gin_ref[:, half * 128 : (half + 1) * 128] = sc["tokens"][half]
-    place_gradients(n_dp, srows, grows, orders, halves, (gfirst_ref, gsecond_ref), sc)
-
-
-def compute(n_dp, srows, grows, drops, images, cotangent, first, second):
-    n = 2 * n_dp
+        cols = slice(half * 128, (half + 1) * 128)
+        stores.append(
+            pltpu.make_async_copy(
+                sc["tokens"].at[half], gin_ref.at[:, cols], sc["local"].at[2 + half]
+            )
+        )
+        stores[-1].start()
+    place_group(sc)
+    gscatter.start(last)
+    for g in range(last, -1, -1):
+        gscatter.wait(g)
+        if g > 0:
+            gscatter.start(g - 1)
+    finish(
+        n_dp,
+        soff,
+        goff,
+        sc["ssum0"][0],
+        sc["gsum0"][0],
+        smine_ref,
+        gmine_ref,
+        norm_ref,
+        near,
+        far,
+        sc,
+    )
+    for store in stores:
+        store.wait()
+
+
+def chain(actions):
+    def run_all():
+        for action in actions:
+            action()
+
+    return run_all
+
+
+def step(n_dp, drops, images, cotangent, sown, gown):
     count = images.shape[0]
-    halves = (first.shape[1], second.shape[1])
+    srows = sown.shape[0]
+    grows = window_rows(GROUP_PARAMS, n_dp, CARRIED)
     shapes = scratch_shapes(n_dp, srows, grows, count)
     vmem = pl.BlockSpec(memory_space=pltpu.VMEM)
+    anywhere = pl.BlockSpec(memory_space=pl.ANY)
 
     def rows(array):
         return jnp.swapaxes(array, 0, 1).reshape(TOK * count, D)
@@ -770,26 +922,23 @@
     def unrows(array):
         return jnp.swapaxes(array.reshape(TOK, count, D), 0, 1)
 
-    out, gin, first, second = pl.pallas_call(
-        partial(
-            compute_kernel,
-            n_dp,
-            srows,
-            grows,
-            exchange_orders(n_dp),
-            halves,
-            count,
-            tuple(shapes),
+    out, gin, smine, gmine, norm = pl.pallas_call(
+        partial(step_kernel, n_dp, count, tuple(shapes)),
+        in_specs=[pl.BlockSpec(memory_space=pltpu.SMEM), anywhere, anywhere, vmem, vmem],
+        out_specs=[anywhere, anywhere, vmem, vmem, vmem],
+        out_shape=[jax.ShapeDtypeStruct((TOK * count, D), f32)] * 2
+        + [
+            jax.ShapeDtypeStruct((srows, 128), f32),
+            jax.ShapeDtypeStruct((grows, 128), f32),
+            jax.ShapeDtypeStruct((8, 128), f32),
+        ],
+        scratch_shapes=list(shapes.values()),
+        compiler_params=pltpu.CompilerParams(
+            collective_id=0, has_side_effects=True, vmem_limit_bytes=62 * 1024 * 1024
         ),
-        in_specs=[pl.BlockSpec(memory_space=pltpu.SMEM)] + [vmem] * 4,
-        out_specs=[vmem] * 4,
-        out_shape=[jax.ShapeDtypeStruct((TOK * count, D), f32)] * 2
-        + [jax.ShapeDtypeStruct((n, half, 128), f32) for half in halves],
-        scratch_shapes=[pltpu.VMEM(*shape) for shape in shapes.values()],
-        compiler_params=pltpu.CompilerParams(vmem_limit_bytes=60 * 1024 * 1024),
-        name="block",
-    )(drops.T, rows(images), rows(cotangent), first, second)
-    return unrows(out), unrows(gin), first, second
+        name="step",
+    )(drops.T, rows(images), rows(cotangent), sown, gown)
+    return unrows(out), unrows(gin), smine, gmine, norm
 
 
 def adam_step(master, gradient, first, second, step):
@@ -817,28 +966,19 @@
 ):
     n = 2 * n_dp
     srows = window_rows(SHARED_PARAMS, n)
-    grows = window_rows(GROUP_PARAMS, n_dp)
-    dp = lax.axis_index("dp")
-    me = dp * 2 + lax.axis_index("heads")
     sshare, gshare = SHARED_PARAMS // n, GROUP_PARAMS // n_dp
-    soff = lax.rem(me * sshare, UNIT)
-    goff = lax.rem(dp * gshare, UNIT)
-    sblock = lax.dynamic_update_slice(jnp.zeros((srows * 128,), f32), shared_master, (soff,))
-    gblock = lax.dynamic_update_slice(jnp.zeros((grows * 128,), f32), group_master[0], (goff,))
-    own = jnp.concatenate([sblock.reshape(srows, 128), gblock.reshape(grows, 128)], axis=0)
-    first, second = gather(n_dp, srows + grows, own)
-    output, input_grad, first, second = compute(
-        n_dp, srows, grows, drop_masks, images, cotangent, first, second
+    sown = jnp.pad(shared_master, (0, srows * 128 - sshare)).reshape(srows, 128)
+    output, input_grad, smine, gmine, norm = step(
+        n_dp, drop_masks, images, cotangent, sown, group_master
     )
-    mine, norm = reduce(n_dp, srows, first, second)
-    shared_grad = lax.dynamic_slice(mine[:srows].reshape(-1), (soff,), (sshare,))
-    group_grad = lax.dynamic_slice(mine[srows:].reshape(-1), (goff,), (gshare,))[None, :]
-    step = jnp.float32(STEP)
+    shared_grad = smine.reshape(-1)[:sshare]
+    group_grad = gmine.reshape(-1)[:gshare][None, :]
+    now = jnp.float32(STEP)
     group_new, group_first, group_second = adam_step(
-        group_master, group_grad, group_m1, group_m2, step
+        group_master, group_grad, group_m1, group_m2, now
     )
     shared_new, shared_first, shared_second = adam_step(
-        shared_master, shared_grad, shared_m1, shared_m2, step
+        shared_master, shared_grad, shared_m1, shared_m2, now
     )
     return (
         output,

time: 114 us -> 105 us (0.921)
  Pallas kernels: 104 us -> 93.7 us
  local copies, waits for them, and re-layouts: 5.35 us -> 7.42 us
    pallas_call x3 -> x1, Pallas kernels: 104 us -> 93.7 us  [step(): pl.pallas_call(partial(step_kernel, n_dp, count, tuple(shapes)), in_specs...]
    unnamed x12 -> x16, local copies, waits for them, and re-layouts: 0.03 us -> 3.98 us
    dynamic_update_slice x2 -> x0, local copies, waits for them, and re-layouts: 1.81 us -> none  [the longest x1 1.3 us: on_device(): lax.dynamic_update_slice(jnp.zeros((srows * 128,), f32), shared_master, (...]
where the time goes in v4:
time: 105 us
  Pallas kernels  93.7 us (89%)
  local copies, waits for them, and re-layouts  7.42 us (7%)
  other arithmetic  3.25 us (3%)
    pallas_call x1, Pallas kernels, step(): pl.pallas_call(partial(step_kernel, n_dp, count, tuple(shapes)), in_specs...  93.7 us
    unnamed x16, local copies, waits for them, and re-layouts  3.98 us

profile of v4, /device:TPU:0, one launch (start us, length us, event | category | flops | bytes accessed | tf_op | source)
XLA Modules:
  0.0 105.0 jit_solution(17416105122836306140)
XLA Ops:
  0.6 0.0 copy-start.1
  0.7 0.0 copy-start.2
  0.7 0.0 copy-start.3
  0.7 0.0 copy-start.4
  0.7 0.0 copy-start.5
  0.7 0.0 copy-start.6
  0.7 1.6 %pad_bitcast_fusion.sown_ref = f32[144,128]{1,0:T(8,128)} fusion(f32[16464]{0:T(1024)} %param.15), kind=kLoop, calls=%fused_computation.1 | loop fusion | bytes 139584 | tf_op jit(solution)/shard_map/reshape | solution.py:970
  2.3 93.7 %step.1 = (f32[1568,256]{1,0:T(8,128)}, f32[1568,256]{1,0:T(8,128)}, f32[144,128]{1,0:T(8,128)}, f32[80,128]{1,0:T(8,128)}, f32[8,128]{1,0:T(8,128)}) custom-call(s32[2,8]{1,0:T(2,128)} %bitcast.24, bf16[1568,256]{1,0:T(8,128)(2,1)} %bitcast.20, bf16[1568,256]{1,0:T(8,128)(2,1)} %bitcast.21, f32[144,128]{1,0:T(8,128)} %pad_bitcast_fusion.sown_ref, ...), custom_call_target="tpu_custom_call" | custom-call | tf_op jit(solution)/shard_map/step/pallas_call | solution.py:925
  96.0 1.2 %slice.9 = f32[1,1]{1,0:T(1,128)} slice(f32[8,128]{1,0:T(8,128)} %get-tuple-element.20), slice={[0:1], [0:1]} | slice | bytes 8 | tf_op jit(solution)/shard_map/slice | solution.py:986
  97.2 0.8 broadcast_multiply_fusion
  98.0 0.6 broadcast_in_dim.3
  98.6 0.0 copy-done.2
  98.6 0.0 copy-done.5
  98.6 0.0 copy-done.6
  98.6 0.9 fusion.3
  99.5 0.0 copy-done.1
  99.5 0.0 copy-done.3
  99.5 0.0 copy-done.4
  99.5 1.6 %fusion.1 = (bf16[16464]{0:T(1024)(128)(2,1)}, f32[16464]{0:T(1024)}, f32[16464]{0:T(1024)}, f32[16464]{0:T(1024)}, f32[16464]{0:T(1024)}) fusion(f32[16464]{0:T(1024)S(1)} %copy-done.1, f32[16464]{0:T(1024)S(1)} %copy-done.3, f32[16464]{0:T(1024)S(1)} %copy-done.4, f32[18432]{0:T(1024)} %bitcast.22), kind=kLoop, calls=%fused_computation.10 | loop fusion | flops 263424 | bytes 559776 | tf_op jit(solution)/shard_map/convert_element_type | solution.py:996
  101.1 0.0 copy-start
  101.1 2.8 %copy.24 = f32[8,196,256]{2,0,1:T(8,128)} copy(f32[8,196,256]{2,0,1:T(8,128)} %bitcast.19) | data formatting | bytes 3211264
  103.9 0.0 copy-done
  103.9 1.2 %copy.25 = f32[8,196,256]{2,0,1:T(8,128)} copy(f32[8,196,256]{2,0,1:T(8,128)S(1)} %bitcast.18) | data formatting | bytes 3211264
Async XLA Ops:
  0.6 98.8 %copy-start.1 = (f32[16464]{0:T(1024)S(1)}, f32[16464]{0:T(1024)}, u32[]{:S(2)}) copy-start(f32[16464]{0:T(1024)} %param.15) | copy-start | bytes 197572
  0.7 97.9 %copy-start.2 = (f32[1,8288]{1,0:T(1,128)S(1)}, f32[1,8288]{1,0:T(1,128)}, u32[]{:S(2)}) copy-start(f32[1,8288]{1,0:T(1,128)} %gown_ref.1) | copy-start | bytes 99460
  0.7 98.8 %copy-start.3 = (f32[16464]{0:T(1024)S(1)}, f32[16464]{0:T(1024)}, u32[]{:S(2)}) copy-start(f32[16464]{0:T(1024)} %param.17) | copy-start | bytes 197572
  0.7 98.8 %copy-start.4 = (f32[16464]{0:T(1024)S(1)}, f32[16464]{0:T(1024)}, u32[]{:S(2)}) copy-start(f32[16464]{0:T(1024)} %param.16) | copy-start | bytes 197572
  0.7 97.9 %copy-start.5 = (f32[1,8288]{1,0:T(1,128)S(1)}, f32[1,8288]{1,0:T(1,128)}, u32[]{:S(2)}) copy-start(f32[1,8288]{1,0:T(1,128)} %param.14) | copy-start | bytes 99460
  0.7 97.9 %copy-start.6 = (f32[1,8288]{1,0:T(1,128)S(1)}, f32[1,8288]{1,0:T(1,128)}, u32[]{:S(2)}) copy-start(f32[1,8288]{1,0:T(1,128)} %param.13) | copy-start | bytes 99460
  101.1 2.8 %copy-start = (f32[1568,256]{1,0:T(8,128)S(1)}, f32[1568,256]{1,0:T(8,128)}, u32[]{:S(2)}) copy-start(f32[1568,256]{1,0:T(8,128)} %get-tuple-element.19) | copy-start | bytes 4816900

commit v5 on v4

--- a/solution.py
+++ b/solution.py
@@ -46,7 +46,7 @@
 
 
 HEADS_BIT = -1
-FAST_BITS = 2
+FAST_BITS = 4
 CARRIED = 4
 GAIN_ROW = 4106
 
@@ -504,55 +504,66 @@
 def mlp_both(images, count, drop_ref, sc):
     down_bias = sc["vecs"][0:1]
     gain_two, shift_two, out_bias = sc["vecs"][3:4], sc["vecs"][4:5], sc["vecs"][5:6]
-    ones = jnp.ones((8, GRID), bf16)
     a_vec = sc["a_vec"]
     uw, dw, ubias = sc["uw"], sc["dw"], sc["ubias"]
+    many = len(images)
+    ones = jnp.ones((8, many * GRID), bf16)
+
+    def join(parts):
+        return jnp.concatenate(parts, axis=0)
+
+    def part_of(joined, i):
+        return joined[i * GRID : (i + 1) * GRID]
+
+    heads = sc["heads"][pl.ds(images[0], many)].reshape(many * GRID, D)
+    branch = nn(heads, sc["ow"][...])
     state = []
-    for image in images:
+    for i, image in enumerate(images):
         scale_one = drop_ref[0, image].astype(f32) / keep_prob
         scale_two = drop_ref[1, image].astype(f32) / keep_prob
-        branch = nn(sc["heads"][image], sc["ow"][...])
-        middle = sc["x"][image] + scale_one * (branch + out_bias)
+        middle = sc["x"][image] + scale_one * (part_of(branch, i) + out_bias)
         unit_two, inverse_two = norm_parts(middle)
-        normed_two = (unit_two * gain_two + shift_two).astype(bf16)
         grad_output = sc["co"][image]
         grad_mlp_f = scale_two * grad_output
         a_vec[0] += tile_sum(grad_mlp_f)
-        grad_mlp = grad_mlp_f.astype(bf16)
-        state.append(
-            (scale_one, scale_two, middle, unit_two, inverse_two, normed_two, grad_output, grad_mlp)
-        )
-    mlps = [None] * len(images)
-    grads = [None] * len(images)
+        state.append((scale_one, scale_two, middle, unit_two, inverse_two, grad_output, grad_mlp_f))
+    normed_two = join([(st[3] * gain_two + shift_two).astype(bf16) for st in state])
+    grad_mlp = join([st[6].astype(bf16) for st in state])
+    mlp = None
+    grad_normed = None
     for c in range(4):
         cols = slice(c * 256, (c + 1) * 256)
-        for i in range(len(images)):
-            normed_two, grad_mlp = state[i][5], state[i][7]
-            hidden = nn(normed_two, uw[:, cols]) + ubias[:, cols]
-            density = jnp.exp(hidden * hidden * -0.5) * (1.0 / math.sqrt(2.0 * math.pi))
-            phi = 0.5 + 0.5 * lax.erf(hidden * math.sqrt(0.5))
-            active = (hidden * phi).astype(bf16)
-            part = nn(active, dw[cols, :])
-            mlps[i] = part if mlps[i] is None else mlps[i] + part
-            sc["a_dwt"][:, cols] += tn(grad_mlp, active)
-            grad_active = nt(grad_mlp, dw[cols, :])
-            grad_hidden = (grad_active * (phi + hidden * density)).astype(bf16)
-            sc["a_ub"][:, cols] += nn(ones, grad_hidden)
-            sc["a_uw"][:, cols] += tn(normed_two, grad_hidden)
-            part = nt(grad_hidden, uw[:, cols])
-            grads[i] = part if grads[i] is None else grads[i] + part
+        hidden = nn(normed_two, uw[:, cols]) + ubias[:, cols]
+        density = jnp.exp(hidden * hidden * -0.5) * (1.0 / math.sqrt(2.0 * math.pi))
+        phi = 0.5 + 0.5 * lax.erf(hidden * math.sqrt(0.5))
+        active = (hidden * phi).astype(bf16)
+        part = nn(active, dw[cols, :])
+        mlp = part if mlp is None else mlp + part
+        sc["a_dwt"][:, cols] += tn(grad_mlp, active)
+        grad_active = nt(grad_mlp, dw[cols, :])
+        grad_hidden = (grad_active * (phi + hidden * density)).astype(bf16)
+        sc["a_ub"][:, cols] += nn(ones, grad_hidden)
+        sc["a_uw"][:, cols] += tn(normed_two, grad_hidden)
+        part = nt(grad_hidden, uw[:, cols])
+        grad_normed = part if grad_normed is None else grad_normed + part
+    grad_branch = []
     for i, image in enumerate(images):
-        scale_one, scale_two, middle, unit_two, inverse_two, _, grad_output, _ = state[i]
-        from_grid(middle + scale_two * (mlps[i] + down_bias), sc["outs"], image, count)
-        a_vec[3] += tile_sum(grads[i] * unit_two)
-        a_vec[4] += tile_sum(grads[i])
-        grad_middle = grad_output + norm_back(grads[i], unit_two, inverse_two, gain_two)
+        scale_one, scale_two, middle, unit_two, inverse_two, grad_output, _ = state[i]
+        from_grid(
+            middle + scale_two * (part_of(mlp, i) + down_bias), sc["outs"], image, count
+        )
+        grad = part_of(grad_normed, i)
+        a_vec[3] += tile_sum(grad * unit_two)
+        a_vec[4] += tile_sum(grad)
+        grad_middle = grad_output + norm_back(grad, unit_two, inverse_two, gain_two)
         sc["gmid"][image] = grad_middle
         grad_branch_f = scale_one * grad_middle
         a_vec[5] += tile_sum(grad_branch_f)
-        grad_branch = grad_branch_f.astype(bf16)
-        sc["a_ow"][...] += tn(sc["heads"][image], grad_branch)
-        sc["gheads"][image] = nt(grad_branch, sc["ow"][...]).astype(bf16)
+        grad_branch.append(grad_branch_f.astype(bf16))
+    grad_branch = join(grad_branch)
+    sc["a_ow"][...] += tn(heads, grad_branch)
+    grad_heads = nt(grad_branch, sc["ow"][...]).astype(bf16)
+    sc["gheads"][pl.ds(images[0], many)] = grad_heads.reshape(many, GRID, D)
 
 
 def attention_back(images, count, sc):
@@ -690,6 +701,8 @@
 
 ACCUMULATORS = ("a_wq", "a_ow", "a_uw", "a_dwt", "a_pb", "a_ub", "a_vec", "a_conv")
 TOGETHER = 2
+MLP_TOGETHER = 4
+GATHER_STEP = 2
 
 
 def own_windows(n_dp, sown_ref, gown_ref, soff, goff, stages, sc):
@@ -771,6 +784,9 @@
     soff = (own_number() * (SHARED_PARAMS // n)) % UNIT
     goff = (lax.axis_index("dp") * (GROUP_PARAMS // n_dp)) % UNIT
     own_windows(n_dp, sown_ref, gown_ref, soff, goff, stages, sc)
+    sc["turn"][...] = turn_matrix()
+    load_x.wait()
+    to_grid(sc["x_in"], sc["tokens"], sc["x"])
     pl.semaphore_wait(barrier, len(devices))
     ggather = Gather(stages, sc["gweights"], sc["ggather_send"], sc["ggather_recv"])
     sgather = Gather(stages, sc["sweights"], sc["sgather_send"], sc["sgather_recv"])
@@ -788,34 +804,31 @@
     last = len(stages) - 1
     ggather.start(0)
     sgather.start(0)
-    load_x.wait()
-    to_grid(sc["x_in"], sc["tokens"], sc["x"])
     for g in range(last):
+        if g == last - 1:
+            run(lambda images: first_norm(images, sc))
         ggather.wait(g)
         ggather.start(g + 1)
-        if g == 0:
-            sc["turn"][...] = turn_matrix()
-            run(lambda images: first_norm(images, sc))
-            for name in ACCUMULATORS:
-                sc[name][...] = jnp.zeros_like(sc[name])
+        if g < last - 1:
+            sgather.wait(g)
+            sgather.start(g + 1)
+    for name in ACCUMULATORS:
+        sc[name][...] = jnp.zeros_like(sc[name])
     load_co.wait()
     to_grid(sc["co_in"], sc["tokens"], sc["co"])
     ggather.wait(last)
     prepare_group(n_dp, stages, sc)
 
     steps = count // TOGETHER
-    forward, backward = {}, {}
-    for g in range(last):
-        def advance(g=g):
-            sgather.wait(g)
-            sgather.start(g + 1)
-
-        at = min(g, steps - 1)
-        forward[at] = forward.get(at, []) + [advance]
-    run(lambda images: attention_forward(images, sc), {at: chain(todo) for at, todo in forward.items()})
+    backward = {}
+    def spread_cores():
+        sgather.wait(last - 1)
+        sgather.start(last)
+
+    run(lambda images: attention_forward(images, sc), {min(GATHER_STEP, steps - 1): spread_cores})
     sgather.wait(last)
     prepare_shared(n_dp, stages, sc)
-    run(lambda images: mlp_both(images, count, drop_ref, sc))
+    run(lambda images: mlp_both(images, count, drop_ref, sc), None, MLP_TOGETHER)
     stores = []
     for half in range(2):
         cols = slice(half * 128, (half + 1) * 128)
@@ -857,13 +870,12 @@
     sscatter = scatter("s", swindow)
     gscatter = scatter("g", gwindow)
     sscatter.start(last)
-    for g in range(last, -1, -1):
+    for g in range(last, 0, -1):
         def advance(g=g):
             sscatter.wait(g)
-            if g > 0:
-                sscatter.start(g - 1)
-
-        at = min(last - g + 1, steps - 1)
+            sscatter.start(g - 1)
+
+        at = min(1 + 2 * (last - g), steps - 1)
         backward[at] = backward.get(at, []) + [advance]
     run(
         lambda images: attention_back(images, count, sc),
@@ -879,6 +891,7 @@
         stores[-1].start()
     place_group(sc)
     gscatter.start(last)
+    sscatter.wait(0)
     for g in range(last, -1, -1):
         gscatter.wait(g)
         if g > 0:

time: 105 us -> 89.4 us (0.85)
  Pallas kernels: 93.7 us -> 77.6 us
    pallas_call x1, Pallas kernels: 93.7 us -> 77.6 us  [step(): pl.pallas_call(partial(step_kernel, n_dp, count, tuple(shapes)), in_specs...]
where the time goes in v5:
time: 89.4 us; the launch traced here: 89 us
  Pallas kernels  77.6 us (87%)
  local copies, waits for them, and re-layouts  7.42 us (8%)
  other arithmetic  3.25 us (4%)
    pallas_call x1, Pallas kernels, step(): pl.pallas_call(partial(step_kernel, n_dp, count, tuple(shapes)), in_specs...  77.6 us
    unnamed x16, local copies, waits for them, and re-layouts  3.98 us

profile of v5, /device:TPU:0, one launch (start us, length us, event | category | flops | bytes accessed | tf_op | source)
XLA Modules:
  0.0 89.0 jit_solution(18161926426747330460)
XLA Ops:
  0.6 0.0 copy-start.1
  0.7 0.0 copy-start.2
  0.7 0.0 copy-start.3
  0.7 0.0 copy-start.4
  0.7 0.0 copy-start.5
  0.7 0.0 copy-start.6
  0.7 1.6 %pad_bitcast_fusion.sown_ref = f32[144,128]{1,0:T(8,128)} fusion(f32[16464]{0:T(1024)} %param.15), kind=kLoop, calls=%fused_computation.1 | loop fusion | bytes 139584 | tf_op jit(solution)/shard_map/reshape | solution.py:983
  2.3 77.6 %step.1 = (f32[1568,256]{1,0:T(8,128)}, f32[1568,256]{1,0:T(8,128)}, f32[144,128]{1,0:T(8,128)}, f32[80,128]{1,0:T(8,128)}, f32[8,128]{1,0:T(8,128)}) custom-call(s32[2,8]{1,0:T(2,128)} %bitcast.24, bf16[1568,256]{1,0:T(8,128)(2,1)} %bitcast.20, bf16[1568,256]{1,0:T(8,128)(2,1)} %bitcast.21, f32[144,128]{1,0:T(8,128)} %pad_bitcast_fusion.sown_ref, ...), custom_call_target="tpu_custom_call" | custom-call | tf_op jit(solution)/shard_map/step/pallas_call | solution.py:938
  80.0 1.2 %slice.9 = f32[1,1]{1,0:T(1,128)} slice(f32[8,128]{1,0:T(8,128)} %get-tuple-element.20), slice={[0:1], [0:1]} | slice | bytes 8 | tf_op jit(solution)/shard_map/slice | solution.py:999
  81.1 0.8 broadcast_multiply_fusion
  81.9 0.6 broadcast_in_dim.3
  82.6 0.0 copy-done.2
  82.6 0.0 copy-done.5
  82.6 0.0 copy-done.6
  82.6 0.9 fusion.3
  83.4 0.0 copy-done.1
  83.4 0.0 copy-done.3
  83.4 0.0 copy-done.4
  83.4 1.6 %fusion.1 = (bf16[16464]{0:T(1024)(128)(2,1)}, f32[16464]{0:T(1024)}, f32[16464]{0:T(1024)}, f32[16464]{0:T(1024)}, f32[16464]{0:T(1024)}) fusion(f32[16464]{0:T(1024)S(1)} %copy-done.1, f32[16464]{0:T(1024)S(1)} %copy-done.3, f32[16464]{0:T(1024)S(1)} %copy-done.4, f32[18432]{0:T(1024)} %bitcast.22), kind=kLoop, calls=%fused_computation.10 | loop fusion | flops 263424 | bytes 559776 | tf_op jit(solution)/shard_map/convert_element_type | solution.py:1009
  85.1 0.0 copy-start
  85.1 2.8 %copy.24 = f32[8,196,256]{2,0,1:T(8,128)} copy(f32[8,196,256]{2,0,1:T(8,128)} %bitcast.19) | data formatting | bytes 3211264
  87.9 0.0 copy-done
  87.9 1.2 %copy.25 = f32[8,196,256]{2,0,1:T(8,128)} copy(f32[8,196,256]{2,0,1:T(8,128)S(1)} %bitcast.18) | data formatting | bytes 3211264
Async XLA Ops:
  0.6 82.8 %copy-start.1 = (f32[16464]{0:T(1024)S(1)}, f32[16464]{0:T(1024)}, u32[]{:S(2)}) copy-start(f32[16464]{0:T(1024)} %param.15) | copy-start | bytes 197572
  0.7 81.9 %copy-start.2 = (f32[1,8288]{1,0:T(1,128)S(1)}, f32[1,8288]{1,0:T(1,128)}, u32[]{:S(2)}) copy-start(f32[1,8288]{1,0:T(1,128)} %gown_ref.1) | copy-start | bytes 99460
  0.7 82.8 %copy-start.3 = (f32[16464]{0:T(1024)S(1)}, f32[16464]{0:T(1024)}, u32[]{:S(2)}) copy-start(f32[16464]{0:T(1024)} %param.17) | copy-start | bytes 197572
  0.7 82.8 %copy-start.4 = (f32[16464]{0:T(1024)S(1)}, f32[16464]{0:T(1024)}, u32[]{:S(2)}) copy-start(f32[16464]{0:T(1024)} %param.16) | copy-start | bytes 197572
  0.7 81.9 %copy-start.5 = (f32[1,8288]{1,0:T(1,128)S(1)}, f32[1,8288]{1,0:T(1,128)}, u32[]{:S(2)}) copy-start(f32[1,8288]{1,0:T(1,128)} %param.14) | copy-start | bytes 99460
  0.7 81.9 %copy-start.6 = (f32[1,8288]{1,0:T(1,128)S(1)}, f32[1,8288]{1,0:T(1,128)}, u32[]{:S(2)}) copy-start(f32[1,8288]{1,0:T(1,128)} %param.13) | copy-start | bytes 99460
  85.1 2.8 %copy-start = (f32[1568,256]{1,0:T(8,128)S(1)}, f32[1568,256]{1,0:T(8,128)}, u32[]{:S(2)}) copy-start(f32[1568,256]{1,0:T(8,128)} %get-tuple-element.19) | copy-start | bytes 4816900

commit v6 on v5

--- a/solution.py
+++ b/solution.py
@@ -294,7 +294,7 @@
 
 
 def head_masks(dtype):
-    lane = lax.broadcasted_iota(jnp.int32, (1, HALF), 1) // HD
+    lane = lax.broadcasted_iota(jnp.int32, (1, D), 1) % HALF // HD
     return [(lane == h).astype(f32).astype(dtype) for h in range(HEADS)]
 
 
@@ -303,40 +303,81 @@
 
 
 def pick_heads(stacked):
-    lane = lax.broadcasted_iota(jnp.int32, (STRIPE, HALF), 1)
+    lane = lax.broadcasted_iota(jnp.int32, (STRIPE, D), 1) % HALF
     picked = stacked[(HEADS - 1) * STRIPE :]
     for h in range(HEADS - 2, -1, -1):
         picked = jnp.where(lane < (h + 1) * HD, stacked[h * STRIPE : (h + 1) * STRIPE], picked)
     return picked
 
 
-def row_shift(values, step):
-    if step == 0:
+def beside(rows):
+    return jnp.concatenate([rows[:STRIPE], rows[STRIPE:]], axis=1)
+
+
+def above(columns):
+    return jnp.concatenate([columns[:, :HALF], columns[:, HALF:]], axis=0)
+
+
+def diagonal(rows):
+    gap = jnp.zeros((HALF - STRIPE, HALF), rows.dtype)
+    other = jnp.zeros((HALF, HALF), rows.dtype)
+    first = jnp.concatenate([rows[:STRIPE], gap], axis=0)
+    second = jnp.concatenate([rows[STRIPE:], gap], axis=0)
+    return jnp.concatenate(
+        [jnp.concatenate([first, other], axis=1), jnp.concatenate([other, second], axis=1)], axis=0
+    )
+
+
+def from_diagonal(square):
+    return jnp.concatenate(
+        [square[:STRIPE, :HALF], square[HALF : HALF + STRIPE, HALF:]], axis=1
+    )
+
+
+def row_shift(values, rows):
+    if rows == 0:
         return values
-    zero = jnp.zeros((16, HALF), f32)
-    if step > 0:
-        return jnp.concatenate([values[16:], zero], axis=0)
-    return jnp.concatenate([zero, values[:-16]], axis=0)
-
-
-def neighbours(values):
-    return [pltpu.roll(values, 1, 0), values, pltpu.roll(values, STRIPE - 1, 0)]
+    zero = jnp.zeros((abs(rows), values.shape[1]), f32)
+    if rows > 0:
+        return jnp.concatenate([values[rows:], zero], axis=0)
+    return jnp.concatenate([zero, values[:rows]], axis=0)
+
+
+def neighbours(values, j):
+    before, after = pltpu.roll(values, 1, 0), pltpu.roll(values, STRIPE - 1, 0)
+    if j == 0:
+        row = lax.broadcasted_iota(jnp.int32, values.shape, 0) % 16
+        before = jnp.where(row == 8, pltpu.roll(values, 2, 0), before)
+        after = jnp.where(row == 6, pltpu.roll(values, STRIPE - 2, 0), after)
+    return [before, values, after]
+
+
+SHIFT = (16, 8)
+
+
+def tap(j, outer, inner):
+    return 3 * outer + inner if j == 0 else 3 * inner + outer
+
+
+def to_stripes(rows):
+    tiles = rows.reshape(SIDE, 2, 8, rows.shape[1])
+    return jnp.concatenate(
+        [tiles[:, s].reshape(STRIPE, rows.shape[1]) for s in range(2)], axis=0
+    )
+
+
+def from_stripes(columns):
+    halves = [columns[:, s * HALF : (s + 1) * HALF].reshape(SIDE, 1, 8, HALF) for s in range(2)]
+    return jnp.concatenate(halves, axis=1).reshape(GRID, HALF)
 
 
 def tile_sum(values):
     return jnp.sum(values.reshape(-1, 8, values.shape[1]), axis=0)
 
 
-def turn_matrix():
-    to = lax.broadcasted_iota(jnp.int32, (GRID, GRID), 0)
-    src = lax.broadcasted_iota(jnp.int32, (GRID, GRID), 1)
-    first, second = to // 16, to % 16
-    return ((second < SIDE) & (src == second * 16 + first)).astype(f32).astype(bf16)
-
-
 def row_mask():
     row = lax.broadcasted_iota(jnp.int32, (GRID, 1), 0)
-    return (row % 16 < SIDE).astype(f32)
+    return (row % 8 < SW).astype(f32)
 
 
 def to_grid(source, tokens, grid_ref):
@@ -346,17 +387,17 @@
         cols = slice(half * 128, (half + 1) * 128)
         tokens[half] = source[:, cols].astype(f32)
         for image in range(images):
-            for r in range(SIDE):
-                grid_ref[image, 16 * r : 16 * r + SIDE, cols] = tokens[
-                    half, pl.ds(r * SIDE * images + image, SIDE, stride=images), :
+            for r in range(2 * SIDE):
+                grid_ref[image, 8 * r : 8 * r + SW, cols] = tokens[
+                    half, pl.ds(r * SW * images + image, SW, stride=images), :
                 ]
 
 
 def from_grid(value, tokens, image, images):
     for half in range(2):
-        for r in range(SIDE):
-            tokens[half, pl.ds(r * SIDE * images + image, SIDE, stride=images), :] = value[
-                16 * r : 16 * r + SIDE, half * 128 : (half + 1) * 128
+        for r in range(2 * SIDE):
+            tokens[half, pl.ds(r * SW * images + image, SW, stride=images), :] = value[
+                8 * r : 8 * r + SW, half * 128 : (half + 1) * 128
             ]
 
 
@@ -386,7 +427,9 @@
         sc["qbias"][:, j * 384 : j * 384 + 128] = gflat[j, 768:769, :]
         sc["qbias"][:, j * 384 + 128 : j * 384 + 256] = jnp.zeros((1, 128), f32)
         sc["qbias"][:, j * 384 + 256 : j * 384 + 384] = gflat[j, 769:770, :]
-        sc["conv"][j, 0:10] = gflat[j, 1026:1036, :]
+        for half in range(2):
+            cols = slice(half * 128, (half + 1) * 128)
+            sc["conv"][j, 0:10, cols] = gflat[j, 1026:1036, :]
 
 
 def prepare_shared(n_dp, stages, sc):
@@ -443,7 +486,8 @@
         gflat[j, 768:769, :] = sc["a_pb"][0:1, j * 384 : j * 384 + 128]
         gflat[j, 769:770, :] = sc["a_pb"][0:1, j * 384 + 256 : j * 384 + 384]
         for i in range(10):
-            gflat[j, 1026 + i : 1027 + i, :] = column_sum(sc["a_conv"][j, i])
+            both = column_sum(sc["a_conv"][j, i])
+            gflat[j, 1026 + i : 1027 + i, :] = both[:, :HALF] + both[:, HALF:]
     for c in range(2):
         cols = slice(c * 128, (c + 1) * 128)
         sc["carried"][4 + c : 5 + c, :] = column_sum(sc["a_vec"][1, :, cols])
@@ -460,45 +504,42 @@
     scale = HD ** (-0.5)
     masks = head_masks(bf16)
     inside = row_mask()
-    key_row = lax.broadcasted_iota(jnp.int32, (1, SW, 16, STRIPE), 2)
+    key_row = lax.broadcasted_iota(jnp.int32, (1, SIDE, 8, D), 2)
     gain_one, shift_one = sc["vecs"][1:2], sc["vecs"][2:3]
     qkv_ref, conv = sc["qkv"], sc["conv"]
+    many = len(images)
     for image in images:
         sc["normed"][image] = (sc["unit"][image] * gain_one + shift_one).astype(bf16)
-    for image in images:
-        triple = (nn(sc["normed"][image], sc["wq"][...]) + sc["qbias"][...]) * inside
-        triple = triple.astype(bf16)
-        qkv_ref[image, 0] = triple[:, :384]
-        qkv_ref[image, 1] = nn(sc["turn"][...], triple[:, 384:]).astype(bf16)
+    normed = sc["normed"][pl.ds(images[0], many)].reshape(many * GRID, D)
+    triples = nn(normed, sc["wq"][...]) + sc["qbias"][...]
+    for i, image in enumerate(images):
+        triple = triples[i * GRID : (i + 1) * GRID] * inside
+        qkv_ref[image, 0] = triple[:, :384].astype(bf16)
+        qkv_ref[image, 1] = to_stripes(triple[:, 384:]).astype(bf16)
     for j in range(2):
-        padded = [[] for _ in images]
-        for s in range(2):
-            for image, parts in zip(images, padded):
-                rows = slice(s * STRIPE, (s + 1) * STRIPE)
-                query = qkv_ref[image, j, rows, 0:128]
-                keys = spread_heads(qkv_ref[image, j, rows, 128:256], masks)
-                value = qkv_ref[image, j, rows, 256:384]
-                scores = nt(keys, query).reshape(HEADS, SW, 16, STRIPE) * scale
-                scores = jnp.where(key_row < SIDE, scores, -1e30)
-                scores = scores.reshape(HEADS, STRIPE, STRIPE)
-                weights = jnp.exp(scores - jnp.max(scores, axis=1, keepdims=True))
-                probs = weights * (1.0 / jnp.sum(weights, axis=1, keepdims=True))
-                probs = probs.reshape(HEADS * STRIPE, STRIPE)
-                sc["probs"][image, 2 * j + s] = probs
-                attended = tn(probs.astype(bf16), spread_heads(value, masks))
-                near = neighbours(value.astype(f32))
-                total = attended + conv[j, 9:10]
-                for a in range(3):
-                    part = near[0] * conv[j, 3 * a : 3 * a + 1]
-                    for b in range(1, 3):
-                        part = part + near[b] * conv[j, 3 * a + b : 3 * a + b + 1]
-                    total = total + row_shift(part, a - 1)
-                parts.append(total.astype(bf16))
-        for image, parts in zip(images, padded):
-            both = jnp.concatenate(parts, axis=0)
-            if j == 1:
-                both = nn(sc["turn"][...], both).astype(bf16)
-            sc["heads"][image, :, j * 128 : (j + 1) * 128] = both
+        for image in images:
+            query = diagonal(qkv_ref[image, j, :, 0:128])
+            keys = spread_heads(beside(qkv_ref[image, j, :, 128:256]), masks)
+            value = beside(qkv_ref[image, j, :, 256:384])
+            scores = nt(keys, query).reshape(HEADS, SIDE, 8, D) * scale
+            scores = jnp.where(key_row < SW, scores, -1e30)
+            scores = scores.reshape(HEADS, STRIPE, D)
+            weights = jnp.exp(scores - jnp.max(scores, axis=1, keepdims=True))
+            probs = weights * (1.0 / jnp.sum(weights, axis=1, keepdims=True))
+            probs = probs.reshape(HEADS * STRIPE, D)
+            sc["probs"][image, j] = probs
+            total = from_diagonal(tn(probs.astype(bf16), spread_heads(value, masks)))
+            total = total + conv[j, 9:10]
+            near = neighbours(value.astype(f32), j)
+            for outer in range(3):
+                part = None
+                for inner in range(3):
+                    k = tap(j, outer, inner)
+                    term = near[inner] * conv[j, k : k + 1]
+                    part = term if part is None else part + term
+                total = total + row_shift(part, SHIFT[j] * (outer - 1))
+            both = above(total) if j == 0 else from_stripes(total)
+            sc["heads"][image, :, j * 128 : (j + 1) * 128] = both.astype(bf16)
 
 
 def mlp_both(images, count, drop_ref, sc):
@@ -562,8 +603,11 @@
         grad_branch.append(grad_branch_f.astype(bf16))
     grad_branch = join(grad_branch)
     sc["a_ow"][...] += tn(heads, grad_branch)
-    grad_heads = nt(grad_branch, sc["ow"][...]).astype(bf16)
-    sc["gheads"][pl.ds(images[0], many)] = grad_heads.reshape(many, GRID, D)
+    grad_heads = nt(grad_branch, sc["ow"][...])
+    for i, image in enumerate(images):
+        grad = part_of(grad_heads, i)
+        sc["gheads"][image, :, :128] = grad[:, :128].astype(bf16)
+        sc["gheads"][image, :, 128:] = to_stripes(grad[:, 128:]).astype(bf16)
 
 
 def attention_back(images, count, sc):
@@ -571,61 +615,55 @@
     masks = head_masks(bf16)
     inside = row_mask()[:STRIPE]
     gain_one = sc["vecs"][1:2]
-    ones = jnp.ones((8, GRID), bf16)
+    many = len(images)
+    ones = jnp.ones((8, many * GRID), bf16)
     a_vec, a_conv = sc["a_vec"], sc["a_conv"]
     qkv_ref, conv = sc["qkv"], sc["conv"]
     for j in range(2):
-        if j == 0:
-            grads = [sc["gheads"][image, :, 0:128] for image in images]
-        else:
-            grads = [
-                nn(sc["turn"][...], sc["gheads"][image, :, 128:256]).astype(bf16)
-                for image in images
-            ]
-        padded = [[] for _ in images]
-        for s in range(2):
-            for image, parts, all_grad in zip(images, padded, grads):
-                rows = slice(s * STRIPE, (s + 1) * STRIPE)
-                query = qkv_ref[image, j, rows, 0:128]
-                keys = spread_heads(qkv_ref[image, j, rows, 128:256], masks)
-                value = qkv_ref[image, j, rows, 256:384]
-                grad = all_grad[rows]
-                grad_f = grad.astype(f32)
-                probs = sc["probs"][image, 2 * j + s]
-                grad_probs = nt(spread_heads(value, masks), grad)
-                product = (probs * grad_probs).reshape(HEADS, STRIPE, STRIPE)
-                inner = jnp.sum(product, axis=1, keepdims=True)
-                grad_scores = product - probs.reshape(HEADS, STRIPE, STRIPE) * inner
-                grad_scores = grad_scores.reshape(HEADS * STRIPE, STRIPE).astype(bf16)
-                grad_query = tn(grad_scores, keys) * scale
-                grad_key = pick_heads(nn(grad_scores, query)) * scale
-                grad_value = pick_heads(nn(probs.astype(bf16), grad))
-                near = neighbours(grad_f)
-                for a in range(3):
-                    part = near[2] * conv[j, 3 * a : 3 * a + 1]
-                    for b in range(1, 3):
-                        part = part + near[2 - b] * conv[j, 3 * a + b : 3 * a + b + 1]
-                    grad_value = grad_value + row_shift(part, 1 - a)
-                grad_value = grad_value * inside
-                near = neighbours(value.astype(f32))
-                for b in range(3):
-                    a_conv[j, b] += tile_sum(grad_f[16:] * near[b][:-16])
-                    a_conv[j, 3 + b] += tile_sum(grad_f * near[b])
-                    a_conv[j, 6 + b] += tile_sum(grad_f[:-16] * near[b][16:])
-                a_conv[j, 9] += tile_sum(grad_f)
-                parts.append(
-                    jnp.concatenate([grad_query, grad_key, grad_value], axis=1).astype(bf16)
-                )
-        for image, parts in zip(images, padded):
-            both = jnp.concatenate(parts, axis=0)
-            if j == 1:
-                both = nn(sc["turn"][...], both).astype(bf16)
+        for image in images:
+            grad = sc["gheads"][image, :, j * 128 : (j + 1) * 128]
+            grad_square = diagonal(grad)
+            grad_f = beside(grad).astype(f32)
+            query = diagonal(qkv_ref[image, j, :, 0:128])
+            keys = spread_heads(beside(qkv_ref[image, j, :, 128:256]), masks)
+            value = beside(qkv_ref[image, j, :, 256:384])
+            probs = sc["probs"][image, j]
+            grad_probs = nt(spread_heads(value, masks), grad_square)
+            product = (probs * grad_probs).reshape(HEADS, STRIPE, D)
+            inner = jnp.sum(product, axis=1, keepdims=True)
+            grad_scores = product - probs.reshape(HEADS, STRIPE, D) * inner
+            grad_scores = grad_scores.reshape(HEADS * STRIPE, D).astype(bf16)
+            grad_query = from_diagonal(tn(grad_scores, keys)) * scale
+            grad_key = pick_heads(nn(grad_scores, query)) * scale
+            grad_value = pick_heads(nn(probs.astype(bf16), grad_square))
+            near = neighbours(grad_f, j)
+            for outer in range(3):
+                part = None
+                for inner in range(3):
+                    k = tap(j, outer, inner)
+                    term = near[2 - inner] * conv[j, k : k + 1]
+                    part = term if part is None else part + term
+                grad_value = grad_value + row_shift(part, SHIFT[j] * (1 - outer))
+            grad_value = grad_value * inside
+            near = neighbours(value.astype(f32), j)
+            step = SHIFT[j]
+            for inner in range(3):
+                a_conv[j, tap(j, 0, inner)] += tile_sum(grad_f[step:] * near[inner][:-step])
+                a_conv[j, tap(j, 1, inner)] += tile_sum(grad_f * near[inner])
+                a_conv[j, tap(j, 2, inner)] += tile_sum(grad_f[:-step] * near[inner][step:])
+            a_conv[j, 9] += tile_sum(grad_f)
+            order = above if j == 0 else from_stripes
+            both = jnp.concatenate(
+                [order(part) for part in (grad_query, grad_key, grad_value)], axis=1
+            ).astype(bf16)
             sc["gtriple"][image, :, j * 384 : (j + 1) * 384] = both
-    for image in images:
-        grad_triple = sc["gtriple"][image]
-        sc["a_pb"][...] += nn(ones, grad_triple)
-        sc["a_wq"][...] += tn(sc["normed"][image], grad_triple)
-        grad_normed = nt(grad_triple, sc["wq"][...])
+    grad_triple = sc["gtriple"][pl.ds(images[0], many)].reshape(many * GRID, 768)
+    normed = sc["normed"][pl.ds(images[0], many)].reshape(many * GRID, D)
+    sc["a_pb"][...] += nn(ones, grad_triple)
+    sc["a_wq"][...] += tn(normed, grad_triple)
+    grads = nt(grad_triple, sc["wq"][...])
+    for i, image in enumerate(images):
+        grad_normed = grads[i * GRID : (i + 1) * GRID]
         unit, inverse = sc["unit"][image], sc["inverse"][image]
         a_vec[1] += tile_sum(grad_normed * unit)
         a_vec[2] += tile_sum(grad_normed)
@@ -643,8 +681,8 @@
         sweights=((n, srows, 128), bf16),
         gweights=((n, grows, 128), bf16),
         raw=((grows, 128), f32),
+        sraw=((srows, 128), f32),
         carried=((8, 128), f32),
-        turn=((GRID, GRID), bf16),
         wq=((D, 768), bf16),
         ow=((D, D), bf16),
         uw=((D, FF), bf16),
@@ -652,7 +690,7 @@
         qbias=((1, 768), f32),
         ubias=((1, FF), f32),
         vecs=((8, D), f32),
-        conv=((2, 16, 128), f32),
+        conv=((2, 16, D), f32),
         a_wq=((D, 768), f32),
         a_ow=((D, D), f32),
         a_uw=((D, FF), f32),
@@ -660,7 +698,7 @@
         a_pb=((8, 768), f32),
         a_ub=((8, FF), f32),
         a_vec=((6, 8, D), f32),
-        a_conv=((2, 10, 8, 128), f32),
+        a_conv=((2, 10, 8, D), f32),
         x_in=((TOK * count, D), bf16),
         co_in=((TOK * count, D), bf16),
         tokens=((2, TOK * count, 128), f32),
@@ -671,7 +709,7 @@
         inverse=((count, GRID, 1), f32),
         normed=((count, GRID, D), bf16),
         qkv=((count, 2, GRID, 384), bf16),
-        probs=((count, 4, HEADS * STRIPE, STRIPE), f32),
+        probs=((count, 2, HEADS * STRIPE, D), f32),
         heads=((count, GRID, D), bf16),
         gmid=((count, GRID, D), f32),
         gheads=((count, GRID, D), bf16),
@@ -708,11 +746,19 @@
 def own_windows(n_dp, sown_ref, gown_ref, soff, goff, stages, sc):
     n = 2 * n_dp
     mine = sum((1 << t) * bit for t, bit in enumerate(own_bits(stages)))
-    window = shift_on(sown_ref[...], soff)
+    raw = sc["sraw"]
+    share = sown_ref.shape[0]
+    whole = share // UNIT * UNIT
+    raw[...] = jnp.zeros_like(raw)
+    raw[0 : whole // 128, :] = sown_ref[0:whole].reshape(whole // 128, 128)
+    for r in range(whole // 128, -(-share // 128)):
+        size = min(128, share - 128 * r)
+        raw[r : r + 1, 0:size] = sown_ref[128 * r : 128 * r + size].reshape(1, size)
+    window = shift_on(raw[...], soff)
     sc["sweights"][mine] = window.astype(bf16)
     raw = sc["raw"]
     grows = raw.shape[0]
-    share = GROUP_PARAMS // n_dp
+    share = gown_ref.shape[1]
     raw[...] = jnp.zeros_like(raw)
     for r in range(-(-share // 128)):
         size = min(128, share - 128 * r)
@@ -750,7 +796,10 @@
     threshold = math.sqrt(2 * GROUP_PARAMS + SHARED_PARAMS)
     factor = jnp.minimum(1.0, threshold / (norm + 1e-06))
     smine_ref[...] = shift_back(shared * factor, soff)
-    gmine_ref[...] = shift_back(grouped * factor, goff)
+    grouped = shift_back(grouped * factor, goff)
+    for r in range(-(-gshare // 128)):
+        size = min(128, gshare - 128 * r)
+        gmine_ref[0:1, 128 * r : 128 * r + size] = grouped[r : r + 1, 0:size]
 
 
 def step_kernel(
@@ -784,7 +833,6 @@
     soff = (own_number() * (SHARED_PARAMS // n)) % UNIT
     goff = (lax.axis_index("dp") * (GROUP_PARAMS // n_dp)) % UNIT
     own_windows(n_dp, sown_ref, gown_ref, soff, goff, stages, sc)
-    sc["turn"][...] = turn_matrix()
     load_x.wait()
     to_grid(sc["x_in"], sc["tokens"], sc["x"])
     pl.semaphore_wait(barrier, len(devices))
@@ -921,9 +969,10 @@
     return run_all
 
 
-def step(n_dp, drops, images, cotangent, sown, gown):
+def step(n_dp, drops, images, cotangent, state):
     count = images.shape[0]
-    srows = sown.shape[0]
+    gown, _, _, sown, _, _ = state
+    srows = window_rows(SHARED_PARAMS, 2 * n_dp)
     grows = window_rows(GROUP_PARAMS, n_dp, CARRIED)
     shapes = scratch_shapes(n_dp, srows, grows, count)
     vmem = pl.BlockSpec(memory_space=pltpu.VMEM)
@@ -942,7 +991,7 @@
         out_shape=[jax.ShapeDtypeStruct((TOK * count, D), f32)] * 2
         + [
             jax.ShapeDtypeStruct((srows, 128), f32),
-            jax.ShapeDtypeStruct((grows, 128), f32),
+            jax.ShapeDtypeStruct(gown.shape, f32),
             jax.ShapeDtypeStruct((8, 128), f32),
         ],
         scratch_shapes=list(shapes.values()),
@@ -951,18 +1000,76 @@
         ),
         name="step",
     )(drops.T, rows(images), rows(cotangent), sown, gown)
-    return unrows(out), unrows(gin), smine, gmine, norm
-
-
-def adam_step(master, gradient, first, second, step):
+    first, second, *updated = update(out, gin, smine.reshape(-1), gmine, norm, *state)
+    return (unrows(first), unrows(second), *updated)
+
+
+def adam_step(master, gradient, first, second):
     first_new = beta_one * first + (1.0 - beta_one) * gradient
     second_new = beta_two * second + (1.0 - beta_two) * gradient * gradient
-    first_hat = first_new / (1.0 - jnp.power(jnp.float32(beta_one), step))
-    second_hat = second_new / (1.0 - jnp.power(jnp.float32(beta_two), step))
+    first_hat = first_new / (1.0 - beta_one**STEP)
+    second_hat = second_new / (1.0 - beta_two**STEP)
     master_new = master - learn_rate * (
         first_hat / (jnp.sqrt(second_hat) + adam_eps) + decay_rate * master
     )
     return (master_new, first_new, second_new)
+
+
+CHUNKS = 4
+
+
+def update_kernel(out_in, gin_in, smine, gmine, norm_in, *refs):
+    gstate, sstate, refs = refs[:3], refs[3:6], refs[6:]
+    out_ref, gin_ref, norm_ref = refs[:3]
+    gnew, snew, (out_buf, gin_buf, in_sem, out_sem) = refs[3:8], refs[8:13], refs[13:]
+    size = out_in.shape[0] // CHUNKS
+    arrays = ((out_in, out_buf, out_ref), (gin_in, gin_buf, gin_ref))
+    loads, stores = [], []
+    for i in range(CHUNKS):
+        rows = pl.ds(i * size, size)
+        for k, (source, held, target) in enumerate(arrays):
+            loads.append(
+                pltpu.make_async_copy(source.at[rows], held.at[rows], in_sem.at[k, i])
+            )
+            stores.append(
+                pltpu.make_async_copy(held.at[rows], target.at[rows], out_sem.at[k, i])
+            )
+            loads[-1].start()
+    for load, store in zip(loads, stores):
+        load.wait()
+        store.start()
+    norm_ref[...] = norm_in[0:1, 0:1]
+    for gradient, (master, first, second), new in (
+        (gmine[...], gstate, gnew),
+        (smine[0 : sstate[0].shape[0]], sstate, snew),
+    ):
+        new[0][...] = gradient
+        new[1][...], new[2][...], new[3][...] = adam_step(
+            master[...], gradient, first[...], second[...]
+        )
+        new[4][...] = new[1][...].astype(bf16)
+    for store in stores:
+        store.wait()
+
+
+def update(out, gin, smine, gmine, norm, *state):
+    vmem = pl.BlockSpec(memory_space=pltpu.VMEM)
+    anywhere = pl.BlockSpec(memory_space=pl.ANY)
+    like = jax.ShapeDtypeStruct
+    big = like(out.shape, f32)
+    news = []
+    for master in (state[0], state[3]):
+        news += [like(master.shape, f32)] * 4 + [like(master.shape, bf16)]
+    return pl.pallas_call(
+        update_kernel,
+        in_specs=[anywhere] * 2 + [vmem] * 9,
+        out_specs=[anywhere] * 2 + [vmem] * 11,
+        out_shape=[big, big, like((1, 1), f32)] + news,
+        scratch_shapes=[pltpu.VMEM(out.shape, f32)] * 2
+        + [pltpu.SemaphoreType.DMA((2, CHUNKS))] * 2,
+        compiler_params=pltpu.CompilerParams(vmem_limit_bytes=62 * 1024 * 1024),
+        name="update",
+    )(out, gin, smine, gmine, norm, *state)
 
 
 def on_device(
@@ -977,37 +1084,9 @@
     shared_m1,
     shared_m2,
 ):
-    n = 2 * n_dp
-    srows = window_rows(SHARED_PARAMS, n)
-    sshare, gshare = SHARED_PARAMS // n, GROUP_PARAMS // n_dp
-    sown = jnp.pad(shared_master, (0, srows * 128 - sshare)).reshape(srows, 128)
-    output, input_grad, smine, gmine, norm = step(
-        n_dp, drop_masks, images, cotangent, sown, group_master
-    )
-    shared_grad = smine.reshape(-1)[:sshare]
-    group_grad = gmine.reshape(-1)[:gshare][None, :]
-    now = jnp.float32(STEP)
-    group_new, group_first, group_second = adam_step(
-        group_master, group_grad, group_m1, group_m2, now
-    )
-    shared_new, shared_first, shared_second = adam_step(
-        shared_master, shared_grad, shared_m1, shared_m2, now
-    )
-    return (
-        output,
-        input_grad,
-        norm[0, 0:1],
-        group_grad,
-        group_new,
-        group_first,
-        group_second,
-        group_new.astype(jnp.bfloat16),
-        shared_grad,
-        shared_new,
-        shared_first,
-        shared_second,
-        shared_new.astype(jnp.bfloat16),
-    )
+    state = (group_master, group_m1, group_m2, shared_master, shared_m1, shared_m2)
+    output, input_grad, norm, *updated = step(n_dp, drop_masks, images, cotangent, state)
+    return (output, input_grad, norm.reshape(1), *updated)
 
 
 def solution(mesh):

time: 89.4 us -> 79.7 us (0.89)
  local copies, waits for them, and re-layouts: 7.42 us -> 0 us
  other arithmetic: 3.25 us -> 0 us
  Pallas kernels: 77.6 us -> 78.8 us
    pallas_call x0 -> x1, Pallas kernels: none -> 4.63 us  [update(): pl.pallas_call(update_kernel, in_specs=[anywhere] * 2 + [vmem] * 9, out_s...]
    unnamed x16 -> x0, local copies, waits for them, and re-layouts: 3.98 us -> none
    pallas_call x1, Pallas kernels: 77.6 us -> 74.2 us  [step(): pl.pallas_call(partial(step_kernel, n_dp, count, tuple(shapes)), in_specs...]
    convert_element_type x2 -> x0, other arithmetic: 2.48 us -> none  [the longest x1 1.61 us: on_device(): shared_new.astype(jnp.bfloat16)]
    reshape x1 -> x0, local copies, waits for them, and re-layouts: 1.61 us -> none  [on_device(): sown = jnp.pad(shared_master, (0, srows * 128 - sshare)).reshape(srows, 128)]
    slice x1 -> x0, local copies, waits for them, and re-layouts: 1.19 us -> none  [on_device(): norm[0, 0:1]]
where the time goes in v6:
time: 79.7 us; the launch traced here: 79.5 us
  Pallas kernels  78.8 us (99%)
    pallas_call x1, Pallas kernels, step(): pl.pallas_call(partial(step_kernel, n_dp, count, tuple(shapes)), in_specs...  74.2 us
    pallas_call x1, Pallas kernels, update(): pl.pallas_call(update_kernel, in_specs=[anywhere] * 2 + [vmem] * 9, out_s...  4.63 us

profile of v6, /device:TPU:0, one launch (start us, length us, event | category | flops | bytes accessed | tf_op | source)
XLA Modules:
  0.0 79.5 jit_solution(3080985389791555798)
XLA Ops:
  0.6 74.2 %step.1 = (f32[1568,256]{1,0:T(8,128)}, f32[1568,256]{1,0:T(8,128)}, f32[144,128]{1,0:T(8,128)}, f32[1,8288]{1,0:T(1,128)}, f32[8,128]{1,0:T(8,128)}) custom-call(s32[2,8]{1,0:T(2,128)} %bitcast.18, bf16[1568,256]{1,0:T(8,128)(2,1)} %bitcast.15, bf16[1568,256]{1,0:T(8,128)(2,1)} %bitcast.16, f32[16464]{0:T(1024)} %refs_3_.1, f32[1,8288]{1,0:T(1,128)} %refs_0_.1), custom_call_target="tpu_custom_call" | custom-call | tf_op jit(solution)/shard_map/step/pallas_call | solution.py:987
  74.8 4.6 %update.1 = (f32[1568,256]{1,0:T(8,128)}, f32[1568,256]{1,0:T(8,128)}, f32[1,1]{1,0:T(1,128)}, f32[1,8288]{1,0:T(1,128)}, f32[1,8288]{1,0:T(1,128)}, /*index=5*/...) custom-call(f32[1568,256]{1,0:T(8,128)} %get-tuple-element.31.out_in, ...), custom_call_target="tpu_custom_call" | custom-call | tf_op jit(solution)/shard_map/update/pallas_call | solution.py:1063

commit v7 on v6

--- a/solution.py
+++ b/solution.py
@@ -118,38 +118,37 @@
     return (me, near), (high, far)
 
 
+UNROLL = 4
+
+
 class Gather:
     def __init__(self, stages, buffer, send_sem, recv_sem):
         self.stages, self.buffer = stages, buffer
         self.send_sem, self.recv_sem = send_sem, recv_sem
         self.bits = own_bits(stages)
 
-    def copies(self, g, arriving):
+    def copy(self, g, held, mask):
+        return pltpu.make_async_remote_copy(
+            src_ref=held,
+            dst_ref=held,
+            send_sem=self.send_sem.at[g],
+            recv_sem=self.recv_sem.at[g],
+            device_id=peer(self.stages[g], mask),
+        )
+
+    def start(self, g):
         start = sum(len(stage) for stage in self.stages[:g])
+        base = sum((1 << u) * bit for u, bit in enumerate(self.bits) if u >= start)
+        held = self.buffer.at[pl.ds(base, 1 << start)]
         for mask in range(1, 1 << len(self.stages[g])):
-            base = 0
-            for u, bit in enumerate(self.bits):
-                flipped = start <= u < start + len(self.stages[g]) and mask >> (u - start) & 1
-                if u >= start:
-                    base = base + (1 << u) * (1 - bit if flipped and arriving else bit)
-            held = self.buffer.at[pl.ds(base, 1 << start)]
-            yield pltpu.make_async_remote_copy(
-                src_ref=held,
-                dst_ref=held,
-                send_sem=self.send_sem.at[g, mask - 1],
-                recv_sem=self.recv_sem.at[g, mask - 1],
-                device_id=peer(self.stages[g], mask),
-            )
-
-    def start(self, g):
-        for copy in self.copies(g, False):
-            copy.start()
+            self.copy(g, held, mask).start()
 
     def wait(self, g):
-        for copy in self.copies(g, True):
-            copy.wait_recv()
-        for copy in self.copies(g, False):
-            copy.wait_send()
+        start = sum(len(stage) for stage in self.stages[:g])
+        peers = (1 << len(self.stages[g])) - 1
+        every = self.copy(g, self.buffer.at[pl.ds(0, peers << start)], 1)
+        every.wait_recv()
+        every.wait_send()
 
 
 class Scatter:
@@ -167,12 +166,12 @@
             return self.window(place)
         return self.sums[g + 1][place]
 
-    def copy(self, g, mask):
+    def copy(self, g, mask, at):
         return pltpu.make_async_remote_copy(
-            src_ref=self.outgoing[g].at[mask - 1],
-            dst_ref=self.incoming[g].at[mask - 1],
-            send_sem=self.send_sem.at[g, mask - 1],
-            recv_sem=self.recv_sem.at[g, mask - 1],
+            src_ref=self.outgoing[g].at[at],
+            dst_ref=self.incoming[g].at[at],
+            send_sem=self.send_sem.at[g],
+            recv_sem=self.recv_sem.at[g],
             device_id=peer(self.stages[g], mask),
         )
 
@@ -191,13 +190,13 @@
                 self.outgoing[g][mask - 1, i] = self.held(g, part + i).astype(bf16)
                 return carry
 
-            lax.fori_loop(0, 1 << self.offset(g), fill, 0)
-            self.copy(g, mask).start()
+            blocks = 1 << self.offset(g)
+            lax.fori_loop(0, blocks, fill, 0, unroll=min(blocks, UNROLL))
+            self.copy(g, mask, mask - 1).start()
 
     def wait(self, g):
         masks = range(1, 1 << len(self.stages[g]))
-        for mask in masks:
-            self.copy(g, mask).wait()
+        self.copy(g, 1, pl.ds(0, len(masks))).wait()
         part = self.part(g, 0)
 
         def add(i, carry):
@@ -207,7 +206,8 @@
             self.sums[g][i] = value
             return carry
 
-        lax.fori_loop(0, 1 << self.offset(g), add, 0)
+        blocks = 1 << self.offset(g)
+        lax.fori_loop(0, blocks, add, 0, unroll=min(blocks, UNROLL))
 
 
 def scatter_shapes(stages, rows):
@@ -221,27 +221,21 @@
 
 
 def all_share(me, peers, stat_ref, send_sem, recv_sem):
-    copies = []
-    for other, device in peers:
-        copy = pltpu.make_async_remote_copy(
-            src_ref=stat_ref.at[me],
-            dst_ref=stat_ref.at[me],
-            send_sem=send_sem.at[other],
-            recv_sem=recv_sem.at[me],
+    def copy(held, device):
+        return pltpu.make_async_remote_copy(
+            src_ref=held,
+            dst_ref=held,
+            send_sem=send_sem.at[0],
+            recv_sem=recv_sem.at[0],
             device_id=device,
         )
-        copy.start()
-        copies.append(copy)
-    for other, device in peers:
-        pltpu.make_async_remote_copy(
-            src_ref=stat_ref.at[other],
-            dst_ref=stat_ref.at[other],
-            send_sem=send_sem.at[other],
-            recv_sem=recv_sem.at[other],
-            device_id=device,
-        ).wait_recv()
-    for copy in copies:
-        copy.wait_send()
+
+    for _, device in peers:
+        copy(stat_ref.at[me], device).start()
+    if peers:
+        every = copy(stat_ref.at[pl.ds(0, len(peers))], peers[0][1])
+        every.wait_recv()
+        every.wait_send()
     return jnp.sum(stat_ref[...], axis=0)
 
 
@@ -488,11 +482,6 @@
         for i in range(10):
             both = column_sum(sc["a_conv"][j, i])
             gflat[j, 1026 + i : 1027 + i, :] = both[:, :HALF] + both[:, HALF:]
-    for c in range(2):
-        cols = slice(c * 128, (c + 1) * 128)
-        sc["carried"][4 + c : 5 + c, :] = column_sum(sc["a_vec"][1, :, cols])
-        sc["carried"][6 + c : 7 + c, :] = column_sum(sc["a_vec"][2, :, cols])
-    sc["carried"][0:4, :] = jnp.zeros((4, 128), f32)
 
 
 def first_norm(images, sc):
@@ -542,8 +531,17 @@
             sc["heads"][image, :, j * 128 : (j + 1) * 128] = both.astype(bf16)
 
 
-def mlp_both(images, count, drop_ref, sc):
-    down_bias = sc["vecs"][0:1]
+def mlp_output(images, count, drop_ref, sc):
+    many = len(images)
+    active = sc["active"][pl.ds(images[0], many)].reshape(many * GRID, FF)
+    mlp = nn(active, sc["dw"][...]) + sc["vecs"][0:1]
+    for i, image in enumerate(images):
+        scale_two = drop_ref[1, image].astype(f32) / keep_prob
+        value = sc["x"][image] + scale_two * mlp[i * GRID : (i + 1) * GRID]
+        from_grid(value, sc["outs"], image, count)
+
+
+def mlp_both(images, drop_ref, sc):
     gain_two, shift_two, out_bias = sc["vecs"][3:4], sc["vecs"][4:5], sc["vecs"][5:6]
     a_vec = sc["a_vec"]
     uw, dw, ubias = sc["uw"], sc["dw"], sc["ubias"]
@@ -570,7 +568,6 @@
         state.append((scale_one, scale_two, middle, unit_two, inverse_two, grad_output, grad_mlp_f))
     normed_two = join([(st[3] * gain_two + shift_two).astype(bf16) for st in state])
     grad_mlp = join([st[6].astype(bf16) for st in state])
-    mlp = None
     grad_normed = None
     for c in range(4):
         cols = slice(c * 256, (c + 1) * 256)
@@ -578,8 +575,7 @@
         density = jnp.exp(hidden * hidden * -0.5) * (1.0 / math.sqrt(2.0 * math.pi))
         phi = 0.5 + 0.5 * lax.erf(hidden * math.sqrt(0.5))
         active = (hidden * phi).astype(bf16)
-        part = nn(active, dw[cols, :])
-        mlp = part if mlp is None else mlp + part
+        sc["active"][pl.ds(images[0], many), :, cols] = active.reshape(many, GRID, 256)
         sc["a_dwt"][:, cols] += tn(grad_mlp, active)
         grad_active = nt(grad_mlp, dw[cols, :])
         grad_hidden = (grad_active * (phi + hidden * density)).astype(bf16)
@@ -589,10 +585,8 @@
         grad_normed = part if grad_normed is None else grad_normed + part
     grad_branch = []
     for i, image in enumerate(images):
-        scale_one, scale_two, middle, unit_two, inverse_two, grad_output, _ = state[i]
-        from_grid(
-            middle + scale_two * (part_of(mlp, i) + down_bias), sc["outs"], image, count
-        )
+        scale_one, _, middle, unit_two, inverse_two, grad_output, _ = state[i]
+        sc["x"][image] = middle
         grad = part_of(grad_normed, i)
         a_vec[3] += tile_sum(grad * unit_two)
         a_vec[4] += tile_sum(grad)
@@ -610,14 +604,13 @@
         sc["gheads"][image, :, 128:] = to_stripes(grad[:, 128:]).astype(bf16)
 
 
-def attention_back(images, count, sc):
+def attention_back(images, sc):
     scale = HD ** (-0.5)
     masks = head_masks(bf16)
     inside = row_mask()[:STRIPE]
-    gain_one = sc["vecs"][1:2]
     many = len(images)
     ones = jnp.ones((8, many * GRID), bf16)
-    a_vec, a_conv = sc["a_vec"], sc["a_conv"]
+    a_conv = sc["a_conv"]
     qkv_ref, conv = sc["qkv"], sc["conv"]
     for j in range(2):
         for image in images:
@@ -661,6 +654,13 @@
     normed = sc["normed"][pl.ds(images[0], many)].reshape(many * GRID, D)
     sc["a_pb"][...] += nn(ones, grad_triple)
     sc["a_wq"][...] += tn(normed, grad_triple)
+
+
+def input_gradient(images, count, sc):
+    many = len(images)
+    gain_one = sc["vecs"][1:2]
+    a_vec = sc["a_vec"]
+    grad_triple = sc["gtriple"][pl.ds(images[0], many)].reshape(many * GRID, 768)
     grads = nt(grad_triple, sc["wq"][...])
     for i, image in enumerate(images):
         grad_normed = grads[i * GRID : (i + 1) * GRID]
@@ -682,7 +682,8 @@
         gweights=((n, grows, 128), bf16),
         raw=((grows, 128), f32),
         sraw=((srows, 128), f32),
-        carried=((8, 128), f32),
+        sown=((SHARED_PARAMS // n,), f32),
+        gown=((1, GROUP_PARAMS // n_dp), f32),
         wq=((D, 768), bf16),
         ow=((D, D), bf16),
         uw=((D, FF), bf16),
@@ -700,7 +701,6 @@
         a_vec=((6, 8, D), f32),
         a_conv=((2, 10, 8, D), f32),
         x_in=((TOK * count, D), bf16),
-        co_in=((TOK * count, D), bf16),
         tokens=((2, TOK * count, 128), f32),
         outs=((2, TOK * count, 128), f32),
         x=((count, GRID, D), f32),
@@ -712,6 +712,7 @@
         probs=((count, 2, HEADS * STRIPE, D), f32),
         heads=((count, GRID, D), bf16),
         gmid=((count, GRID, D), f32),
+        active=((count, GRID, FF), bf16),
         gheads=((count, GRID, D), bf16),
         gtriple=((count, GRID, 768), bf16),
     )
@@ -728,12 +729,13 @@
     made = {name: pltpu.VMEM(*shape) for name, shape in shapes.items()}
     dma = pltpu.SemaphoreType.DMA
     for name in ("sgather", "ggather", "sscatter", "gscatter"):
-        made[name + "_send"] = dma((len(stages), 3))
-        made[name + "_recv"] = dma((len(stages), 3))
-    for name, size in (("near", 2 * fast), ("far", n_dp // fast)):
-        made[name + "_send"] = dma((size,))
-        made[name + "_recv"] = dma((size,))
-    made["local"] = dma((4,))
+        made[name + "_send"] = dma((len(stages),))
+        made[name + "_recv"] = dma((len(stages),))
+    for name in ("near", "far"):
+        made[name + "_send"] = dma((1,))
+        made[name + "_recv"] = dma((1,))
+    made["local"] = dma((5,))
+    made["drops"] = pltpu.SMEM((2, count), jnp.int32)
     return made
 
 
@@ -741,6 +743,9 @@
 TOGETHER = 2
 MLP_TOGETHER = 4
 GATHER_STEP = 2
+CORE_STEP = 1
+OUT_STEP = 3
+OUT_TOGETHER = 2
 
 
 def own_windows(n_dp, sown_ref, gown_ref, soff, goff, stages, sc):
@@ -776,21 +781,28 @@
     place = lax.broadcasted_iota(jnp.int32, (srows, 128), 0) * 128
     place = place + lax.broadcasted_iota(jnp.int32, (srows, 128), 1)
     shared = jnp.where((place >= soff) & (place < soff + sshare), ssum, 0.0)
-    last = jnp.where(own_number() == n - 1, 1.0, 0.0)
-    at = GAIN_ROW - first_row(SHARED_PARAMS, n, n - 1)
-    smine_ref[...] = shared
-    smine_ref[at : at + CARRIED, :] += gsum[grows - CARRIED :] * last
-    shared = smine_ref[...]
     place = lax.broadcasted_iota(jnp.int32, (grows, 128), 0) * 128
     place = place + lax.broadcasted_iota(jnp.int32, (grows, 128), 1)
     grouped = jnp.where((place >= goff) & (place < goff + gshare), gsum, 0.0)
     near_me, near_peers = near
     far_me, far_peers = far
-    sc["near_stat"][near_me] = tile_sum(shared * shared) + tile_sum(grouped * grouped)
-    total = all_share(near_me, near_peers, sc["near_stat"], sc["near_send"], sc["near_recv"])
-    sc["far_stat"][far_me] = total
-    total = all_share(far_me, far_peers, sc["far_stat"], sc["far_send"], sc["far_recv"])
-    total = jnp.sum(jnp.sum(total, axis=0, keepdims=True), axis=1, keepdims=True)
+    squares = column_sum(tile_sum(shared * shared) + tile_sum(grouped * grouped))
+    sums = [
+        column_sum(sc["a_vec"][i, :, c * 128 : (c + 1) * 128]) for i in (1, 2) for c in range(2)
+    ]
+    tile = jnp.concatenate([*sums, squares, jnp.zeros((3, 128), f32)], axis=0)
+    sc["near_stat"][near_me] = tile
+    tile = all_share(near_me, near_peers, sc["near_stat"], sc["near_send"], sc["near_recv"])
+    sc["far_stat"][far_me] = tile
+    tile = all_share(far_me, far_peers, sc["far_stat"], sc["far_send"], sc["far_recv"])
+    carried = tile[:CARRIED]
+    total = column_sum(carried * carried) + tile[CARRIED : CARRIED + 1]
+    total = jnp.sum(total, axis=1, keepdims=True)
+    last = jnp.where(own_number() == n - 1, 1.0, 0.0)
+    at = GAIN_ROW - first_row(SHARED_PARAMS, n, n - 1)
+    smine_ref[...] = shared
+    smine_ref[at : at + CARRIED, :] += carried * last
+    shared = smine_ref[...]
     norm = jnp.sqrt(total)
     norm_ref[...] = jnp.broadcast_to(norm, (8, 128))
     threshold = math.sqrt(2 * GROUP_PARAMS + SHARED_PARAMS)
@@ -806,7 +818,7 @@
     n_dp,
     count,
     names,
-    drop_ref,
+    drop_in,
     x_ref,
     co_ref,
     sown_ref,
@@ -827,14 +839,24 @@
     for device in devices:
         pl.semaphore_signal(barrier, inc=1, device_id=device)
     load_x = pltpu.make_async_copy(x_ref, sc["x_in"], sc["local"].at[0])
-    load_co = pltpu.make_async_copy(co_ref, sc["co_in"], sc["local"].at[1])
-    load_x.start()
-    load_co.start()
+    load_co = pltpu.make_async_copy(co_ref, sc["x_in"], sc["local"].at[1])
+    loads = [
+        pltpu.make_async_copy(source, sc[name], sc["local"].at[2 + i])
+        for i, (source, name) in enumerate(
+            ((sown_ref, "sown"), (gown_ref, "gown"), (drop_in, "drops"))
+        )
+    ]
+    for load in (*loads, load_x):
+        load.start()
+    drop_ref = sc["drops"]
     soff = (own_number() * (SHARED_PARAMS // n)) % UNIT
     goff = (lax.axis_index("dp") * (GROUP_PARAMS // n_dp)) % UNIT
-    own_windows(n_dp, sown_ref, gown_ref, soff, goff, stages, sc)
+    for load in loads:
+        load.wait()
+    own_windows(n_dp, sc["sown"], sc["gown"], soff, goff, stages, sc)
     load_x.wait()
     to_grid(sc["x_in"], sc["tokens"], sc["x"])
+    load_co.start()
     pl.semaphore_wait(barrier, len(devices))
     ggather = Gather(stages, sc["gweights"], sc["ggather_send"], sc["ggather_recv"])
     sgather = Gather(stages, sc["sweights"], sc["sgather_send"], sc["sgather_recv"])
@@ -863,7 +885,7 @@
     for name in ACCUMULATORS:
         sc[name][...] = jnp.zeros_like(sc[name])
     load_co.wait()
-    to_grid(sc["co_in"], sc["tokens"], sc["co"])
+    to_grid(sc["x_in"], sc["tokens"], sc["co"])
     ggather.wait(last)
     prepare_group(n_dp, stages, sc)
 
@@ -876,18 +898,9 @@
     run(lambda images: attention_forward(images, sc), {min(GATHER_STEP, steps - 1): spread_cores})
     sgather.wait(last)
     prepare_shared(n_dp, stages, sc)
-    run(lambda images: mlp_both(images, count, drop_ref, sc), None, MLP_TOGETHER)
-    stores = []
-    for half in range(2):
-        cols = slice(half * 128, (half + 1) * 128)
-        stores.append(
-            pltpu.make_async_copy(sc["outs"].at[half], out_ref.at[:, cols], sc["local"].at[half])
-        )
-        stores[-1].start()
+    run(lambda images: mlp_both(images, drop_ref, sc), None, MLP_TOGETHER)
     place_shared(sc)
 
-    half_bits = len(flat_bits(stages)) - 1
-    top = own_bits(stages)[half_bits]
     srows, grows = sc["sweights"].shape[1], sc["gweights"].shape[1]
 
     def swindow(place):
@@ -895,19 +908,10 @@
         row = (k * (SHARED_PARAMS // n)) // UNIT * 8
         return sc["flat"][pl.ds(pl.multiple_of(row, 8), srows), :]
 
-    upper = (lax.broadcasted_iota(jnp.int32, (8, 128), 0) < 8 - CARRIED).astype(f32)
-
     def gwindow(place):
         k = device_at(stages, place)
         row = ((k // 2) * (GROUP_PARAMS // n_dp)) // UNIT * 8
-        return jnp.concatenate(
-            [
-                sc["gflat"][k % 2, pl.ds(pl.multiple_of(row, 8), grows - 8), :],
-                sc["gflat"][k % 2, pl.ds(pl.multiple_of(row + grows - 8, 8), 8), :] * upper
-                + sc["carried"][...],
-            ],
-            axis=0,
-        )
+        return sc["gflat"][k % 2, pl.ds(pl.multiple_of(row, 8), grows), :]
 
     def scatter(name, window):
         parts = [[sc[f"{name}{kind}{g}"] for g in range(last + 1)] for kind in ("out", "in", "sum")]
@@ -918,32 +922,45 @@
     sscatter = scatter("s", swindow)
     gscatter = scatter("g", gwindow)
     sscatter.start(last)
-    for g in range(last, 0, -1):
-        def advance(g=g):
-            sscatter.wait(g)
-            sscatter.start(g - 1)
-
-        at = min(1 + 2 * (last - g), steps - 1)
-        backward[at] = backward.get(at, []) + [advance]
+    def advance(scatter, g):
+        def action():
+            scatter.wait(g)
+            scatter.start(g - 1)
+
+        return action
+
+    backward[min(1, steps - 1)] = [advance(sscatter, last)]
     run(
-        lambda images: attention_back(images, count, sc),
+        lambda images: attention_back(images, sc),
         {at: chain(todo) for at, todo in backward.items()},
     )
-    for half in range(2):
-        cols = slice(half * 128, (half + 1) * 128)
-        stores.append(
-            pltpu.make_async_copy(
-                sc["tokens"].at[half], gin_ref.at[:, cols], sc["local"].at[2 + half]
-            )
-        )
-        stores[-1].start()
     place_group(sc)
     gscatter.start(last)
+    stores = []
+
+    def store(held, target):
+        for half in range(2):
+            cols = slice(half * 128, (half + 1) * 128)
+            copy = pltpu.make_async_copy(
+                sc[held].at[half], target.at[:, cols], sc["local"].at[len(stores)]
+            )
+            copy.start()
+            stores.append(copy)
+
+    for g in range(last - 1, 0, -1):
+        advance(sscatter, g)()
+    run(lambda images: input_gradient(images, count, sc), {CORE_STEP: advance(gscatter, last)})
+    store("tokens", gin_ref)
+    for g in range(last - 1, 1, -1):
+        advance(gscatter, g)()
+    run(
+        lambda images: mlp_output(images, count, drop_ref, sc),
+        {OUT_STEP: advance(gscatter, 1)} if last > 1 else None,
+        OUT_TOGETHER,
+    )
+    store("outs", out_ref)
     sscatter.wait(0)
-    for g in range(last, -1, -1):
-        gscatter.wait(g)
-        if g > 0:
-            gscatter.start(g - 1)
+    gscatter.wait(0)
     finish(
         n_dp,
         soff,
@@ -957,8 +974,8 @@
         far,
         sc,
     )
-    for store in stores:
-        store.wait()
+    for copy in stores:
+        copy.wait()
 
 
 def chain(actions):
@@ -986,7 +1003,7 @@
 
     out, gin, smine, gmine, norm = pl.pallas_call(
         partial(step_kernel, n_dp, count, tuple(shapes)),
-        in_specs=[pl.BlockSpec(memory_space=pltpu.SMEM), anywhere, anywhere, vmem, vmem],
+        in_specs=[anywhere] * 5,
         out_specs=[anywhere, anywhere, vmem, vmem, vmem],
         out_shape=[jax.ShapeDtypeStruct((TOK * count, D), f32)] * 2
         + [

time: 79.7 us -> 71.5 us (0.90)
  Pallas kernels: 78.8 us -> 70.7 us
    pallas_call x1, Pallas kernels: 74.2 us -> 66 us  [step(): pl.pallas_call(partial(step_kernel, n_dp, count, tuple(shapes)), in_specs...]
where the time goes in v7:
time: 71.5 us; the launch traced here: 71.3 us
  Pallas kernels  70.7 us (99%)
    pallas_call x1, Pallas kernels, step(): pl.pallas_call(partial(step_kernel, n_dp, count, tuple(shapes)), in_specs...  66 us
    pallas_call x1, Pallas kernels, update(): pl.pallas_call(update_kernel, in_specs=[anywhere] * 2 + [vmem] * 9, out_s...  4.63 us

profile of v7, /device:TPU:0, one launch (start us, length us, event | category | flops | bytes accessed | tf_op | source)
XLA Modules:
  0.0 71.3 jit_solution(18051861703193805062)
XLA Ops:
  0.6 66.0 %step.1 = (f32[1568,256]{1,0:T(8,128)}, f32[1568,256]{1,0:T(8,128)}, f32[144,128]{1,0:T(8,128)}, f32[1,8288]{1,0:T(1,128)}, f32[8,128]{1,0:T(8,128)}) custom-call(s32[2,8]{1,0:T(2,128)} %bitcast.18, bf16[1568,256]{1,0:T(8,128)(2,1)} %bitcast.15, bf16[1568,256]{1,0:T(8,128)(2,1)} %bitcast.16, f32[16464]{0:T(1024)} %refs_3_.1, f32[1,8288]{1,0:T(1,128)} %refs_0_.1), custom_call_target="tpu_custom_call" | custom-call | tf_op jit(solution)/shard_map/step/pallas_call | solution.py:1004
  66.7 4.6 %update.1 = (f32[1568,256]{1,0:T(8,128)}, f32[1568,256]{1,0:T(8,128)}, f32[1,1]{1,0:T(1,128)}, f32[1,8288]{1,0:T(1,128)}, f32[1,8288]{1,0:T(1,128)}, /*index=5*/...) custom-call(f32[1568,256]{1,0:T(8,128)} %get-tuple-element.31.out_in, ...), custom_call_target="tpu_custom_call" | custom-call | tf_op jit(solution)/shard_map/update/pallas_call | solution.py:1080

commit v8 on v7

--- a/solution.py
+++ b/solution.py
@@ -118,7 +118,7 @@
     return (me, near), (high, far)
 
 
-UNROLL = 4
+UNROLL = 16
 
 
 class Gather:
@@ -322,10 +322,16 @@
     )
 
 
-def from_diagonal(square):
-    return jnp.concatenate(
-        [square[:STRIPE, :HALF], square[HALF : HALF + STRIPE, HALF:]], axis=1
-    )
+def turn_heads(stacked):
+    gap = jnp.zeros((HALF - STRIPE, HALF), stacked.dtype)
+    parts = []
+    for h in range(HEADS):
+        rows = stacked[h * STRIPE : (h + 1) * STRIPE]
+        blocks = [
+            jnp.concatenate([rows[:, s * HALF : (s + 1) * HALF], gap], axis=0).T for s in range(2)
+        ]
+        parts.append(jnp.concatenate(blocks, axis=1)[:STRIPE])
+    return jnp.concatenate(parts, axis=0)
 
 
 def row_shift(values, rows):
@@ -517,8 +523,8 @@
             probs = weights * (1.0 / jnp.sum(weights, axis=1, keepdims=True))
             probs = probs.reshape(HEADS * STRIPE, D)
             sc["probs"][image, j] = probs
-            total = from_diagonal(tn(probs.astype(bf16), spread_heads(value, masks)))
-            total = total + conv[j, 9:10]
+            values = diagonal(qkv_ref[image, j, :, 256:384])
+            total = pick_heads(nn(turn_heads(probs.astype(bf16)), values)) + conv[j, 9:10]
             near = neighbours(value.astype(f32), j)
             for outer in range(3):
                 part = None
@@ -604,7 +610,7 @@
         sc["gheads"][image, :, 128:] = to_stripes(grad[:, 128:]).astype(bf16)
 
 
-def attention_back(images, sc):
+def attention_back(images, sc, now, between):
     scale = HD ** (-0.5)
     masks = head_masks(bf16)
     inside = row_mask()[:STRIPE]
@@ -613,12 +619,13 @@
     a_conv = sc["a_conv"]
     qkv_ref, conv = sc["qkv"], sc["conv"]
     for j in range(2):
+        if j == 1:
+            pl.when(now)(between)
         for image in images:
             grad = sc["gheads"][image, :, j * 128 : (j + 1) * 128]
             grad_square = diagonal(grad)
             grad_f = beside(grad).astype(f32)
             query = diagonal(qkv_ref[image, j, :, 0:128])
-            keys = spread_heads(beside(qkv_ref[image, j, :, 128:256]), masks)
             value = beside(qkv_ref[image, j, :, 256:384])
             probs = sc["probs"][image, j]
             grad_probs = nt(spread_heads(value, masks), grad_square)
@@ -626,7 +633,8 @@
             inner = jnp.sum(product, axis=1, keepdims=True)
             grad_scores = product - probs.reshape(HEADS, STRIPE, D) * inner
             grad_scores = grad_scores.reshape(HEADS * STRIPE, D).astype(bf16)
-            grad_query = from_diagonal(tn(grad_scores, keys)) * scale
+            keys = diagonal(qkv_ref[image, j, :, 128:256])
+            grad_query = pick_heads(nn(turn_heads(grad_scores), keys)) * scale
             grad_key = pick_heads(nn(grad_scores, query)) * scale
             grad_value = pick_heads(nn(probs.astype(bf16), grad_square))
             near = neighbours(grad_f, j)
@@ -741,10 +749,13 @@
 
 ACCUMULATORS = ("a_wq", "a_ow", "a_uw", "a_dwt", "a_pb", "a_ub", "a_vec", "a_conv")
 TOGETHER = 2
+FORWARD_TOGETHER = 4
+BACK_TOGETHER = 4
 MLP_TOGETHER = 4
-GATHER_STEP = 2
+GATHER_STEP = 1
 CORE_STEP = 1
 OUT_STEP = 3
+BACK_IMAGE = 0
 OUT_TOGETHER = 2
 
 
@@ -889,13 +900,16 @@
     ggather.wait(last)
     prepare_group(n_dp, stages, sc)
 
-    steps = count // TOGETHER
-    backward = {}
     def spread_cores():
         sgather.wait(last - 1)
         sgather.start(last)
 
-    run(lambda images: attention_forward(images, sc), {min(GATHER_STEP, steps - 1): spread_cores})
+    steps = count // FORWARD_TOGETHER
+    run(
+        lambda images: attention_forward(images, sc),
+        {min(GATHER_STEP, steps - 1): spread_cores},
+        FORWARD_TOGETHER,
+    )
     sgather.wait(last)
     prepare_shared(n_dp, stages, sc)
     run(lambda images: mlp_both(images, drop_ref, sc), None, MLP_TOGETHER)
@@ -929,10 +943,12 @@
 
         return action
 
-    backward[min(1, steps - 1)] = [advance(sscatter, last)]
     run(
-        lambda images: attention_back(images, sc),
-        {at: chain(todo) for at, todo in backward.items()},
+        lambda images: attention_back(
+            images, sc, images[0] == BACK_IMAGE, advance(sscatter, last)
+        ),
+        None,
+        BACK_TOGETHER,
     )
     place_group(sc)
     gscatter.start(last)
@@ -978,14 +994,6 @@
         copy.wait()
 
 
-def chain(actions):
-    def run_all():
-        for action in actions:
-            action()
-
-    return run_all
-
-
 def step(n_dp, drops, images, cotangent, state):
     count = images.shape[0]
     gown, _, _, sown, _, _ = state
@@ -1032,61 +1040,77 @@
     return (master_new, first_new, second_new)
 
 
-CHUNKS = 4
-
-
-def update_kernel(out_in, gin_in, smine, gmine, norm_in, *refs):
-    gstate, sstate, refs = refs[:3], refs[3:6], refs[6:]
-    out_ref, gin_ref, norm_ref = refs[:3]
-    gnew, snew, (out_buf, gin_buf, in_sem, out_sem) = refs[3:8], refs[8:13], refs[13:]
-    size = out_in.shape[0] // CHUNKS
-    arrays = ((out_in, out_buf, out_ref), (gin_in, gin_buf, gin_ref))
+CHUNKS = 1
+
+
+def update_kernel(*refs):
+    big_in, small_in, refs = refs[:2], refs[2:11], refs[11:]
+    big_out, small_out, refs = refs[:2], refs[2:13], refs[13:]
+    big_buf, refs = refs[:2], refs[2:]
+    held_in, held_out, sems = refs[:9], refs[9:20], refs[20:]
+    big_load, big_store, small_load, small_store = sems
+    size = big_in[0].shape[0] // CHUNKS
+
+    def small_loads():
+        for i in range(9):
+            yield pltpu.make_async_copy(small_in[i], held_in[i], small_load.at[i])
+
     loads, stores = [], []
     for i in range(CHUNKS):
         rows = pl.ds(i * size, size)
-        for k, (source, held, target) in enumerate(arrays):
-            loads.append(
-                pltpu.make_async_copy(source.at[rows], held.at[rows], in_sem.at[k, i])
-            )
-            stores.append(
-                pltpu.make_async_copy(held.at[rows], target.at[rows], out_sem.at[k, i])
-            )
-            loads[-1].start()
-    for load, store in zip(loads, stores):
+        for k in range(2):
+            held = big_buf[k].at[rows]
+            loads.append(pltpu.make_async_copy(big_in[k].at[rows], held, big_load.at[k, i]))
+            stores.append(pltpu.make_async_copy(held, big_out[k].at[rows], big_store.at[k, i]))
+    small = list(small_loads())
+    for load in (*small, *loads):
+        load.start()
+    for load in small:
         load.wait()
-        store.start()
-    norm_ref[...] = norm_in[0:1, 0:1]
+    smine, gmine, norm = held_in[:3]
+    states = (held_in[3:6], held_in[6:9])
+    held_out[0][...] = norm[0:1, 0:1]
     for gradient, (master, first, second), new in (
-        (gmine[...], gstate, gnew),
-        (smine[0 : sstate[0].shape[0]], sstate, snew),
+        (gmine[...], states[0], held_out[1:6]),
+        (smine[0 : states[1][0].shape[0]], states[1], held_out[6:11]),
     ):
         new[0][...] = gradient
         new[1][...], new[2][...], new[3][...] = adam_step(
             master[...], gradient, first[...], second[...]
         )
         new[4][...] = new[1][...].astype(bf16)
-    for store in stores:
+    small = [
+        pltpu.make_async_copy(held_out[i], small_out[i], small_store.at[i]) for i in range(11)
+    ]
+    for load, store in zip(loads, stores):
+        load.wait()
+        store.start()
+    for store in small:
+        store.start()
+    for store in (*stores, *small):
         store.wait()
 
 
 def update(out, gin, smine, gmine, norm, *state):
-    vmem = pl.BlockSpec(memory_space=pltpu.VMEM)
     anywhere = pl.BlockSpec(memory_space=pl.ANY)
     like = jax.ShapeDtypeStruct
-    big = like(out.shape, f32)
-    news = []
+    news = [like((1, 1), f32)]
     for master in (state[0], state[3]):
         news += [like(master.shape, f32)] * 4 + [like(master.shape, bf16)]
+    small = (smine, gmine, norm, *state)
+    dma = pltpu.SemaphoreType.DMA
     return pl.pallas_call(
         update_kernel,
-        in_specs=[anywhere] * 2 + [vmem] * 9,
-        out_specs=[anywhere] * 2 + [vmem] * 11,
-        out_shape=[big, big, like((1, 1), f32)] + news,
+        in_specs=[anywhere] * (2 + len(small)),
+        out_specs=[anywhere] * (2 + len(news)),
+        out_shape=[like(out.shape, f32)] * 2 + news,
         scratch_shapes=[pltpu.VMEM(out.shape, f32)] * 2
-        + [pltpu.SemaphoreType.DMA((2, CHUNKS))] * 2,
+        + [pltpu.VMEM(array.shape, array.dtype) for array in (*small, *news)]
+        + [dma((2, CHUNKS))] * 2
+        + [dma((len(small),)), dma((len(news),))],
         compiler_params=pltpu.CompilerParams(vmem_limit_bytes=62 * 1024 * 1024),
         name="update",
-    )(out, gin, smine, gmine, norm, *state)
+    )(out, gin, *small)
 
 
 def on_device(

time: 71.5 us -> 68.8 us (0.962)
  Pallas kernels: 70.7 us -> 67.8 us
    pallas_call x1, Pallas kernels: 66 us -> 64 us  [step(): pl.pallas_call(partial(step_kernel, n_dp, count, tuple(shapes)), in_specs...]
    pallas_call x1, Pallas kernels: 4.63 us -> 3.8 us  [update(): pl.pallas_call(update_kernel, in_specs=[anywhere] * (2 + len(small)), out...]
where the time goes in v8:
time: 68.8 us; the launch traced here: 68.7 us
  Pallas kernels  67.8 us (99%)
  between operations  0.81 us (1%)
    pallas_call x1, Pallas kernels, step(): pl.pallas_call(partial(step_kernel, n_dp, count, tuple(shapes)), in_specs...  64 us
    pallas_call x1, Pallas kernels, update(): pl.pallas_call(update_kernel, in_specs=[anywhere] * (2 + len(small)), out...  3.8 us

profile of v8, /device:TPU:0, one launch (start us, length us, event | category | flops | bytes accessed | tf_op | source)
XLA Modules:
  0.0 68.7 jit_solution(18094872156218820911)
XLA Ops:
  0.6 64.0 %step.1 = (f32[1568,256]{1,0:T(8,128)}, f32[1568,256]{1,0:T(8,128)}, f32[144,128]{1,0:T(8,128)}, f32[1,8288]{1,0:T(1,128)}, f32[8,128]{1,0:T(8,128)}) custom-call(s32[2,8]{1,0:T(2,128)} %bitcast.18, bf16[1568,256]{1,0:T(8,128)(2,1)} %bitcast.15, bf16[1568,256]{1,0:T(8,128)(2,1)} %bitcast.16, f32[16464]{0:T(1024)} %refs_8_.1, f32[1,8288]{1,0:T(1,128)} %refs_5_.1), custom_call_target="tpu_custom_call" | custom-call | tf_op jit(solution)/shard_map/step/pallas_call | solution.py:1012
  64.7 3.8 %update.1 = (f32[1568,256]{1,0:T(8,128)}, f32[1568,256]{1,0:T(8,128)}, f32[1,1]{1,0:T(1,128)}, f32[1,8288]{1,0:T(1,128)}, f32[1,8288]{1,0:T(1,128)}, /*index=5*/...) custom-call(f32[1568,256]{1,0:T(8,128)} %get-tuple-element.31.refs_0, ...), custom_call_target="tpu_custom_call" | custom-call | tf_op jit(solution)/shard_map/update/pallas_call | solution.py:1102

commit v9 on v8

--- a/solution.py
+++ b/solution.py
@@ -208,6 +208,11 @@
 
         blocks = 1 << self.offset(g)
         lax.fori_loop(0, blocks, add, 0, unroll=min(blocks, UNROLL))
+
+
+def group_halves(grows):
+    first = 16 * (-(-grows // 32))
+    return first, grows - first
 
 
 def scatter_shapes(stages, rows):
@@ -456,7 +461,7 @@
     for c in range(8):
         cols = slice(c * 128, (c + 1) * 128)
         flat[pl.ds(c, D, stride=8), :] = sc["a_uw"][:, cols]
-        flat[2048 + c : 2049 + c, :] = sc["a_ub"][0:1, cols]
+        flat[2048 + c : 2049 + c, :] = column_sum(sc["a_ub"][:, cols])
     for q in range(4):
         turned = sc["a_dwt"][:, q * 256 : (q + 1) * 256].T
         for c in range(2):
@@ -483,8 +488,8 @@
             gflat[j, pl.ds(770 + c, HALF, stride=2), :] = sc["a_ow"][
                 j * 128 : (j + 1) * 128, cols
             ]
-        gflat[j, 768:769, :] = sc["a_pb"][0:1, j * 384 : j * 384 + 128]
-        gflat[j, 769:770, :] = sc["a_pb"][0:1, j * 384 + 256 : j * 384 + 384]
+        gflat[j, 768:769, :] = column_sum(sc["a_pb"][:, j * 384 : j * 384 + 128])
+        gflat[j, 769:770, :] = column_sum(sc["a_pb"][:, j * 384 + 256 : j * 384 + 384])
         for i in range(10):
             both = column_sum(sc["a_conv"][j, i])
             gflat[j, 1026 + i : 1027 + i, :] = both[:, :HALF] + both[:, HALF:]
@@ -552,7 +557,6 @@
     a_vec = sc["a_vec"]
     uw, dw, ubias = sc["uw"], sc["dw"], sc["ubias"]
     many = len(images)
-    ones = jnp.ones((8, many * GRID), bf16)
 
     def join(parts):
         return jnp.concatenate(parts, axis=0)
@@ -585,7 +589,7 @@
         sc["a_dwt"][:, cols] += tn(grad_mlp, active)
         grad_active = nt(grad_mlp, dw[cols, :])
         grad_hidden = (grad_active * (phi + hidden * density)).astype(bf16)
-        sc["a_ub"][:, cols] += nn(ones, grad_hidden)
+        sc["a_ub"][:, cols] += tile_sum(grad_hidden.astype(f32))
         sc["a_uw"][:, cols] += tn(normed_two, grad_hidden)
         part = nt(grad_hidden, uw[:, cols])
         grad_normed = part if grad_normed is None else grad_normed + part
@@ -615,7 +619,6 @@
     masks = head_masks(bf16)
     inside = row_mask()[:STRIPE]
     many = len(images)
-    ones = jnp.ones((8, many * GRID), bf16)
     a_conv = sc["a_conv"]
     qkv_ref, conv = sc["qkv"], sc["conv"]
     for j in range(2):
@@ -660,7 +663,7 @@
             sc["gtriple"][image, :, j * 384 : (j + 1) * 384] = both
     grad_triple = sc["gtriple"][pl.ds(images[0], many)].reshape(many * GRID, 768)
     normed = sc["normed"][pl.ds(images[0], many)].reshape(many * GRID, D)
-    sc["a_pb"][...] += nn(ones, grad_triple)
+    sc["a_pb"][...] += tile_sum(grad_triple.astype(f32))
     sc["a_wq"][...] += tn(normed, grad_triple)
 
 
@@ -725,7 +728,8 @@
         gtriple=((count, GRID, 768), bf16),
     )
     stages = exchange_stages(n_dp)
-    for name, rows in (("s", srows), ("g", grows)):
+    first, second = group_halves(grows)
+    for name, rows in (("s", srows), ("g", first), ("h", second)):
         outgoing, sums = scatter_shapes(stages, rows)
         for g, shape in enumerate(outgoing):
             shapes[f"{name}out{g}"] = (shape, bf16)
@@ -736,7 +740,7 @@
     shapes["far_stat"] = ((n_dp // fast, 8, 128), f32)
     made = {name: pltpu.VMEM(*shape) for name, shape in shapes.items()}
     dma = pltpu.SemaphoreType.DMA
-    for name in ("sgather", "ggather", "sscatter", "gscatter"):
+    for name in ("sgather", "ggather", "sscatter", "gscatter", "hscatter"):
         made[name + "_send"] = dma((len(stages),))
         made[name + "_recv"] = dma((len(stages),))
     for name in ("near", "far"):
@@ -922,10 +926,15 @@
         row = (k * (SHARED_PARAMS // n)) // UNIT * 8
         return sc["flat"][pl.ds(pl.multiple_of(row, 8), srows), :]
 
-    def gwindow(place):
-        k = device_at(stages, place)
-        row = ((k // 2) * (GROUP_PARAMS // n_dp)) // UNIT * 8
-        return sc["gflat"][k % 2, pl.ds(pl.multiple_of(row, 8), grows), :]
+    first, second = group_halves(grows)
+
+    def gwindow(begin, size):
+        def window(place):
+            k = device_at(stages, place)
+            row = ((k // 2) * (GROUP_PARAMS // n_dp)) // UNIT * 8 + begin
+            return sc["gflat"][k % 2, pl.ds(pl.multiple_of(row, 8), size), :]
+
+        return window
 
     def scatter(name, window):
         parts = [[sc[f"{name}{kind}{g}"] for g in range(last + 1)] for kind in ("out", "in", "sum")]
@@ -934,24 +943,26 @@
         )
 
     sscatter = scatter("s", swindow)
-    gscatter = scatter("g", gwindow)
+    gscatters = (scatter("g", gwindow(0, first)), scatter("h", gwindow(first, second)))
     sscatter.start(last)
-    def advance(scatter, g):
+    def advance(scatters, g):
         def action():
-            scatter.wait(g)
-            scatter.start(g - 1)
+            for scatter in scatters:
+                scatter.wait(g)
+                scatter.start(g - 1)
 
         return action
 
     run(
         lambda images: attention_back(
-            images, sc, images[0] == BACK_IMAGE, advance(sscatter, last)
+            images, sc, images[0] == BACK_IMAGE, advance((sscatter,), last)
         ),
         None,
         BACK_TOGETHER,
     )
     place_group(sc)
-    gscatter.start(last)
+    for half in gscatters:
+        half.start(last)
     stores = []
 
     def store(held, target):
@@ -964,25 +975,26 @@
             stores.append(copy)
 
     for g in range(last - 1, 0, -1):
-        advance(sscatter, g)()
-    run(lambda images: input_gradient(images, count, sc), {CORE_STEP: advance(gscatter, last)})
+        advance((sscatter,), g)()
+    run(lambda images: input_gradient(images, count, sc), {CORE_STEP: advance(gscatters, last)})
     store("tokens", gin_ref)
     for g in range(last - 1, 1, -1):
-        advance(gscatter, g)()
+        advance(gscatters, g)()
     run(
         lambda images: mlp_output(images, count, drop_ref, sc),
-        {OUT_STEP: advance(gscatter, 1)} if last > 1 else None,
+        {OUT_STEP: advance(gscatters, 1)} if last > 1 else None,
         OUT_TOGETHER,
     )
     store("outs", out_ref)
     sscatter.wait(0)
-    gscatter.wait(0)
+    for half in gscatters:
+        half.wait(0)
     finish(
         n_dp,
         soff,
         goff,
         sc["ssum0"][0],
-        sc["gsum0"][0],
+        jnp.concatenate([sc["gsum0"][0], sc["hsum0"][0]], axis=0),
         smine_ref,
         gmine_ref,
         norm_ref,

time: 68.8 us -> 67.3 us (0.978)
  Pallas kernels: 67.8 us -> 66.4 us
    pallas_call x1, Pallas kernels: 64 us -> 62.5 us  [step(): pl.pallas_call(partial(step_kernel, n_dp, count, tuple(shapes)), in_specs...]
where the time goes in v9:
time: 67.3 us; the launch traced here: 67.2 us
  Pallas kernels  66.4 us (99%)
  between operations  0.81 us (1%)
    pallas_call x1, Pallas kernels, step(): pl.pallas_call(partial(step_kernel, n_dp, count, tuple(shapes)), in_specs...  62.5 us
    pallas_call x1, Pallas kernels, update(): pl.pallas_call(update_kernel, in_specs=[anywhere] * (2 + len(small)), out...  3.8 us

profile of v9, /device:TPU:0, one launch (start us, length us, event | category | flops | bytes accessed | tf_op | source)
XLA Modules:
  0.0 67.2 jit_solution(14083266181717618953)
XLA Ops:
  0.6 62.5 %step.1 = (f32[1568,256]{1,0:T(8,128)}, f32[1568,256]{1,0:T(8,128)}, f32[144,128]{1,0:T(8,128)}, f32[1,8288]{1,0:T(1,128)}, f32[8,128]{1,0:T(8,128)}) custom-call(s32[2,8]{1,0:T(2,128)} %bitcast.18, bf16[1568,256]{1,0:T(8,128)(2,1)} %bitcast.15, bf16[1568,256]{1,0:T(8,128)(2,1)} %bitcast.16, f32[16464]{0:T(1024)} %refs_8_.1, f32[1,8288]{1,0:T(1,128)} %refs_5_.1), custom_call_target="tpu_custom_call" | custom-call | tf_op jit(solution)/shard_map/step/pallas_call | solution.py:1024
  63.2 3.8 %update.1 = (f32[1568,256]{1,0:T(8,128)}, f32[1568,256]{1,0:T(8,128)}, f32[1,1]{1,0:T(1,128)}, f32[1,8288]{1,0:T(1,128)}, f32[1,8288]{1,0:T(1,128)}, /*index=5*/...) custom-call(f32[1568,256]{1,0:T(8,128)} %get-tuple-element.31.refs_0, ...), custom_call_target="tpu_custom_call" | custom-call | tf_op jit(solution)/shard_map/update/pallas_call | solution.py:1114

commit v10 on v9

--- a/solution.py
+++ b/solution.py
@@ -441,10 +441,15 @@
     n = 2 * n_dp
     flat, buffer = sc["flat"], sc["sweights"]
     srows = buffer.shape[1]
-    flat[...] = jnp.zeros_like(flat)
+    done = 0
     for k in range(n):
         at = first_row(SHARED_PARAMS, n, k)
-        flat[at : at + srows] += buffer[place_of(stages, k)].astype(f32)
+        window = buffer[place_of(stages, k)].astype(f32)
+        both = max(done - at, 0)
+        if both:
+            flat[at:done] += window[:both]
+        done = at + srows
+        flat[at + both : done] = window[both:]
     for c in range(8):
         cols = slice(c * 128, (c + 1) * 128)
         sc["uw"][:, cols] = flat[pl.ds(c, D, stride=8), :].astype(bf16)
@@ -522,7 +527,7 @@
             keys = spread_heads(beside(qkv_ref[image, j, :, 128:256]), masks)
             value = beside(qkv_ref[image, j, :, 256:384])
             scores = nt(keys, query).reshape(HEADS, SIDE, 8, D) * scale
-            scores = jnp.where(key_row < SW, scores, -1e30)
+            scores = jnp.where(key_row < SW, scores, -jnp.inf)
             scores = scores.reshape(HEADS, STRIPE, D)
             weights = jnp.exp(scores - jnp.max(scores, axis=1, keepdims=True))
             probs = weights * (1.0 / jnp.sum(weights, axis=1, keepdims=True))

time: 67.3 us -> 67.3 us (level)
  no operation moved by 1% of the time
where the time goes in v10:
time: 67.3 us; the launch traced here: 67.1 us
  Pallas kernels  66.3 us (99%)
  between operations  0.81 us (1%)
    pallas_call x1, Pallas kernels, step(): pl.pallas_call(partial(step_kernel, n_dp, count, tuple(shapes)), in_specs...  62.5 us
    pallas_call x1, Pallas kernels, update(): pl.pallas_call(update_kernel, in_specs=[anywhere] * (2 + len(small)), out...  3.8 us

profile of v10, /device:TPU:0, one launch (start us, length us, event | category | flops | bytes accessed | tf_op | source)
XLA Modules:
  0.0 67.1 jit_solution(14879586744349476338)
XLA Ops:
  0.6 62.5 %step.1 = (f32[1568,256]{1,0:T(8,128)}, f32[1568,256]{1,0:T(8,128)}, f32[144,128]{1,0:T(8,128)}, f32[1,8288]{1,0:T(1,128)}, f32[8,128]{1,0:T(8,128)}) custom-call(s32[2,8]{1,0:T(2,128)} %bitcast.18, bf16[1568,256]{1,0:T(8,128)(2,1)} %bitcast.15, bf16[1568,256]{1,0:T(8,128)(2,1)} %bitcast.16, f32[16464]{0:T(1024)} %refs_8_.1, f32[1,8288]{1,0:T(1,128)} %refs_5_.1), custom_call_target="tpu_custom_call" | custom-call | tf_op jit(solution)/shard_map/step/pallas_call | solution.py:1029
  63.2 3.8 %update.1 = (f32[1568,256]{1,0:T(8,128)}, f32[1568,256]{1,0:T(8,128)}, f32[1,1]{1,0:T(1,128)}, f32[1,8288]{1,0:T(1,128)}, f32[1,8288]{1,0:T(1,128)}, /*index=5*/...) custom-call(f32[1568,256]{1,0:T(8,128)} %get-tuple-element.31.refs_0, ...), custom_call_target="tpu_custom_call" | custom-call | tf_op jit(solution)/shard_map/update/pallas_call | solution.py:1119

commit v11 on v9

--- a/solution.py
+++ b/solution.py
@@ -522,7 +522,7 @@
             keys = spread_heads(beside(qkv_ref[image, j, :, 128:256]), masks)
             value = beside(qkv_ref[image, j, :, 256:384])
             scores = nt(keys, query).reshape(HEADS, SIDE, 8, D) * scale
-            scores = jnp.where(key_row < SW, scores, -1e30)
+            scores = jnp.where(key_row < SW, scores, -jnp.inf)
             scores = scores.reshape(HEADS, STRIPE, D)
             weights = jnp.exp(scores - jnp.max(scores, axis=1, keepdims=True))
             probs = weights * (1.0 / jnp.sum(weights, axis=1, keepdims=True))
@@ -758,9 +758,9 @@
 MLP_TOGETHER = 4
 GATHER_STEP = 1
 CORE_STEP = 1
-OUT_STEP = 3
+OUT_STEP = 1
 BACK_IMAGE = 0
-OUT_TOGETHER = 2
+OUT_TOGETHER = 4
 
 
 def own_windows(n_dp, sown_ref, gown_ref, soff, goff, stages, sc):

time: 67.3 us -> 67.2 us (level)
  no operation moved by 1% of the time
where the time goes in v11:
time: 67.2 us; the launch traced here: 67.1 us
  Pallas kernels  66.3 us (99%)
  between operations  0.81 us (1%)
    pallas_call x1, Pallas kernels, step(): pl.pallas_call(partial(step_kernel, n_dp, count, tuple(shapes)), in_specs...  62.5 us
    pallas_call x1, Pallas kernels, update(): pl.pallas_call(update_kernel, in_specs=[anywhere] * (2 + len(small)), out...  3.8 us

profile of v11, /device:TPU:0, one launch (start us, length us, event | category | flops | bytes accessed | tf_op | source)
XLA Modules:
  0.0 67.1 jit_solution(12132106650551773818)
XLA Ops:
  0.6 62.5 %step.1 = (f32[1568,256]{1,0:T(8,128)}, f32[1568,256]{1,0:T(8,128)}, f32[144,128]{1,0:T(8,128)}, f32[1,8288]{1,0:T(1,128)}, f32[8,128]{1,0:T(8,128)}) custom-call(s32[2,8]{1,0:T(2,128)} %bitcast.18, bf16[1568,256]{1,0:T(8,128)(2,1)} %bitcast.15, bf16[1568,256]{1,0:T(8,128)(2,1)} %bitcast.16, f32[16464]{0:T(1024)} %refs_8_.1, f32[1,8288]{1,0:T(1,128)} %refs_5_.1), custom_call_target="tpu_custom_call" | custom-call | tf_op jit(solution)/shard_map/step/pallas_call | solution.py:1024
  63.1 3.8 %update.1 = (f32[1568,256]{1,0:T(8,128)}, f32[1568,256]{1,0:T(8,128)}, f32[1,1]{1,0:T(1,128)}, f32[1,8288]{1,0:T(1,128)}, f32[1,8288]{1,0:T(1,128)}, /*index=5*/...) custom-call(f32[1568,256]{1,0:T(8,128)} %get-tuple-element.31.refs_0, ...), custom_call_target="tpu_custom_call" | custom-call | tf_op jit(solution)/shard_map/update/pallas_call | solution.py:1114
